TPU v7x, 256 devices: a whole 4x4x8 slice. The times are simulated.
256 devices in a mesh: tx: 8 (over x, y_hi), ty: 32 (over y_lo, z, core).
Axes of the slice: x: 4, y: 4 (y_hi: 2, y_lo: 2; y = y_hi * 2 + y_lo), z: 8, core: 2. Of those that a mesh axis runs over, the one named last changes fastest.
Arguments:
- features: bfloat16 [1536, 32, 512], P(('tx', 'ty')), may hold values from -6 to 6
- occupancy: int32 [1536, 512], P(('tx', 'ty')), may hold values from 0 to 1, as said below
- neighbours: int32 [1536, 6], P(('tx', 'ty')), may hold values from -1 to 1535, as said below
- w_first: bfloat16 [32, 864], replicated, may hold values from -0.21875 to 0.21875
- w_second: bfloat16 [32, 864], replicated, may hold values from -0.21875 to 0.21875
- cotangent: bfloat16 [1536, 32, 512], P(('tx', 'ty')), may hold values from -6 to 6
Outputs:
- result: bfloat16 [1536, 32, 512], P(('tx', 'ty'))
- grad_features: bfloat16 [1536, 32, 512], P(('tx', 'ty'))
- grad_first: float32 [32, 864], replicated
- grad_second: float32 [32, 864], replicated
Inputs may be any that keep to these rules, and one draw needn't show every extreme that they name: Bricks lie on a lattice of 16 x 96 x 1 positions; the tile of device (tx, ty) (brick rows of index tx * 32 + ty) holds positions with x in [tx * 2, (tx+1) * 2) and y in [ty * 3, (ty+1) * 3), one slot each in a drawn order. An id is device * 6 + slot. A neighbour across faces 0 and 1 lies on the same device or on the device one step lower or higher along tx with the same ty; across faces 2 and 3 on the same device or one step along ty; across faces 4 and 5 on the same device. If neighbours[s, f] = t then neighbours[t, f^1] = s. Inactive bricks have all entries -1 and no occupied voxels. `occupancy`: only active bricks have occupied voxels.
All inputs are finite; a program needn't handle non-finite values.
Results may differ from a plain program's by a relative error of at most 0.03.
The roundings to bfloat16 on the way count: a program that leaves them out, or rounds other values in their place, can miss the bound.
Values may be sent and summed in bfloat16 or wider, within the bound.
No kernel may reach another device: no remote copies, remote signals or barrier semaphores. Data moves between devices by JAX's collectives and lax.ppermute only.
A program may use at most 128 MiB of HBM per device.

v0:
```python
import math

import jax
import jax.numpy as jnp
from jax import lax
from jax.sharding import PartitionSpec as P

EDGE = 8


def passed_along(value, axis, steps):
    count = lax.axis_size(axis)
    first, last = (max(0, -steps), min(count, count - steps))
    return lax.ppermute(value, axis, [(source, source + steps) for source in range(first, last)])


def face_planes(field):
    count, chans = (field.shape[0], field.shape[1])
    cube = field.reshape(count, chans, EDGE, EDGE, EDGE)
    faces = [
        cube[:, :, 0],
        cube[:, :, -1],
        cube[:, :, :, 0],
        cube[:, :, :, -1],
        cube[:, :, :, :, 0],
        cube[:, :, :, :, -1],
    ]
    return [face.reshape(count, chans, EDGE * EDGE) for face in faces]


def forward_remote(items):
    return [
        passed_along(items[1], "tx", 1),
        passed_along(items[0], "tx", -1),
        passed_along(items[3], "ty", 1),
        passed_along(items[2], "ty", -1),
    ]


def backward_remote(items):
    return [
        passed_along(items[1].astype(jnp.bfloat16), "tx", 1).astype(jnp.float32),
        passed_along(items[0].astype(jnp.bfloat16), "tx", -1).astype(jnp.float32),
        passed_along(items[3].astype(jnp.bfloat16), "ty", 1).astype(jnp.float32),
        passed_along(items[2].astype(jnp.bfloat16), "ty", -1).astype(jnp.float32),
    ]


def collect_every(items, neighbours, myself, remote_fn):
    slots = items[0].shape[0]
    result = []
    remote = remote_fn(items)
    for face in range(6):
        ident = neighbours[:, face]
        valid = (ident >= 0).astype(items[0].dtype)
        safe = jnp.maximum(ident, 0)
        local = safe % slots
        if face < 4:
            owner = safe // slots
            source = jnp.concatenate([items[face ^ 1], remote[face]], axis=0)
            pick = local + slots * (owner != myself).astype(jnp.int32)
        else:
            source = items[face ^ 1]
            pick = local
        result.append(jnp.take(source, pick, axis=0) * valid[:, None, None])
    return result


def collect(items, neighbours, myself):
    return collect_every(items, neighbours, myself, forward_remote)


def padded(field, halos):
    count, chans = (field.shape[0], field.shape[1])
    cube = field.reshape(count, chans, EDGE, EDGE, EDGE)
    cells = jnp.pad(cube, ((0, 0), (0, 0), (1, 1), (1, 1), (1, 1)))
    sheet = [h.reshape(count, chans, EDGE, EDGE) for h in halos]
    cells = cells.at[:, :, 0, 1:-1, 1:-1].set(sheet[0])
    cells = cells.at[:, :, -1, 1:-1, 1:-1].set(sheet[1])
    cells = cells.at[:, :, 1:-1, 0, 1:-1].set(sheet[2])
    cells = cells.at[:, :, 1:-1, -1, 1:-1].set(sheet[3])
    cells = cells.at[:, :, 1:-1, 1:-1, 0].set(sheet[4])
    cells = cells.at[:, :, 1:-1, 1:-1, -1].set(sheet[5])
    return cells


def columns(block):
    count, chans = (block.shape[0], block.shape[1])
    pieces = []
    for first in range(3):
        for second in range(3):
            for third in range(3):
                piece = block[
                    :, :, first : first + EDGE, second : second + EDGE, third : third + EDGE
                ]
                pieces.append(piece.reshape(count, chans, EDGE * EDGE * EDGE))
    return jnp.concatenate(pieces, axis=1)


def conv_blocks(cells, weight, group):
    count = cells.shape[0]
    blocks = cells.reshape((count // group, group) + cells.shape[1:])

    def conv_one_block(block):
        return jnp.einsum("ok,gkv->gov", weight, columns(block), preferred_element_type=jnp.float32)

    out = lax.map(conv_one_block, blocks)
    return out.reshape(count, weight.shape[0], -1)


def weight_grad(cells, grad, group):
    count = cells.shape[0]
    blocks = cells.reshape((count // group, group) + cells.shape[1:])
    grads = grad.reshape((count // group, group) + grad.shape[1:])

    def weight_one_block(pair):
        return jnp.einsum(
            "gov,gkv->ok", pair[1], columns(pair[0]), preferred_element_type=jnp.float32
        )

    return jnp.sum(lax.map(weight_one_block, (blocks, grads)), axis=0)


def spread_taps(spread):
    count = spread.shape[0]
    chans = spread.shape[1] // 27
    cells = jnp.zeros((count, chans, EDGE + 2, EDGE + 2, EDGE + 2), jnp.float32)
    tap = 0
    for first in range(3):
        for second in range(3):
            for third in range(3):
                piece = spread[:, tap * chans : (tap + 1) * chans].reshape(
                    count, chans, EDGE, EDGE, EDGE
                )
                cells = cells.at[
                    :, :, first : first + EDGE, second : second + EDGE, third : third + EDGE
                ].add(piece)
                tap = tap + 1
    return cells


def transpose_returned(grad, weight, group, neighbours, myself):
    count, chans = (grad.shape[0], grad.shape[1])
    grads = grad.reshape((count // group, group) + grad.shape[1:])

    def transpose_one_block(block):
        spread = jnp.einsum("ok,gov->gkv", weight, block, preferred_element_type=jnp.float32)
        return spread_taps(spread)

    cells = lax.map(transpose_one_block, grads).reshape(count, chans, EDGE + 2, EDGE + 2, EDGE + 2)
    inner = cells[:, :, 1:-1, 1:-1, 1:-1]
    layers = [
        cells[:, :, 0, 1:-1, 1:-1],
        cells[:, :, -1, 1:-1, 1:-1],
        cells[:, :, 1:-1, 0, 1:-1],
        cells[:, :, 1:-1, -1, 1:-1],
        cells[:, :, 1:-1, 1:-1, 0],
        cells[:, :, 1:-1, 1:-1, -1],
    ]
    layers = [layer.reshape(count, chans, EDGE * EDGE) for layer in layers]
    landed = collect_every(layers, neighbours, myself, backward_remote)
    sheet = [piece.reshape(count, chans, EDGE, EDGE) for piece in landed]
    inner = inner.at[:, :, 0].add(sheet[0])
    inner = inner.at[:, :, -1].add(sheet[1])
    inner = inner.at[:, :, :, 0].add(sheet[2])
    inner = inner.at[:, :, :, -1].add(sheet[3])
    inner = inner.at[:, :, :, :, 0].add(sheet[4])
    inner = inner.at[:, :, :, :, -1].add(sheet[5])
    return inner.reshape(count, chans, EDGE * EDGE * EDGE)


def body(features, occupancy, neighbours, w_first, w_second, cotangent):
    slots = features.shape[0]
    group = 2
    myself = lax.axis_index("tx") * lax.axis_size("ty") + lax.axis_index("ty")
    mask = occupancy.astype(jnp.float32)[:, None, :]
    x_zero = (features.astype(jnp.float32) * mask).astype(jnp.bfloat16)
    pad_x = padded(x_zero, collect(face_planes(x_zero), neighbours, myself))
    pre_one = conv_blocks(pad_x, w_first, group)
    hidden = (jnp.maximum(pre_one, 0.0) * mask).astype(jnp.bfloat16)
    pad_h = padded(hidden, collect(face_planes(hidden), neighbours, myself))
    pre_two = conv_blocks(pad_h, w_second, group) + x_zero.astype(jnp.float32)
    result = (jnp.maximum(pre_two, 0.0) * mask).astype(jnp.bfloat16)
    grad_two = jnp.where(pre_two > 0.0, cotangent.astype(jnp.float32) * mask, 0.0).astype(
        jnp.bfloat16
    )
    term_second = weight_grad(pad_h, grad_two, group)
    dhidden = transpose_returned(grad_two, w_second, group, neighbours, myself)
    grad_one = jnp.where(pre_one > 0.0, dhidden * mask, 0.0).astype(jnp.bfloat16)
    term_first = weight_grad(pad_x, grad_one, group)
    dinput = transpose_returned(grad_one, w_first, group, neighbours, myself)
    grad_features = ((dinput + grad_two.astype(jnp.float32)) * mask).astype(jnp.bfloat16)
    total_first, total_second = lax.psum((term_first, term_second), ("tx", "ty"))
    scale = 1.0 / math.sqrt(slots * lax.axis_size("tx") * lax.axis_size("ty") * EDGE * EDGE * EDGE)
    return (result, grad_features, total_first * scale, total_second * scale)


def solution(mesh):
    return jax.shard_map(
        body,
        mesh=mesh,
        in_specs=(
            P(("tx", "ty"), None, None),
            P(("tx", "ty"), None),
            P(("tx", "ty"), None),
            P(),
            P(),
            P(("tx", "ty"), None, None),
        ),
        out_specs=(P(("tx", "ty"), None, None), P(("tx", "ty"), None, None), P(), P()),
        check_vma=False,
    )
```

profile of v0, /device:TPU:24, one launch (start us, length us, event | category | flops | bytes accessed | tf_op | source)
XLA Modules:
  0.0 1238.0 jit_solution(17558030082121253444)
XLA Ops:
  9.8 4.1 collective-permute-start
  13.8 3.3 collective-permute-start.1
  19.1 6.8 collective-permute-start.3
  44.8 6.1 scatter.46
  50.8 6.0 scatter.49
  57.7 70.2 %while.144 = (s32[]{:T(128)}, f32[3,2,32,512]{3,2,1,0:T(8,128)}, bf16[3,2,32,10,10,10]{2,5,4,3,1,0:T(8,128)(2,1)}, bf16[32,864]{1,0:T(8,128)(2,1)S(1)}, s32[]{:T(128)}) while((s32[]{:T(128)}, f32[3,2,32,512]{3,2,1,0:T(8,128)}, bf16[3,2,32,10,10,10]{2,5,4,3,1,0:T(8,128)(2,1)}, bf16[32,864]{1,0:T(8,128)(2,1)S(1)}, s32[]{:T(128)}) %tuple.690), condition=%wide.region_1.4_spmd, body=%wide.region_0.3_spmd.sunk | while | flops 56623104 | bytes 14402281 | solution.py:107
  131.3 3.1 collective-permute-start.7
  138.3 6.6 collective-permute-start.4
  159.1 6.0 scatter.56
  165.1 6.0 scatter.59
  172.0 69.9 %while.145 = (s32[]{:T(128)}, f32[3,2,32,512]{3,2,1,0:T(8,128)}, bf16[3,2,32,10,10,10]{2,5,4,3,1,0:T(8,128)(2,1)}, bf16[32,864]{1,0:T(8,128)(2,1)S(1)}, s32[]{:T(128)}) while((s32[]{:T(128)}, f32[3,2,32,512]{3,2,1,0:T(8,128)}, bf16[3,2,32,10,10,10]{2,5,4,3,1,0:T(8,128)(2,1)}, bf16[32,864]{1,0:T(8,128)(2,1)S(1)}, s32[]{:T(128)}) %tuple.688), condition=%wide.region_3.6_spmd, body=%wide.region_2.5_spmd.sunk | while | flops 56623104 | bytes 14402281 | solution.py:107
  247.1 2.9 broadcast.1529.clone2
  250.0 249.1 %while.146 = (s32[]{:T(128)}, f32[3,2,32,10,10,10]{2,5,4,1,0,3:T(8,128)}, bf16[3,2,32,512]{3,2,1,0:T(8,128)(2,1)}, bf16[32,864]{1,0:T(8,128)(2,1)S(1)}, s32[]{:T(128)}, /*index=5*/f32[]{:T(128)}, s32[]{:T(128)}, s32[]{:T(128)}) while((s32[]{:T(128)}, f32[3,2,32,10,10,10]{2,5,4,1,0,3:T(8,128)}, bf16[3,2,32,512]{3,2,1,0:T(8,128)(2,1)}, ...), condition=%wide.region_5.8_spmd, body=%wide.region_4.7_spmd.sunk | while | flops 57475072 | bytes 60730716 | solution.py:150
  265.8 2.8 scatter-add.434
  268.9 2.8 scatter-add.435
  278.1 4.8 scatter-add.437
  286.3 2.9 fusion.176
  336.6 2.8 scatter-add.451
  344.8 2.8 scatter-add.434
  347.9 2.8 scatter-add.435
  357.1 4.8 scatter-add.437
  365.3 2.9 fusion.176
  415.5 2.8 scatter-add.451
  423.8 2.8 scatter-add.434
  426.9 2.8 scatter-add.435
  436.1 4.8 scatter-add.437
  444.3 2.9 fusion.176
  494.5 2.8 scatter-add.451
  507.2 5.2 collective-permute-start.11
  516.9 6.3 collective-permute-start.8
  526.8 73.0 %while.149 = (s32[]{:T(128)}, f32[3,32,864]{2,1,0:T(8,128)}, bf16[3,2,32,512]{3,2,1,0:T(8,128)(2,1)}, bf16[3,2,32,10,10,10]{2,5,4,3,1,0:T(8,128)(2,1)}, s32[]{:T(128)}) while((s32[]{:T(128)}, f32[3,32,864]{2,1,0:T(8,128)}, bf16[3,2,32,512]{3,2,1,0:T(8,128)(2,1)}, bf16[3,2,32,10,10,10]{2,5,4,3,1,0:T(8,128)(2,1)}, s32[]{:T(128)}) %tuple.682), condition=%wide.region_13.18_spmd, body=%wide.region_12.17_spmd.sunk | while | flops 56623104 | bytes 14396649 | solution.py:121
  618.6 4.0 scatter-add.253
  622.9 4.0 scatter-add.256
  628.5 2.8 broadcast.1529.clone
  631.3 237.2 %while.147 = (s32[]{:T(128)}, f32[3,2,32,10,10,10]{2,5,4,1,0,3:T(8,128)}, bf16[3,2,32,512]{3,2,1,0:T(8,128)(2,1)}, bf16[32,864]{1,0:T(8,128)(2,1)S(1)}, s32[]{:T(128)}, /*index=5*/f32[]{:T(128)}, s32[]{:T(128)}, s32[]{:T(128)}) while((s32[]{:T(128)}, f32[3,2,32,10,10,10]{2,5,4,1,0,3:T(8,128)}, bf16[3,2,32,512]{3,2,1,0:T(8,128)(2,1)}, ...), condition=%wide.region_7.12_spmd, body=%wide.region_6.11_spmd.sunk | while | flops 57475072 | bytes 60730716 | solution.py:150
  647.8 4.6 scatter-add.465
  656.0 3.0 fusion.190
  726.8 4.6 scatter-add.465
  734.9 3.0 fusion.190
  805.7 4.6 scatter-add.465
  813.9 3.0 fusion.190
  874.2 3.0 fusion.98
  878.1 73.1 %while.148 = (s32[]{:T(128)}, f32[3,32,864]{2,1,0:T(8,128)}, bf16[3,2,32,512]{3,2,1,0:T(8,128)(2,1)}, bf16[3,2,32,10,10,10]{2,5,4,3,1,0:T(8,128)(2,1)}, s32[]{:T(128)}) while((s32[]{:T(128)}, f32[3,32,864]{2,1,0:T(8,128)}, bf16[3,2,32,512]{3,2,1,0:T(8,128)(2,1)}, bf16[3,2,32,10,10,10]{2,5,4,3,1,0:T(8,128)(2,1)}, s32[]{:T(128)}) %tuple.679), condition=%wide.region_9.14_spmd, body=%wide.region_8.13_spmd.sunk | while | flops 56623104 | bytes 14396649 | solution.py:121
  952.2 5.2 collective-permute-start.15
  963.4 5.7 collective-permute-start.12
  985.0 4.0 scatter-add.263
  989.3 4.0 scatter-add.266
  994.9 232.8 %all-reduce.7.cloned.1.call-done = (f32[32,864]{1,0:T(8,128)}, f32[32,864]{1,0:T(8,128)}) async-done(((f32[32,864]{1,0:T(8,128)}, f32[32,864]{1,0:T(8,128)}), (f32[32,864]{1,0:T(8,128)}, f32[32,864]{1,0:T(8,128)})) %all-reduce.7.cloned.1.call-update) | async-done | bytes 221200 | tf_op jit(solution)/shard_map/psum | solution.py:193
  (1690 shorter events, 800.9 us)
Async XLA Ops:
  7.2 18.8 %copy-start.50 = (s32[6,6]{1,0:T(8,128)S(1)}, s32[6,6]{1,0:T(8,128)}, u32[]{:S(2)}) copy-start(s32[6,6]{1,0:T(8,128)} %param.184) | copy-start | bytes 436
  7.2 1220.5 %all-reduce.7.cloned.1.call-start = ((), (), s32[]{:S(2)}) async-start(), calls=%async_computation | async-start | bytes 458752 | tf_op jit(solution)/shard_map/psum | solution.py:193
  7.9 235.5 %copy-start.56 = (f32[6,512]{1,0:T(8,128)}, f32[6,512]{1,0:T(8,128)S(1)}, u32[]{:S(2)}) copy-start(f32[6,512]{1,0:T(8,128)S(1)} %convert_element_type.223) | copy-start | bytes 36868
  9.3 19.1 %copy-start.36 = (bf16[6,32,512]{1,2,0:T(8,128)(2,1)}, bf16[6,32,512]{1,2,0:T(8,128)(2,1)S(1)}, u32[]{:S(2)}) copy-start(bf16[6,32,512]{1,2,0:T(8,128)(2,1)S(1)} %copy.172) | copy-start | bytes 589828
  9.8 25.1 %collective-permute-start = (bf16[6,32,64]{1,2,0:T(8,128)(2,1)S(1)}, bf16[6,32,64]{1,2,0:T(8,128)(2,1)S(1)}, u32[]{:S(2)}, u32[]{:S(2)}) collective-permute-start(bf16[6,32,64]{1,2,0:T(8,128)(2,1)S(1)} %get-tuple-element.1689), channel_id=1, source_target_pairs={{0,32},{32,64},{64,96},{96,128},{128,160},{160,192},{192,224},{1,3... | collective-permute-start | bytes 73736 | tf_op jit(solution)/shard_map/ppermute | solution.py:14
  13.8 21.1 %collective-permute-start.1 = (bf16[6,32,64]{1,2,0:T(8,128)(2,1)S(1)}, bf16[6,32,64]{1,2,0:T(8,128)(2,1)S(1)}, u32[]{:S(2)}, u32[]{:S(2)}) collective-permute-start(bf16[6,32,64]{1,2,0:T(8,128)(2,1)S(1)} %get-tuple-element.1688), channel_id=1, source_target_pairs={{32,0},{64,32},{96,64},{128,96},{160,128},{192,160},{224,192},{33,... | collective-permute-start | bytes 73736 | tf_op jit(solution)/shard_map/ppermute | solution.py:14
  17.2 19.0 %collective-permute-start.2 = (bf16[6,32,64]{1,2,0:T(8,128)(2,1)S(1)}, bf16[6,32,64]{1,2,0:T(8,128)(2,1)S(1)}, u32[]{:S(2)}, u32[]{:S(2)}) collective-permute-start(bf16[6,32,64]{1,2,0:T(8,128)(2,1)S(1)} %get-tuple-element.1687), channel_id=1, source_target_pairs={{0,1},{1,2},{2,3},{3,4},{4,5},{5,6},{6,7},{7,8},{8,9},{9,10},{10,1... | collective-permute-start | bytes 73736 | tf_op jit(solution)/shard_map/ppermute | solution.py:14
  19.1 23.2 %collective-permute-start.3 = (bf16[6,32,64]{1,2,0:T(8,128)(2,1)S(1)}, bf16[6,32,64]{1,2,0:T(8,128)(2,1)S(1)}, u32[]{:S(2)}, u32[]{:S(2)}) collective-permute-start(bf16[6,32,64]{1,2,0:T(8,128)(2,1)S(1)} %get-tuple-element.1686), channel_id=1, source_target_pairs={{1,0},{2,1},{3,2},{4,3},{5,4},{6,5},{7,6},{8,7},{9,8},{10,9},{11,1... | collective-permute-start | bytes 73736 | tf_op jit(solution)/shard_map/ppermute | solution.py:14
  27.7 124.5 %copy-start.61 = (pred[6]{0:T(512)(128)(4,1)}, pred[6]{0:T(512)(128)(4,1)S(1)}, u32[]{:S(2)}) copy-start(pred[6]{0:T(512)(128)(4,1)S(1)} %get-tuple-element.1490) | copy-start | bytes 22
  27.8 9.0 copy-start.102
  27.8 123.5 %copy-start.64 = (pred[6]{0:T(512)(128)(4,1)}, pred[6]{0:T(512)(128)(4,1)S(1)}, u32[]{:S(2)}) copy-start(pred[6]{0:T(512)(128)(4,1)S(1)} %get-tuple-element.1488) | copy-start | bytes 22
  28.0 8.9 copy-start.104
  28.0 9.0 copy-start.67
  28.0 121.8 %copy-start.82 = (s32[1024]{0:T(1024)}, s32[1024]{0:T(1024)S(1)}, u32[]{:S(2)}) copy-start(s32[1024]{0:T(1024)S(1)} %pad_clamp_fusion.3) | copy-start | bytes 12292
  28.2 8.9 copy-start.106
  28.2 121.5 %copy-start.71 = (pred[6]{0:T(512)(128)(4,1)}, pred[6]{0:T(512)(128)(4,1)S(1)}, u32[]{:S(2)}) copy-start(pred[6]{0:T(512)(128)(4,1)S(1)} %get-tuple-element.1484) | copy-start | bytes 22
  28.2 120.9 %copy-start.83 = (s32[1024]{0:T(1024)}, s32[1024]{0:T(1024)S(1)}, u32[]{:S(2)}) copy-start(s32[1024]{0:T(1024)S(1)} %pad_clamp_fusion.2) | copy-start | bytes 12292
  28.2 117.4 %copy-start.77 = (pred[6]{0:T(512)(128)(4,1)}, pred[6]{0:T(512)(128)(4,1)S(1)}, u32[]{:S(2)}) copy-start(pred[6]{0:T(512)(128)(4,1)S(1)} %get-tuple-element.1700) | copy-start | bytes 22
  28.2 118.2 %copy-start.74 = (pred[6]{0:T(512)(128)(4,1)}, pred[6]{0:T(512)(128)(4,1)S(1)}, u32[]{:S(2)}) copy-start(pred[6]{0:T(512)(128)(4,1)S(1)} %get-tuple-element.1480) | copy-start | bytes 22
  30.0 13.0 %copy-start.108 = (bf16[6]{0:T(256)(128)(2,1)}, bf16[6]{0:T(256)(128)(2,1)S(1)}, u32[]{:S(2)}) copy-start(bf16[6]{0:T(256)(128)(2,1)S(1)} %convert_reduce_fusion.8) | copy-start | bytes 40
  36.2 21.4 %copy-start.41 = (bf16[32,864]{1,0:T(8,128)(2,1)S(1)}, bf16[32,864]{1,0:T(8,128)(2,1)}, u32[]{:S(2)}) copy-start(bf16[32,864]{1,0:T(8,128)(2,1)} %param.185) | copy-start | bytes 165892
  130.4 15.2 %copy-start.101 = (bf16[6]{0:T(256)(128)(2,1)S(1)}, bf16[6]{0:T(256)(128)(2,1)}, u32[]{:S(2)}) copy-start(bf16[6]{0:T(256)(128)(2,1)} %copy-done.100) | copy-start | bytes 40
  130.9 15.6 %copy-start.99 = (bf16[6]{0:T(256)(128)(2,1)S(1)}, bf16[6]{0:T(256)(128)(2,1)}, u32[]{:S(2)}) copy-start(bf16[6]{0:T(256)(128)(2,1)} %copy-done.98) | copy-start | bytes 40
  131.3 17.7 %collective-permute-start.7 = (bf16[6,32,64]{1,2,0:T(8,128)(2,1)S(1)}, bf16[6,32,64]{1,2,0:T(8,128)(2,1)S(1)}, u32[]{:S(2)}, u32[]{:S(2)}) collective-permute-start(bf16[6,32,64]{1,2,0:T(8,128)(2,1)S(1)} %get-tuple-element.1680), channel_id=1, source_target_pairs={{1,0},{2,1},{3,2},{4,3},{5,4},{6,5},{7,6},{8,7},{9,8},{10,9},{11,1... | collective-permute-start | bytes 73736 | tf_op jit(solution)/shard_map/ppermute | solution.py:14
  134.5 15.3 %collective-permute-start.6 = (bf16[6,32,64]{1,2,0:T(8,128)(2,1)S(1)}, bf16[6,32,64]{1,2,0:T(8,128)(2,1)S(1)}, u32[]{:S(2)}, u32[]{:S(2)}) collective-permute-start(bf16[6,32,64]{1,2,0:T(8,128)(2,1)S(1)} %get-tuple-element.1681), channel_id=1, source_target_pairs={{0,1},{1,2},{2,3},{3,4},{4,5},{5,6},{6,7},{7,8},{8,9},{9,10},{10,1... | collective-permute-start | bytes 73736 | tf_op jit(solution)/shard_map/ppermute | solution.py:14
  136.4 14.1 %collective-permute-start.5 = (bf16[6,32,64]{1,2,0:T(8,128)(2,1)S(1)}, bf16[6,32,64]{1,2,0:T(8,128)(2,1)S(1)}, u32[]{:S(2)}, u32[]{:S(2)}) collective-permute-start(bf16[6,32,64]{1,2,0:T(8,128)(2,1)S(1)} %get-tuple-element.1682), channel_id=1, source_target_pairs={{32,0},{64,32},{96,64},{128,96},{160,128},{192,160},{224,192},{33,... | collective-permute-start | bytes 73736 | tf_op jit(solution)/shard_map/ppermute | solution.py:14
  138.3 13.1 %collective-permute-start.4 = (bf16[6,32,64]{1,2,0:T(8,128)(2,1)S(1)}, bf16[6,32,64]{1,2,0:T(8,128)(2,1)S(1)}, u32[]{:S(2)}, u32[]{:S(2)}) collective-permute-start(bf16[6,32,64]{1,2,0:T(8,128)(2,1)S(1)} %get-tuple-element.1683), channel_id=1, source_target_pairs={{0,32},{32,64},{64,96},{96,128},{128,160},{160,192},{192,224},{1,3... | collective-permute-start | bytes 73736 | tf_op jit(solution)/shard_map/ppermute | solution.py:14
  150.4 21.5 %copy-start.40 = (bf16[32,864]{1,0:T(8,128)(2,1)S(1)}, bf16[32,864]{1,0:T(8,128)(2,1)}, u32[]{:S(2)}) copy-start(bf16[32,864]{1,0:T(8,128)(2,1)} %param.186) | copy-start | bytes 165892
  500.3 12.1 copy-start.46
  500.3 12.7 %copy-start.47 = (f32[6,32,8,1,8]{1,4,3,0,2:T(8,128)}, f32[6,32,8,1,8]{1,4,3,0,2:T(8,128)S(1)}, u32[]{:S(2)}) copy-start(f32[6,32,8,1,8]{1,4,3,0,2:T(8,128)S(1)} %get-tuple-element.1670) | copy-start | bytes 147460
  507.2 100.5 %collective-permute-start.11 = (bf16[6,32,64]{1,2,0:T(8,128)(2,1)}, bf16[6,32,64]{1,2,0:T(8,128)(2,1)}, u32[]{:S(2)}, u32[]{:S(2)}) collective-permute-start(bf16[6,32,64]{1,2,0:T(8,128)(2,1)} %bitcast.399), channel_id=1, source_target_pairs={{1,0},{2,1},{3,2},{4,3},{5,4},{6,5},{7,6},{8,7},{9,8},{10,9},{11,1... | collective-permute-start | bytes 73736 | tf_op jit(solution)/shard_map/ppermute | solution.py:14
  513.0 95.6 %collective-permute-start.10 = (bf16[6,32,64]{1,2,0:T(8,128)(2,1)}, bf16[6,32,64]{1,2,0:T(8,128)(2,1)}, u32[]{:S(2)}, u32[]{:S(2)}) collective-permute-start(bf16[6,32,64]{1,2,0:T(8,128)(2,1)} %bitcast.398), channel_id=1, source_target_pairs={{0,1},{1,2},{2,3},{3,4},{4,5},{5,6},{6,7},{7,8},{8,9},{9,10},{10,1... | collective-permute-start | bytes 73736 | tf_op jit(solution)/shard_map/ppermute | solution.py:14
  514.9 95.5 %collective-permute-start.9 = (bf16[6,32,64]{1,2,0:T(8,128)(2,1)}, bf16[6,32,64]{1,2,0:T(8,128)(2,1)}, u32[]{:S(2)}, u32[]{:S(2)}) collective-permute-start(bf16[6,32,64]{1,2,0:T(8,128)(2,1)} %get-tuple-element.1674), channel_id=1, source_target_pairs={{32,0},{64,32},{96,64},{128,96},{160,128},{192,160},{224,192},{33,... | collective-permute-start | bytes 73736 | tf_op jit(solution)/shard_map/ppermute | solution.py:14
  516.9 98.3 %collective-permute-start.8 = (bf16[6,32,64]{1,2,0:T(8,128)(2,1)}, bf16[6,32,64]{1,2,0:T(8,128)(2,1)}, u32[]{:S(2)}, u32[]{:S(2)}) collective-permute-start(bf16[6,32,64]{1,2,0:T(8,128)(2,1)} %get-tuple-element.1675), channel_id=1, source_target_pairs={{0,32},{32,64},{64,96},{96,128},{128,160},{160,192},{192,224},{1,3... | collective-permute-start | bytes 73736 | tf_op jit(solution)/shard_map/ppermute | solution.py:14
  526.8 73.1 %copy-start.78 = (pred[6]{0:T(512)(128)(4,1)S(1)}, pred[6]{0:T(512)(128)(4,1)}, u32[]{:S(2)}) copy-start(pred[6]{0:T(512)(128)(4,1)} %copy-done.77) | copy-start | bytes 22
  526.8 73.1 %copy-start.96 = (f32[6]{0:T(128)S(1)}, f32[6]{0:T(128)}, u32[]{:S(2)}) copy-start(f32[6]{0:T(128)} %get-tuple-element.1690) | copy-start | bytes 76
  526.8 74.1 %copy-start.75 = (pred[6]{0:T(512)(128)(4,1)S(1)}, pred[6]{0:T(512)(128)(4,1)}, u32[]{:S(2)}) copy-start(pred[6]{0:T(512)(128)(4,1)} %copy-done.74) | copy-start | bytes 22
  526.8 74.1 %copy-start.94 = (f32[6]{0:T(128)S(1)}, f32[6]{0:T(128)}, u32[]{:S(2)}) copy-start(f32[6]{0:T(128)} %get-tuple-element.1468) | copy-start | bytes 76
  878.1 92.7 %copy-start.79 = (pred[6]{0:T(512)(128)(4,1)S(1)}, pred[6]{0:T(512)(128)(4,1)}, u32[]{:S(2)}) copy-start(pred[6]{0:T(512)(128)(4,1)} %copy-done.77) | copy-start | bytes 22
  878.1 92.7 %copy-start.97 = (f32[6]{0:T(128)S(1)}, f32[6]{0:T(128)}, u32[]{:S(2)}) copy-start(f32[6]{0:T(128)} %get-tuple-element.1690) | copy-start | bytes 76
  951.2 21.4 %copy-start.76 = (pred[6]{0:T(512)(128)(4,1)S(1)}, pred[6]{0:T(512)(128)(4,1)}, u32[]{:S(2)}) copy-start(pred[6]{0:T(512)(128)(4,1)} %copy-done.74) | copy-start | bytes 22
  951.2 21.4 %copy-start.95 = (f32[6]{0:T(128)S(1)}, f32[6]{0:T(128)}, u32[]{:S(2)}) copy-start(f32[6]{0:T(128)} %get-tuple-element.1468) | copy-start | bytes 76
  951.2 21.5 %copy-start.45 = (f32[6,32,8,1,8]{1,4,3,0,2:T(8,128)S(1)}, f32[6,32,8,1,8]{1,4,3,0,2:T(8,128)}, u32[]{:S(2)}) copy-start(f32[6,32,8,1,8]{1,4,3,0,2:T(8,128)} %get-tuple-element.1662) | copy-start | bytes 147460
  951.2 21.5 %copy-start.44 = (f32[6,32,8,1,8]{1,4,3,0,2:T(8,128)S(1)}, f32[6,32,8,1,8]{1,4,3,0,2:T(8,128)}, u32[]{:S(2)}) copy-start(f32[6,32,8,1,8]{1,4,3,0,2:T(8,128)} %get-tuple-element.1663) | copy-start | bytes 147460
  952.2 23.4 %collective-permute-start.15 = (bf16[6,32,64]{1,2,0:T(8,128)(2,1)S(1)}, bf16[6,32,64]{1,2,0:T(8,128)(2,1)S(1)}, u32[]{:S(2)}, u32[]{:S(2)}) collective-permute-start(bf16[6,32,64]{1,2,0:T(8,128)(2,1)S(1)} %bitcast.985), channel_id=1, source_target_pairs={{1,0},{2,1},{3,2},{4,3},{5,4},{6,5},{7,6},{8,7},{9,8},{10,9},{11,1... | collective-permute-start | bytes 73736 | tf_op jit(solution)/shard_map/ppermute | solution.py:14
  959.0 16.7 %collective-permute-start.14 = (bf16[6,32,64]{1,2,0:T(8,128)(2,1)}, bf16[6,32,64]{1,2,0:T(8,128)(2,1)}, u32[]{:S(2)}, u32[]{:S(2)}) collective-permute-start(bf16[6,32,64]{1,2,0:T(8,128)(2,1)} %bitcast.400), channel_id=1, source_target_pairs={{0,1},{1,2},{2,3},{3,4},{4,5},{5,6},{6,7},{7,8},{8,9},{9,10},{10,1... | collective-permute-start | bytes 73736 | tf_op jit(solution)/shard_map/ppermute | solution.py:14
  960.9 16.6 %collective-permute-start.13 = (bf16[6,32,64]{1,2,0:T(8,128)(2,1)}, bf16[6,32,64]{1,2,0:T(8,128)(2,1)}, u32[]{:S(2)}, u32[]{:S(2)}) collective-permute-start(bf16[6,32,64]{1,2,0:T(8,128)(2,1)} %get-tuple-element.1666), channel_id=1, source_target_pairs={{32,0},{64,32},{96,64},{128,96},{160,128},{192,160},{224,192},{33,... | collective-permute-start | bytes 73736 | tf_op jit(solution)/shard_map/ppermute | solution.py:14
  963.4 18.1 %collective-permute-start.12 = (bf16[6,32,64]{1,2,0:T(8,128)(2,1)}, bf16[6,32,64]{1,2,0:T(8,128)(2,1)}, u32[]{:S(2)}, u32[]{:S(2)}) collective-permute-start(bf16[6,32,64]{1,2,0:T(8,128)(2,1)} %get-tuple-element.1667), channel_id=1, source_target_pairs={{0,32},{32,64},{64,96},{96,128},{128,160},{160,192},{192,224},{1,3... | collective-permute-start | bytes 73736 | tf_op jit(solution)/shard_map/ppermute | solution.py:14
  (147 other events, 672.1 us)
Sparse Core Ops, SparseCore 0:
  975.7 251.8 all-reduce.6
where the time goes:
time: 1260 us; the launch traced here: 1240 us
  local copies, waits for them, and re-layouts  823 us (65%)
  waiting for transfers between devices  233 us (18%)
  starting transfers between devices  60.4 us (5%)
  other arithmetic  55.3 us (4%)
  matrix products  28.2 us (2%)
  loops' own time  21.4 us (2%)
  between operations  16.4 us (1%)
    scatter-add x114, local copies, waits for them, and re-layouts, spread_taps(): cells = cells.at[:, :, first:first + EDGE, second:second + EDGE, third:th...  317 us
    psum x1, waiting for transfers between devices, body(): lax.psum((term_first, term_second), ('tx', 'ty'))  233 us
    reshape x324, local copies, waits for them, and re-layouts, columns(): pieces.append(piece.reshape(count, chans, EDGE * EDGE * EDGE))  198 us
    slice x174, local copies, waits for them, and re-layouts, spread_taps(): spread[:, tap * chans:(tap + 1) * chans]  93.9 us
    ppermute x16, starting transfers between devices, passed_along(): lax.ppermute(value, axis, [(source, source + steps) for source in range(f...  60.4 us
    slice x24, local copies, waits for them, and re-layouts, columns(): block[:, :, first:first + EDGE, second:second + EDGE, third:third + EDGE]  46.2 us
  transfers between devices with their start and end apart: 17, of which 1 were waited for; matrix products, arithmetic and copies ran while one was open for 11% of the time, Pallas kernels for 0%

commit v1 on v0

v1 whole, which is shorter than its diff:
```python
import functools
import math

import jax
import jax.numpy as jnp
import numpy as np
from jax import lax
from jax.experimental import pallas as pl
from jax.experimental.pallas import tpu as pltpu
from jax.sharding import PartitionSpec as P

EDGE = 8
LANES = 128
PITCH = 10
SLOTS = 6
CHANS = 32
INNER = EDGE * LANES
WHOLE = (EDGE + 2) * LANES
BF16 = jnp.bfloat16
F32 = jnp.float32
VMEM_LIMIT = 24 * 1024 * 1024


def lane_of(row, col):
    return (row + 1) * PITCH + col + 1


def spread_matrix():
    out = np.zeros((2 * EDGE * EDGE, 2 * LANES), np.float32)
    for half in range(2):
        for row in range(EDGE):
            for col in range(EDGE):
                out[half * 64 + row * EDGE + col, half * LANES + lane_of(row, col)] = 1
    return out


def face_matrices():
    pick = np.zeros((INNER, 256), np.float32)
    put = np.zeros((256, INNER), np.float32)
    for plane in range(EDGE):
        base = plane * LANES
        for at in range(EDGE):
            col = plane * EDGE + at
            pick[base + lane_of(EDGE - 1, at), col] = 1
            pick[base + lane_of(0, at), 64 + col] = 1
            pick[base + lane_of(at, EDGE - 1), 128 + col] = 1
            pick[base + lane_of(at, 0), 192 + col] = 1
            put[col, base + lane_of(-1, at)] = 1
            put[64 + col, base + lane_of(EDGE, at)] = 1
            put[128 + col, base + lane_of(at, -1)] = 1
            put[192 + col, base + lane_of(at, EDGE)] = 1
    return pick, put


SPREAD = spread_matrix()
PICK, PUT = face_matrices()


def dot(lhs, rhs):
    return jnp.dot(lhs, rhs, preferred_element_type=F32)


def spread(field, matrix):
    return [dot(field[:, at * LANES : (at + 1) * LANES], matrix) for at in range(4)]


def emit_faces(inner_ref, pick_ref, low_ref, high_ref, side_ref):
    low_ref[...] = inner_ref[:, :, :LANES]
    high_ref[...] = inner_ref[:, :, INNER - LANES :]
    flat = inner_ref[...].reshape(SLOTS * CHANS, INNER)
    side_ref[...] = dot(flat, pick_ref[...]).astype(BF16).reshape(SLOTS, CHANS, 256)


def build_cells(cells_ref, sheet_ref, inner_ref, side_ref, remote_refs, put_ref, neighbours_ref, base):
    lane = lax.broadcasted_iota(jnp.int32, (1, LANES), 1)
    lower = (lane < 64).astype(F32).astype(BF16)
    upper = (lane >= 64).astype(F32).astype(BF16)
    zero = jnp.zeros((CHANS, LANES), BF16)

    def picked(slot, face, local, remote_ref):
        ident = neighbours_ref[slot, face]
        place = lax.rem(jnp.maximum(ident, 0), SLOTS)
        value = local(place)
        if remote_ref is not None:
            here = (ident >= base) & (ident < base + SLOTS)
            value = jnp.where(here, value, remote_ref[place])
        return jnp.where(ident >= 0, value, zero)

    rows_ref, cols_ref, before_ref, after_ref = remote_refs
    for slot in range(SLOTS):
        cells_ref[slot, :, :LANES] = picked(
            slot, 0, lambda at: inner_ref[at, :, INNER - LANES :], rows_ref
        )
        cells_ref[slot, :, WHOLE - LANES :] = picked(
            slot, 1, lambda at: inner_ref[at, :, :LANES], cols_ref
        )
        sides = lambda at: side_ref[at, :, :LANES]
        ends = lambda at: side_ref[at, :, LANES:]
        rows = pl.ds(slot * CHANS, CHANS)
        sheet_ref[rows, :LANES] = (
            picked(slot, 2, sides, before_ref) * lower + picked(slot, 3, sides, after_ref) * upper
        )
        sheet_ref[rows, LANES:] = (
            picked(slot, 4, ends, None) * lower + picked(slot, 5, ends, None) * upper
        )
    halo = dot(sheet_ref[...], put_ref[...]).astype(BF16).reshape(SLOTS, CHANS, INNER)
    cells_ref[:, :, LANES : LANES + INNER] = inner_ref[...] + halo


def shift_planes(columns_ref, cells_ref, slot):
    for plane in range(EDGE + 2):
        span = slice(plane * LANES, (plane + 1) * LANES)
        tile = cells_ref[slot, :, span]
        for tap in range(9):
            shift = (tap // 3 - 1) * PITCH + tap % 3 - 1
            moved = tile if shift == 0 else pltpu.roll(tile, (-shift) % LANES, 1)
            columns_ref[tap * CHANS : (tap + 1) * CHANS, span] = moved


def stacked(weight):
    return jnp.concatenate([weight[:, at * 288 : (at + 1) * 288] for at in range(3)], axis=0)


def convolve(columns_ref, weight):
    raw = dot(weight, columns_ref[...])
    return (
        raw[:CHANS, :INNER]
        + raw[CHANS : 2 * CHANS, LANES : LANES + INNER]
        + raw[2 * CHANS :, 2 * LANES :]
    )


def enter_kernel(features_ref, occupancy_ref, spread_ref, pick_ref, inner_ref, mask_ref, low_ref, high_ref, side_ref):
    mask = occupancy_ref[...].astype(F32).astype(BF16)
    matrix = spread_ref[...]
    for at, part in enumerate(spread(mask, matrix)):
        mask_ref[:, at * 256 : (at + 1) * 256] = part
    masked = jnp.concatenate(
        [features_ref[slot] * mask[slot : slot + 1, :] for slot in range(SLOTS)], axis=0
    )
    for at, part in enumerate(spread(masked, matrix)):
        inner_ref[:, :, at * 256 : (at + 1) * 256] = part.astype(BF16).reshape(SLOTS, CHANS, 256)
    emit_faces(inner_ref, pick_ref, low_ref, high_ref, side_ref)


def spread_kernel(cotangent_ref, mask_ref, spread_ref, out_ref):
    flat = cotangent_ref[...].reshape(SLOTS * CHANS, 512)
    for at, part in enumerate(spread(flat, spread_ref[...])):
        span = slice(at * 256, (at + 1) * 256)
        for slot in range(SLOTS):
            out_ref[slot, :, span] = (
                part[slot * CHANS : (slot + 1) * CHANS] * mask_ref[slot : slot + 1, span]
            ).astype(BF16)


def first_kernel(neighbours_ref, base_ref, inner_ref, side_ref, r0, r1, r2, r3, put_ref, pick_ref, weight_ref, mask_ref,
                 cells_ref, hidden_ref, low_ref, high_ref, hidden_side_ref, sheet_ref, columns_ref):
    build_cells(cells_ref, sheet_ref, inner_ref, side_ref, (r0, r1, r2, r3), put_ref, neighbours_ref, base_ref[0])
    weight = stacked(weight_ref[...])
    for slot in range(SLOTS):
        buffer = columns_ref.at[slot % 2]
        shift_planes(buffer, cells_ref, slot)
        pre = convolve(buffer, weight)
        hidden_ref[slot] = (jnp.maximum(pre, 0.0) * mask_ref[slot : slot + 1, :]).astype(BF16)
    emit_faces(hidden_ref, pick_ref, low_ref, high_ref, hidden_side_ref)


def pack_rows(inner, gather):
    return [dot(inner[:, at * 256 : (at + 1) * 256], gather) for at in range(4)]


def second_kernel(neighbours_ref, base_ref, inner_ref, side_ref, r0, r1, r2, r3, put_ref, pick_ref, gather_ref, weight_ref,
                  mask_ref, skip_ref, cotangent_ref,
                  cells_ref, result_ref, grad_ref, low_ref, high_ref, grad_side_ref, sheet_ref, columns_ref, wide_ref):
    build_cells(cells_ref, sheet_ref, inner_ref, side_ref, (r0, r1, r2, r3), put_ref, neighbours_ref, base_ref[0])
    weight = stacked(weight_ref[...])
    for slot in range(SLOTS):
        buffer = columns_ref.at[slot % 2]
        shift_planes(buffer, cells_ref, slot)
        pre = convolve(buffer, weight) + skip_ref[slot].astype(F32)
        wide_ref[slot] = (jnp.maximum(pre, 0.0) * mask_ref[slot : slot + 1, :]).astype(BF16)
        grad_ref[slot] = jnp.where(pre > 0.0, cotangent_ref[slot].astype(F32), 0.0).astype(BF16)
    emit_faces(grad_ref, pick_ref, low_ref, high_ref, grad_side_ref)
    flat = wide_ref[...].reshape(SLOTS * CHANS, INNER)
    for at, part in enumerate(pack_rows(flat, gather_ref[...])):
        result_ref[:, :, at * LANES : (at + 1) * LANES] = part.astype(BF16).reshape(SLOTS, CHANS, LANES)


def third_kernel(neighbours_ref, base_ref, inner_ref, side_ref, r0, r1, r2, r3, put_ref, pick_ref, weight_ref, mask_ref,
                 hidden_ref, grad_ref, low_ref, high_ref, grad_side_ref, cells_ref, sheet_ref, columns_ref):
    build_cells(cells_ref, sheet_ref, inner_ref, side_ref, (r0, r1, r2, r3), put_ref, neighbours_ref, base_ref[0])
    weight = weight_ref[...]
    for slot in range(SLOTS):
        buffer = columns_ref.at[slot % 2]
        shift_planes(buffer, cells_ref, slot)
        grad = convolve(buffer, weight) * mask_ref[slot : slot + 1, :]
        grad_ref[slot] = jnp.where(hidden_ref[slot].astype(F32) > 0.0, grad, 0.0).astype(BF16)
    emit_faces(grad_ref, pick_ref, low_ref, high_ref, grad_side_ref)


def last_kernel(neighbours_ref, base_ref, inner_ref, side_ref, r0, r1, r2, r3, put_ref, gather_ref, weight_ref, mask_ref,
                grad_ref, out_ref, cells_ref, sheet_ref, columns_ref, wide_ref):
    build_cells(cells_ref, sheet_ref, inner_ref, side_ref, (r0, r1, r2, r3), put_ref, neighbours_ref, base_ref[0])
    weight = weight_ref[...]
    for slot in range(SLOTS):
        buffer = columns_ref.at[slot % 2]
        shift_planes(buffer, cells_ref, slot)
        grad = convolve(buffer, weight) + grad_ref[slot].astype(F32)
        wide_ref[slot] = (grad * mask_ref[slot : slot + 1, :]).astype(BF16)
    flat = wide_ref[...].reshape(SLOTS * CHANS, INNER)
    for at, part in enumerate(pack_rows(flat, gather_ref[...])):
        out_ref[:, :, at * LANES : (at + 1) * LANES] = part.astype(BF16).reshape(SLOTS, CHANS, LANES)


def weight_kernel(cells_ref, grad_ref, out_ref, columns_ref, grads_ref):
    grads_ref[...] = jnp.zeros_like(grads_ref)
    total = jnp.zeros((9 * CHANS, 3 * CHANS), F32)
    for slot in range(SLOTS):
        buffer = columns_ref.at[slot % 2]
        shift_planes(buffer, cells_ref, slot)
        spot = grads_ref.at[slot % 2]
        for at in range(3):
            spot[at * CHANS : (at + 1) * CHANS, at * LANES : at * LANES + INNER] = grad_ref[slot]
        total = total + lax.dot_general(
            buffer[...], spot[...], (((1,), (1,)), ((), ())), preferred_element_type=F32
        )
    turned = total.T
    for at in range(3):
        out_ref[:, at * 288 : (at + 1) * 288] = turned[at * CHANS : (at + 1) * CHANS]


def shape(dims, dtype=BF16):
    return jax.ShapeDtypeStruct(dims, dtype)


FIELD = (SLOTS, CHANS, 512)
INSIDE = (SLOTS, CHANS, INNER)
CELLS = (SLOTS, CHANS, WHOLE)
FACE = (SLOTS, CHANS, LANES)
SIDE = (SLOTS, CHANS, 2 * LANES)
FACES = [shape(FACE), shape(FACE), shape(SIDE)]
SCRATCH = [pltpu.VMEM((SLOTS * CHANS, 256), BF16), pltpu.VMEM((2, 9 * CHANS, WHOLE), BF16)]


def call(kernel, outs, scratch, scalars, flops, name):
    def run(*args):
        specs = [
            pl.BlockSpec(memory_space=pltpu.SMEM if at < scalars else pltpu.VMEM)
            for at in range(len(args))
        ]
        moved = sum(a.size * a.dtype.itemsize for a in args)
        moved += sum(math.prod(o.shape) * o.dtype.itemsize for o in outs)
        result = pl.pallas_call(
            kernel,
            out_shape=outs,
            in_specs=specs,
            out_specs=[pl.BlockSpec(memory_space=pltpu.VMEM)] * len(outs),
            scratch_shapes=scratch,
            compiler_params=pltpu.CompilerParams(vmem_limit_bytes=VMEM_LIMIT),
            cost_estimate=pl.CostEstimate(flops=flops, bytes_accessed=moved, transcendentals=0),
            name=name,
        )(*args)
        return result

    return run


def passed_along(value, axis, steps):
    count = lax.axis_size(axis)
    first, last = (max(0, -steps), min(count, count - steps))
    return lax.ppermute(value, axis, [(source, source + steps) for source in range(first, last)])


def exchanged(low, high, side):
    return (
        passed_along(high, "tx", 1),
        passed_along(low, "tx", -1),
        passed_along(side[:, :, :LANES], "ty", 1),
        passed_along(side[:, :, :LANES], "ty", -1),
    )


def swapped(value, axis, bit):
    count = lax.axis_size(axis)
    return lax.ppermute(value, axis, [(at, at ^ bit) for at in range(count)])


def summed(first, second):
    odd = lax.rem(lax.axis_index("ty"), 2) == 1
    kept = jnp.where(odd, second, first)
    total = kept + swapped(jnp.where(odd, first, second), "ty", 1)
    for axis, bit in (("ty", 2), ("ty", 4), ("ty", 8), ("ty", 16), ("tx", 1), ("tx", 2), ("tx", 4)):
        mine = total.astype(BF16)
        total = mine.astype(F32) + swapped(mine, axis, bit).astype(F32)
    other = swapped(total, "ty", 1)
    return jnp.where(odd, other, total), jnp.where(odd, total, other)


def turned(weight):
    taps = weight.reshape(CHANS, 3, 3, 3, CHANS)[:, ::-1, ::-1, ::-1]
    return taps.transpose(1, 4, 2, 3, 0).reshape(3 * CHANS, 9 * CHANS)


CONV_FLOPS = 2 * 96 * 288 * WHOLE * SLOTS


def body(features, occupancy, neighbours, w_first, w_second, cotangent):
    myself = lax.axis_index("tx") * lax.axis_size("ty") + lax.axis_index("ty")
    base = (myself * SLOTS).astype(jnp.int32).reshape(1)
    widen = jnp.asarray(SPREAD, BF16)
    narrow = jnp.asarray(SPREAD.T, BF16)
    pick = jnp.asarray(PICK, BF16)
    put = jnp.asarray(PUT, BF16)
    x_inner, mask, low, high, side = call(
        enter_kernel, [shape(INSIDE), shape((SLOTS, INNER), F32)] + FACES, [], 0, 2 * 192 * 512 * 1024, "enter"
    )(features, occupancy, widen, pick)
    remote = exchanged(low, high, side)
    (cot_inner,) = call(spread_kernel, [shape(INSIDE)], [], 0, 2 * 192 * 512 * 256, "spread")(
        cotangent, mask, widen
    )
    back_second, back_first = turned(w_second), turned(w_first)
    x_cells, hidden, low, high, hidden_side = call(
        first_kernel, [shape(CELLS), shape(INSIDE)] + FACES, SCRATCH, 2, CONV_FLOPS, "first"
    )(neighbours, base, x_inner, side, *remote, put, pick, w_first, mask)
    remote = exchanged(low, high, hidden_side)
    hidden_cells, result, grad_two, low, high, grad_side = call(
        second_kernel,
        [shape(CELLS), shape(FIELD), shape(INSIDE)] + FACES,
        SCRATCH + [pltpu.VMEM(INSIDE, BF16)],
        2,
        CONV_FLOPS,
        "second",
    )(neighbours, base, hidden, hidden_side, *remote, put, pick, narrow, w_second, mask, x_inner, cot_inner)
    remote = exchanged(low, high, grad_side)
    weight_scratch = [SCRATCH[1], pltpu.VMEM((2, 3 * CHANS, WHOLE), BF16)]
    weight_call = call(weight_kernel, [shape((CHANS, 27 * CHANS), F32)], weight_scratch, 0, CONV_FLOPS, "weights")
    (term_second,) = weight_call(hidden_cells, grad_two)
    grad_one, low, high, one_side = call(
        third_kernel, [shape(INSIDE)] + FACES, [pltpu.VMEM(CELLS, BF16)] + SCRATCH, 2, CONV_FLOPS, "third"
    )(neighbours, base, grad_two, grad_side, *remote, put, pick, back_second, mask, hidden)
    remote = exchanged(low, high, one_side)
    (term_first,) = weight_call(x_cells, grad_one)
    (grad_features,) = call(
        last_kernel,
        [shape(FIELD)],
        [pltpu.VMEM(CELLS, BF16)] + SCRATCH + [pltpu.VMEM(INSIDE, BF16)],
        2,
        CONV_FLOPS,
        "last",
    )(neighbours, base, grad_one, one_side, *remote, put, narrow, back_first, mask, grad_two)
    total_first, total_second = summed(term_first, term_second)
    scale = 1.0 / math.sqrt(SLOTS * lax.axis_size("tx") * lax.axis_size("ty") * EDGE**3)
    return (result, grad_features, total_first * scale, total_second * scale)


def solution(mesh):
    return jax.shard_map(
        body,
        mesh=mesh,
        in_specs=(
            P(("tx", "ty"), None, None),
            P(("tx", "ty"), None),
            P(("tx", "ty"), None),
            P(),
            P(),
            P(("tx", "ty"), None, None),
        ),
        out_specs=(P(("tx", "ty"), None, None), P(("tx", "ty"), None, None), P(), P()),
        check_vma=False,
    )
```

time: 1260 us -> 146 us (0.12); the launches traced: 1240 us -> 146 us
  local copies, waits for them, and re-layouts: 823 us -> 11.1 us
  waiting for transfers between devices: 233 us -> 45.8 us
  other arithmetic: 55.3 us -> 0.87 us
  matrix products: 28.2 us -> 0 us
  loops' own time: 21.4 us -> 0 us
  Pallas kernels: 0 us -> 16.7 us
  between operations: 16.4 us -> 1.16 us
    scatter-add x120 -> x0, local copies, waits for them, and re-layouts: 333 us -> none  [the longest x114 317 us: spread_taps(): cells = cells.at[:, :, first:first + EDGE, second:second + EDGE, third:th...]
    psum x1 -> x0, waiting for transfers between devices: 233 us -> none  [body(): lax.psum((term_first, term_second), ('tx', 'ty'))]
    reshape x324 -> x4, local copies, waits for them, and re-layouts: 198 us -> 0.77 us  [the longest x2 0.39 us: turned(): taps = weight.reshape(CHANS, 3, 3, 3, CHANS)[:, ::-1, ::-1, ::-1]]
    slice x218 -> x4, local copies, waits for them, and re-layouts: 161 us -> 0.04 us  [exchanged(): side[:, :, :LANES]]
    scatter x12 -> x0, local copies, waits for them, and re-layouts: 37.9 us -> none  [the longest x2 12.1 us: padded(): cells = cells.at[:, :, 1:-1, 1:-1, 0].set(sheet[4])]
    ppermute x0 -> x9, waiting for transfers between devices: none -> 31.8 us  [swapped(): return lax.ppermute(value, axis, [(at, at ^ bit) for at in range(count)])]
    dot_general x18 -> x0, matrix products: 28.2 us -> none  [the longest x6 12.7 us: weight_one_block(): jnp.einsum('gov,gkv->ok', pair[1], columns(pair[0]), preferred_element_ty...]
    add x106 -> x1, other arithmetic: 21.8 us -> 0.01 us  [summed(): total = mine.astype(F32) + swapped(mine, axis, bit).astype(F32)]
  transfers between devices with their start and end apart: 17 -> 25, of which waited for: 1 -> 13; matrix products, arithmetic and copies ran while one was open for 11% -> 3% of each run, Pallas kernels for 0% -> 4%
where the time goes in v1:
time: 146 us
  starting transfers between devices  70.1 us (48%)
  waiting for transfers between devices  45.8 us (31%)
  Pallas kernels  16.7 us (11%)
  local copies, waits for them, and re-layouts  11.1 us (8%)
    ppermute x16, starting transfers between devices, passed_along(): lax.ppermute(value, axis, [(source, source + steps) for source in range(f...  62 us
    ppermute x9, waiting for transfers between devices, swapped(): return lax.ppermute(value, axis, [(at, at ^ bit) for at in range(count)])  31.8 us
    pallas_call x8, Pallas kernels, run(): pl.pallas_call(kernel, out_shape=outs, in_specs=specs, out_specs=[pl.Bloc...  16.7 us
    ppermute x16, waiting for transfers between devices, passed_along(): lax.ppermute(value, axis, [(source, source + steps) for source in range(f...  14.1 us
    ppermute x9, starting transfers between devices, swapped(): return lax.ppermute(value, axis, [(at, at ^ bit) for at in range(count)])  8.1 us
    unnamed x30, local copies, waits for them, and re-layouts  6.45 us
  transfers between devices with their start and end apart: 25, of which 13 were waited for; matrix products, arithmetic and copies ran while one was open for 3% of the time, Pallas kernels for 4%

profile of v1, /device:TPU:24, one launch (start us, length us, event | category | flops | bytes accessed | tf_op | source)
XLA Modules:
  0.0 145.7 jit_solution(3252329444180512752)
XLA Ops:
  0.7 1.1 copy-done.1
  1.7 0.8 copy-done.5
  2.6 0.9 copy-done.9
  3.5 0.7 copy-done.12
  4.8 1.9 %collective-permute-start.2 = (bf16[6,32,128]{2,1,0:T(8,128)(2,1)S(1)}, bf16[6,32,128]{2,1,0:T(8,128)(2,1)S(1)}, u32[]{:S(2)}, u32[]{:S(2)}) collective-permute-start(bf16[6,32,128]{2,1,0:T(8,128)(2,1)S(1)} %slice.16), channel_id=1, source_target_pairs={{0,1},{1,2},{2,3},{3,4},{4,5},{5,6},{6,7},{7,8},{8,9},{9,10},{10,1... | collective-permute-start | bytes 147464 | tf_op jit(solution)/shard_map/ppermute | solution.py:271
  6.7 7.4 %collective-permute-start.3 = (bf16[6,32,128]{2,1,0:T(8,128)(2,1)S(1)}, bf16[6,32,128]{2,1,0:T(8,128)(2,1)S(1)}, u32[]{:S(2)}, u32[]{:S(2)}) collective-permute-start(bf16[6,32,128]{2,1,0:T(8,128)(2,1)S(1)} %slice.16), channel_id=1, source_target_pairs={{1,0},{2,1},{3,2},{4,3},{5,4},{6,5},{7,6},{8,7},{9,8},{10,9},{11,1... | collective-permute-start | bytes 147464 | tf_op jit(solution)/shard_map/ppermute | solution.py:271
  14.1 3.8 %collective-permute-start = (bf16[6,32,128]{2,1,0:T(8,128)(2,1)S(1)}, bf16[6,32,128]{2,1,0:T(8,128)(2,1)S(1)}, u32[]{:S(2)}, u32[]{:S(2)}) collective-permute-start(bf16[6,32,128]{2,1,0:T(8,128)(2,1)S(1)} %get-tuple-element.26), channel_id=1, source_target_pairs={{0,32},{32,64},{64,96},{96,128},{128,160},{160,192},{192,224},{1,3... | collective-permute-start | bytes 147464 | tf_op jit(solution)/shard_map/ppermute | solution.py:271
  17.9 3.6 %collective-permute-start.1 = (bf16[6,32,128]{2,1,0:T(8,128)(2,1)S(1)}, bf16[6,32,128]{2,1,0:T(8,128)(2,1)S(1)}, u32[]{:S(2)}, u32[]{:S(2)}) collective-permute-start(bf16[6,32,128]{2,1,0:T(8,128)(2,1)S(1)} %get-tuple-element.27), channel_id=1, source_target_pairs={{32,0},{64,32},{96,64},{128,96},{160,128},{192,160},{224,192},{33,... | collective-permute-start | bytes 147464 | tf_op jit(solution)/shard_map/ppermute | solution.py:271
  21.5 0.6 collective-permute-done.r0
  22.1 4.2 %collective-permute-done.1.r1 = bf16[6,32,128]{2,1,0:T(8,128)(2,1)S(1)} collective-permute-done((bf16[6,32,128]{2,1,0:T(8,128)(2,1)S(1)}, bf16[6,32,128]{2,1,0:T(8,128)(2,1)S(1)}, u32[]{:S(2)}, u32[]{:S(2)}) %collective-permute-start.1) | collective-permute-done | bytes 49184 | tf_op jit(solution)/shard_map/ppermute | solution.py:271
  26.3 1.0 copy-done.2
  27.4 2.5 %first.1 = (bf16[6,32,1280]{2,1,0:T(8,128)(2,1)S(1)}, bf16[6,32,1024]{2,1,0:T(8,128)(2,1)S(1)}, bf16[6,32,128]{2,1,0:T(8,128)(2,1)S(1)}, bf16[6,32,128]{2,1,0:T(8,128)(2,1)S(1)}, bf16[6,32,256]{2,1,0:T(8,128)(2,1)S(1)}) custom-call(s32[6,6]{1,0:T(8,128)S(1)} %copy-done.11, s32[1]{0:T(128)} %bitcast.base_ref, ...), custom_call_target="tpu_custom_call" | custom-call | flops 424673280 | bytes 2898068 | tf_op jit(solution)/shard_map/first/pallas_call | solution.py:253
  29.9 2.1 %collective-permute-start.6 = (bf16[6,32,128]{2,1,0:T(8,128)(2,1)S(1)}, bf16[6,32,128]{2,1,0:T(8,128)(2,1)S(1)}, u32[]{:S(2)}, u32[]{:S(2)}) collective-permute-start(bf16[6,32,128]{2,1,0:T(8,128)(2,1)S(1)} %slice.17), channel_id=1, source_target_pairs={{0,1},{1,2},{2,3},{3,4},{4,5},{5,6},{6,7},{7,8},{8,9},{9,10},{10,1... | collective-permute-start | bytes 147464 | tf_op jit(solution)/shard_map/ppermute | solution.py:271
  32.0 5.8 %collective-permute-start.7 = (bf16[6,32,128]{2,1,0:T(8,128)(2,1)S(1)}, bf16[6,32,128]{2,1,0:T(8,128)(2,1)S(1)}, u32[]{:S(2)}, u32[]{:S(2)}) collective-permute-start(bf16[6,32,128]{2,1,0:T(8,128)(2,1)S(1)} %slice.17), channel_id=1, source_target_pairs={{1,0},{2,1},{3,2},{4,3},{5,4},{6,5},{7,6},{8,7},{9,8},{10,9},{11,1... | collective-permute-start | bytes 147464 | tf_op jit(solution)/shard_map/ppermute | solution.py:271
  37.7 3.6 %collective-permute-start.4 = (bf16[6,32,128]{2,1,0:T(8,128)(2,1)S(1)}, bf16[6,32,128]{2,1,0:T(8,128)(2,1)S(1)}, u32[]{:S(2)}, u32[]{:S(2)}) collective-permute-start(bf16[6,32,128]{2,1,0:T(8,128)(2,1)S(1)} %get-tuple-element.31), channel_id=1, source_target_pairs={{0,32},{32,64},{64,96},{96,128},{128,160},{160,192},{192,224},{1,3... | collective-permute-start | bytes 147464 | tf_op jit(solution)/shard_map/ppermute | solution.py:271
  41.4 3.9 %collective-permute-start.5 = (bf16[6,32,128]{2,1,0:T(8,128)(2,1)S(1)}, bf16[6,32,128]{2,1,0:T(8,128)(2,1)S(1)}, u32[]{:S(2)}, u32[]{:S(2)}) collective-permute-start(bf16[6,32,128]{2,1,0:T(8,128)(2,1)S(1)} %get-tuple-element.32), channel_id=1, source_target_pairs={{32,0},{64,32},{96,64},{128,96},{160,128},{192,160},{224,192},{33,... | collective-permute-start | bytes 147464 | tf_op jit(solution)/shard_map/ppermute | solution.py:271
  45.7 4.1 %collective-permute-done.5.r1 = bf16[6,32,128]{2,1,0:T(8,128)(2,1)S(1)} collective-permute-done((bf16[6,32,128]{2,1,0:T(8,128)(2,1)S(1)}, bf16[6,32,128]{2,1,0:T(8,128)(2,1)S(1)}, u32[]{:S(2)}, u32[]{:S(2)}) %collective-permute-start.5) | collective-permute-done | bytes 49184 | tf_op jit(solution)/shard_map/ppermute | solution.py:271
  49.9 3.4 %second.1 = (bf16[6,32,1280]{2,1,0:T(8,128)(2,1)S(1)}, bf16[6,32,512]{2,1,0:T(8,128)(2,1)}, bf16[6,32,1024]{2,1,0:T(8,128)(2,1)S(1)}, bf16[6,32,128]{2,1,0:T(8,1...) custom-call(s32[6,6]{1,0:T(8,128)S(1)} %copy-done.11, s32[1]{0:T(128)} %bitcast.base_ref, ...), custom_call_target="tpu_custom_call" | custom-call | flops 424673280 | bytes 3946644 | tf_op jit(solution)/shard_map/second/pallas_call | solution.py:253
  53.3 0.8 copy-done.13
  54.0 1.9 %collective-permute-start.10 = (bf16[6,32,128]{2,1,0:T(8,128)(2,1)S(1)}, bf16[6,32,128]{2,1,0:T(8,128)(2,1)S(1)}, u32[]{:S(2)}, u32[]{:S(2)}) collective-permute-start(bf16[6,32,128]{2,1,0:T(8,128)(2,1)S(1)} %slice.18), channel_id=1, source_target_pairs={{0,1},{1,2},{2,3},{3,4},{4,5},{5,6},{6,7},{7,8},{8,9},{9,10},{10,1... | collective-permute-start | bytes 147464 | tf_op jit(solution)/shard_map/ppermute | solution.py:271
  56.0 5.8 %collective-permute-start.11 = (bf16[6,32,128]{2,1,0:T(8,128)(2,1)S(1)}, bf16[6,32,128]{2,1,0:T(8,128)(2,1)S(1)}, u32[]{:S(2)}, u32[]{:S(2)}) collective-permute-start(bf16[6,32,128]{2,1,0:T(8,128)(2,1)S(1)} %slice.18), channel_id=1, source_target_pairs={{1,0},{2,1},{3,2},{4,3},{5,4},{6,5},{7,6},{8,7},{9,8},{10,9},{11,1... | collective-permute-start | bytes 147464 | tf_op jit(solution)/shard_map/ppermute | solution.py:271
  61.7 3.8 %collective-permute-start.8 = (bf16[6,32,128]{2,1,0:T(8,128)(2,1)S(1)}, bf16[6,32,128]{2,1,0:T(8,128)(2,1)S(1)}, u32[]{:S(2)}, u32[]{:S(2)}) collective-permute-start(bf16[6,32,128]{2,1,0:T(8,128)(2,1)S(1)} %get-tuple-element.36), channel_id=1, source_target_pairs={{0,32},{32,64},{64,96},{96,128},{128,160},{160,192},{192,224},{1,3... | collective-permute-start | bytes 147464 | tf_op jit(solution)/shard_map/ppermute | solution.py:271
  65.5 3.6 %collective-permute-start.9 = (bf16[6,32,128]{2,1,0:T(8,128)(2,1)S(1)}, bf16[6,32,128]{2,1,0:T(8,128)(2,1)S(1)}, u32[]{:S(2)}, u32[]{:S(2)}) collective-permute-start(bf16[6,32,128]{2,1,0:T(8,128)(2,1)S(1)} %get-tuple-element.37), channel_id=1, source_target_pairs={{32,0},{64,32},{96,64},{128,96},{160,128},{192,160},{224,192},{33,... | collective-permute-start | bytes 147464 | tf_op jit(solution)/shard_map/ppermute | solution.py:271
  69.3 1.7 %rev.6 = bf16[32,3,3,3,32]{4,3,2,1,0:T(4,128)(2,1)} reverse(bf16[32,3,3,3,32]{4,3,2,1,0:T(4,128)(2,1)S(1)} %reshape.24), dimensions={1,2,3} | reverse | bytes 110592 | tf_op jit(solution)/shard_map/rev | solution.py:300
  71.0 1.2 copy.16
  72.4 1.0 copy-done.14
  73.4 1.9 %weights.2 = f32[32,864]{1,0:T(8,128)S(1)} custom-call(bf16[6,32,1280]{2,1,0:T(8,128)(2,1)S(1)} %copy-done.14, bf16[6,32,1024]{2,1,0:T(8,128)(2,1)S(1)} %get-tuple-element.34.inner_ref.grad_ref), custom_call_target="tpu_custom_call" | custom-call | flops 424673280 | bytes 995328 | tf_op jit(solution)/shard_map/weights/pallas_call | solution.py:253
  75.4 3.0 %third.1 = (bf16[6,32,1024]{2,1,0:T(8,128)(2,1)S(1)}, bf16[6,32,128]{2,1,0:T(8,128)(2,1)}, bf16[6,32,128]{2,1,0:T(8,128)(2,1)}, bf16[6,32,256]{2,1,0:T(8,128)(2,1)S(1)}) custom-call(s32[6,6]{1,0:T(8,128)S(1)} %copy-done.11, s32[1]{0:T(128)} %bitcast.base_ref, bf16[6,32,1024]{2,1,0:T(8,128)(2,1)S(1)} %get-tuple-element.34.inner_ref.grad_ref, ...), custom_call_target="tpu_custom_call" | custom-call | flops 424673280 | bytes 2799764 | tf_op jit(solution)/shard_map/third/pallas_call | solution.py:253
  78.4 1.9 %weights.3 = f32[32,864]{1,0:T(8,128)S(1)} custom-call(bf16[6,32,1280]{2,1,0:T(8,128)(2,1)S(1)} %get-tuple-element.43.cells_ref, bf16[6,32,1024]{2,1,0:T(8,128)(2,1)S(1)} %get-tuple-element.38.inner_ref.grad_ref), custom_call_target="tpu_custom_call" | custom-call | flops 424673280 | bytes 995328 | tf_op jit(solution)/shard_map/weights/pallas_call | solution.py:253
  80.4 1.3 collective-permute-done.16
  81.9 4.2 %collective-permute-done.17 = bf16[32,864]{1,0:T(8,128)(2,1)S(1)} collective-permute-done((bf16[32,864]{1,0:T(8,128)(2,1)S(1)}, bf16[32,864]{1,0:T(8,128)(2,1)S(1)}, u32[]{:S(2)}, u32[]{:S(2)}) %collective-permute-start.17) | collective-permute-done | bytes 55328 | tf_op jit(solution)/shard_map/ppermute | solution.py:285
  86.1 5.2 %collective-permute-done.18 = bf16[32,864]{1,0:T(8,128)(2,1)S(1)} collective-permute-done((bf16[32,864]{1,0:T(8,128)(2,1)S(1)}, bf16[32,864]{1,0:T(8,128)(2,1)S(1)}, u32[]{:S(2)}, u32[]{:S(2)}) %collective-permute-start.18) | collective-permute-done | bytes 55328 | tf_op jit(solution)/shard_map/ppermute | solution.py:285
  91.4 3.1 %collective-permute-start.19 = (bf16[32,864]{1,0:T(8,128)(2,1)S(1)}, bf16[32,864]{1,0:T(8,128)(2,1)S(1)}, u32[]{:S(2)}, u32[]{:S(2)}) collective-permute-start(bf16[32,864]{1,0:T(8,128)(2,1)S(1)} %add_convert_fusion.4), channel_id=1, source_target_pairs={{0,8},{1,9},{2,10},{3,11},{4,12},{5,13},{6,14},{7,15},{8,0},{9,1},... | collective-permute-start | bytes 165896 | tf_op jit(solution)/shard_map/ppermute | solution.py:285
  94.5 5.6 %collective-permute-done.19 = bf16[32,864]{1,0:T(8,128)(2,1)S(1)} collective-permute-done((bf16[32,864]{1,0:T(8,128)(2,1)S(1)}, bf16[32,864]{1,0:T(8,128)(2,1)S(1)}, u32[]{:S(2)}, u32[]{:S(2)}) %collective-permute-start.19) | collective-permute-done | bytes 55328 | tf_op jit(solution)/shard_map/ppermute | solution.py:285
  100.2 4.2 %collective-permute-done.20 = bf16[32,864]{1,0:T(8,128)(2,1)S(1)} collective-permute-done((bf16[32,864]{1,0:T(8,128)(2,1)S(1)}, bf16[32,864]{1,0:T(8,128)(2,1)S(1)}, u32[]{:S(2)}, u32[]{:S(2)}) %collective-permute-start.20) | collective-permute-done | bytes 55328 | tf_op jit(solution)/shard_map/ppermute | solution.py:285
  104.5 5.7 %collective-permute-done.21 = bf16[32,864]{1,0:T(8,128)(2,1)S(1)} collective-permute-done((bf16[32,864]{1,0:T(8,128)(2,1)S(1)}, bf16[32,864]{1,0:T(8,128)(2,1)S(1)}, u32[]{:S(2)}, u32[]{:S(2)}) %collective-permute-start.21) | collective-permute-done | bytes 55328 | tf_op jit(solution)/shard_map/ppermute | solution.py:285
  110.2 1.6 %collective-permute-start.22 = (bf16[32,864]{1,0:T(8,128)(2,1)S(1)}, bf16[32,864]{1,0:T(8,128)(2,1)S(1)}, u32[]{:S(2)}, u32[]{:S(2)}) collective-permute-start(bf16[32,864]{1,0:T(8,128)(2,1)S(1)} %add_convert_fusion.1), channel_id=1, source_target_pairs={{0,64},{32,96},{64,0},{96,32},{128,192},{160,224},{192,128},{224,1... | collective-permute-start | bytes 165896 | tf_op jit(solution)/shard_map/ppermute | solution.py:285
  111.8 2.7 %collective-permute-done.22 = bf16[32,864]{1,0:T(8,128)(2,1)S(1)} collective-permute-done((bf16[32,864]{1,0:T(8,128)(2,1)S(1)}, bf16[32,864]{1,0:T(8,128)(2,1)S(1)}, u32[]{:S(2)}, u32[]{:S(2)}) %collective-permute-start.22) | collective-permute-done | bytes 55328 | tf_op jit(solution)/shard_map/ppermute | solution.py:285
  114.5 2.8 %collective-permute-start.23 = (bf16[32,864]{1,0:T(8,128)(2,1)S(1)}, bf16[32,864]{1,0:T(8,128)(2,1)S(1)}, u32[]{:S(2)}, u32[]{:S(2)}) collective-permute-start(bf16[32,864]{1,0:T(8,128)(2,1)S(1)} %add_convert_fusion), channel_id=1, source_target_pairs={{0,128},{32,160},{64,192},{96,224},{128,0},{160,32},{192,64},{224,... | collective-permute-start | bytes 165896 | tf_op jit(solution)/shard_map/ppermute | solution.py:285
  117.3 2.9 %collective-permute-done.23 = bf16[32,864]{1,0:T(8,128)(2,1)S(1)} collective-permute-done((bf16[32,864]{1,0:T(8,128)(2,1)S(1)}, bf16[32,864]{1,0:T(8,128)(2,1)S(1)}, u32[]{:S(2)}, u32[]{:S(2)}) %collective-permute-start.23) | collective-permute-done | bytes 55328 | tf_op jit(solution)/shard_map/ppermute | solution.py:285
  120.4 2.4 %collective-permute-start.14 = (bf16[6,32,128]{2,1,0:T(8,128)(2,1)S(1)}, bf16[6,32,128]{2,1,0:T(8,128)(2,1)S(1)}, u32[]{:S(2)}, u32[]{:S(2)}) collective-permute-start(bf16[6,32,128]{2,1,0:T(8,128)(2,1)S(1)} %slice.19), channel_id=1, source_target_pairs={{0,1},{1,2},{2,3},{3,4},{4,5},{5,6},{6,7},{7,8},{8,9},{9,10},{10,1... | collective-permute-start | bytes 147464 | tf_op jit(solution)/shard_map/ppermute | solution.py:271
  122.8 5.3 %collective-permute-start.15 = (bf16[6,32,128]{2,1,0:T(8,128)(2,1)S(1)}, bf16[6,32,128]{2,1,0:T(8,128)(2,1)S(1)}, u32[]{:S(2)}, u32[]{:S(2)}) collective-permute-start(bf16[6,32,128]{2,1,0:T(8,128)(2,1)S(1)} %slice.19), channel_id=1, source_target_pairs={{1,0},{2,1},{3,2},{4,3},{5,4},{6,5},{7,6},{8,7},{9,8},{10,9},{11,1... | collective-permute-start | bytes 147464 | tf_op jit(solution)/shard_map/ppermute | solution.py:271
  128.1 5.1 %collective-permute-start.12 = (bf16[6,32,128]{2,1,0:T(8,128)(2,1)}, bf16[6,32,128]{2,1,0:T(8,128)(2,1)S(1)}, u32[]{:S(2)}, u32[]{:S(2)}) collective-permute-start(bf16[6,32,128]{2,1,0:T(8,128)(2,1)} %get-tuple-element.40), channel_id=1, source_target_pairs={{0,32},{32,64},{64,96},{96,128},{128,160},{160,192},{192,224},{1,3... | collective-permute-start | bytes 147464 | tf_op jit(solution)/shard_map/ppermute | solution.py:271
  133.2 2.3 %collective-permute-start.13 = (bf16[6,32,128]{2,1,0:T(8,128)(2,1)}, bf16[6,32,128]{2,1,0:T(8,128)(2,1)S(1)}, u32[]{:S(2)}, u32[]{:S(2)}) collective-permute-start(bf16[6,32,128]{2,1,0:T(8,128)(2,1)} %get-tuple-element.41), channel_id=1, source_target_pairs={{32,0},{64,32},{96,64},{128,96},{160,128},{192,160},{224,192},{33,... | collective-permute-start | bytes 147464 | tf_op jit(solution)/shard_map/ppermute | solution.py:271
  135.6 0.7 rev.7
  136.8 4.9 %collective-permute-done.13.r1 = bf16[6,32,128]{2,1,0:T(8,128)(2,1)S(1)} collective-permute-done((bf16[6,32,128]{2,1,0:T(8,128)(2,1)}, bf16[6,32,128]{2,1,0:T(8,128)(2,1)S(1)}, u32[]{:S(2)}, u32[]{:S(2)}) %collective-permute-start.13) | collective-permute-done | bytes 49184 | tf_op jit(solution)/shard_map/ppermute | solution.py:271
  141.8 3.2 %last.1 = bf16[6,32,512]{2,1,0:T(8,128)(2,1)} custom-call(s32[6,6]{1,0:T(8,128)S(1)} %copy-done.11, s32[1]{0:T(128)} %bitcast.base_ref, bf16[6,32,1024]{2,1,0:T(8,128)(2,1)S(1)} %get-tuple-element.38.inner_ref.grad_ref, bf16[6,32,256]{2,1,0:T(8,128)(2,1)S(1)} %get-tuple-element.39.side_ref, bf16[6,32,128]{2,1,0:T(8,128)(2,1)S(1)} %collective-permute-done.12.r0, ...), custom_call_target="tpu_custom_call" | custom-call | flops 424673280 | bytes 1947796 | tf_op jit(solution)/shard_map/last/pallas_call | solution.py:253
  144.9 0.7 select_multiply_fusion
  (62 shorter events, 2.8 us)
Async XLA Ops:
  0.6 25.7 %copy-start = (bf16[256,1024]{1,0:T(8,128)(2,1)S(1)}, bf16[256,1024]{1,0:T(8,128)(2,1)}, u32[]{:S(2)}) copy-start(bf16[256,1024]{1,0:T(8,128)(2,1)} %constant.32.clone.put_ref) | copy-start | bytes 1572868
  0.6 1.1 copy-start.1
  1.7 0.8 copy-start.5
  2.6 0.9 copy-start.9
  3.5 0.7 copy-start.12
  4.8 21.5 %copy-start.8 = (bf16[32,864]{1,0:T(8,128)(2,1)S(1)}, bf16[32,864]{1,0:T(8,128)(2,1)}, u32[]{:S(2)}) copy-start(bf16[32,864]{1,0:T(8,128)(2,1)} %weight_ref.2) | copy-start | bytes 165892
  4.8 16.7 %collective-permute-start.2 = (bf16[6,32,128]{2,1,0:T(8,128)(2,1)S(1)}, bf16[6,32,128]{2,1,0:T(8,128)(2,1)S(1)}, u32[]{:S(2)}, u32[]{:S(2)}) collective-permute-start(bf16[6,32,128]{2,1,0:T(8,128)(2,1)S(1)} %slice.16), channel_id=1, source_target_pairs={{0,1},{1,2},{2,3},{3,4},{4,5},{5,6},{6,7},{7,8},{8,9},{9,10},{10,1... | collective-permute-start | bytes 147464 | tf_op jit(solution)/shard_map/ppermute | solution.py:271
  6.7 14.8 %collective-permute-start.3 = (bf16[6,32,128]{2,1,0:T(8,128)(2,1)S(1)}, bf16[6,32,128]{2,1,0:T(8,128)(2,1)S(1)}, u32[]{:S(2)}, u32[]{:S(2)}) collective-permute-start(bf16[6,32,128]{2,1,0:T(8,128)(2,1)S(1)} %slice.16), channel_id=1, source_target_pairs={{1,0},{2,1},{3,2},{4,3},{5,4},{6,5},{7,6},{8,7},{9,8},{10,9},{11,1... | collective-permute-start | bytes 147464 | tf_op jit(solution)/shard_map/ppermute | solution.py:271
  14.1 8.0 %collective-permute-start = (bf16[6,32,128]{2,1,0:T(8,128)(2,1)S(1)}, bf16[6,32,128]{2,1,0:T(8,128)(2,1)S(1)}, u32[]{:S(2)}, u32[]{:S(2)}) collective-permute-start(bf16[6,32,128]{2,1,0:T(8,128)(2,1)S(1)} %get-tuple-element.26), channel_id=1, source_target_pairs={{0,32},{32,64},{64,96},{96,128},{128,160},{160,192},{192,224},{1,3... | collective-permute-start | bytes 147464 | tf_op jit(solution)/shard_map/ppermute | solution.py:271
  17.9 8.4 %collective-permute-start.1 = (bf16[6,32,128]{2,1,0:T(8,128)(2,1)S(1)}, bf16[6,32,128]{2,1,0:T(8,128)(2,1)S(1)}, u32[]{:S(2)}, u32[]{:S(2)}) collective-permute-start(bf16[6,32,128]{2,1,0:T(8,128)(2,1)S(1)} %get-tuple-element.27), channel_id=1, source_target_pairs={{32,0},{64,32},{96,64},{128,96},{160,128},{192,160},{224,192},{33,... | collective-permute-start | bytes 147464 | tf_op jit(solution)/shard_map/ppermute | solution.py:271
  21.5 4.8 %copy-start.11 = (s32[6,6]{1,0:T(8,128)S(1)}, s32[6,6]{1,0:T(8,128)}, u32[]{:S(2)}) copy-start(s32[6,6]{1,0:T(8,128)} %neighbours_ref.7) | copy-start | bytes 436
  26.3 1.0 copy-start.2
  27.3 17.9 %copy-start.6 = (bf16[128,256]{1,0:T(8,128)(2,1)S(1)}, bf16[128,256]{1,0:T(8,128)(2,1)}, u32[]{:S(2)}) copy-start(bf16[128,256]{1,0:T(8,128)(2,1)} %constant.29.clone.spread_ref) | copy-start | bytes 196612
  27.3 17.9 %copy-start.10 = (bf16[6,32,512]{2,1,0:T(8,128)(2,1)S(1)}, bf16[6,32,512]{2,1,0:T(8,128)(2,1)}, u32[]{:S(2)}) copy-start(bf16[6,32,512]{2,1,0:T(8,128)(2,1)} %cotangent_ref.1) | copy-start | bytes 589828
  29.9 20.0 %copy-start.3 = (bf16[1024,256]{1,0:T(8,128)(2,1)S(1)}, bf16[1024,256]{1,0:T(8,128)(2,1)}, u32[]{:S(2)}) copy-start(bf16[1024,256]{1,0:T(8,128)(2,1)} %constant.31.clone.pick_ref) | copy-start | bytes 1572868
  29.9 15.6 %collective-permute-start.6 = (bf16[6,32,128]{2,1,0:T(8,128)(2,1)S(1)}, bf16[6,32,128]{2,1,0:T(8,128)(2,1)S(1)}, u32[]{:S(2)}, u32[]{:S(2)}) collective-permute-start(bf16[6,32,128]{2,1,0:T(8,128)(2,1)S(1)} %slice.17), channel_id=1, source_target_pairs={{0,1},{1,2},{2,3},{3,4},{4,5},{5,6},{6,7},{7,8},{8,9},{9,10},{10,1... | collective-permute-start | bytes 147464 | tf_op jit(solution)/shard_map/ppermute | solution.py:271
  32.0 13.6 %collective-permute-start.7 = (bf16[6,32,128]{2,1,0:T(8,128)(2,1)S(1)}, bf16[6,32,128]{2,1,0:T(8,128)(2,1)S(1)}, u32[]{:S(2)}, u32[]{:S(2)}) collective-permute-start(bf16[6,32,128]{2,1,0:T(8,128)(2,1)S(1)} %slice.17), channel_id=1, source_target_pairs={{1,0},{2,1},{3,2},{4,3},{5,4},{6,5},{7,6},{8,7},{9,8},{10,9},{11,1... | collective-permute-start | bytes 147464 | tf_op jit(solution)/shard_map/ppermute | solution.py:271
  37.7 8.0 %collective-permute-start.4 = (bf16[6,32,128]{2,1,0:T(8,128)(2,1)S(1)}, bf16[6,32,128]{2,1,0:T(8,128)(2,1)S(1)}, u32[]{:S(2)}, u32[]{:S(2)}) collective-permute-start(bf16[6,32,128]{2,1,0:T(8,128)(2,1)S(1)} %get-tuple-element.31), channel_id=1, source_target_pairs={{0,32},{32,64},{64,96},{96,128},{128,160},{160,192},{192,224},{1,3... | collective-permute-start | bytes 147464 | tf_op jit(solution)/shard_map/ppermute | solution.py:271
  41.3 8.5 %copy-start.4 = (bf16[256,128]{1,0:T(8,128)(2,1)S(1)}, bf16[256,128]{1,0:T(8,128)(2,1)}, u32[]{:S(2)}) copy-start(bf16[256,128]{1,0:T(8,128)(2,1)} %constant.30.clone.gather_ref) | copy-start | bytes 196612
  41.3 8.5 %copy-start.7 = (bf16[32,864]{1,0:T(8,128)(2,1)S(1)}, bf16[32,864]{1,0:T(8,128)(2,1)}, u32[]{:S(2)}) copy-start(bf16[32,864]{1,0:T(8,128)(2,1)} %weight_ref.3) | copy-start | bytes 165892
  41.4 8.5 %collective-permute-start.5 = (bf16[6,32,128]{2,1,0:T(8,128)(2,1)S(1)}, bf16[6,32,128]{2,1,0:T(8,128)(2,1)S(1)}, u32[]{:S(2)}, u32[]{:S(2)}) collective-permute-start(bf16[6,32,128]{2,1,0:T(8,128)(2,1)S(1)} %get-tuple-element.32), channel_id=1, source_target_pairs={{32,0},{64,32},{96,64},{128,96},{160,128},{192,160},{224,192},{33,... | collective-permute-start | bytes 147464 | tf_op jit(solution)/shard_map/ppermute | solution.py:271
  53.3 0.8 copy-start.13
  54.0 21.3 %collective-permute-start.10 = (bf16[6,32,128]{2,1,0:T(8,128)(2,1)S(1)}, bf16[6,32,128]{2,1,0:T(8,128)(2,1)S(1)}, u32[]{:S(2)}, u32[]{:S(2)}) collective-permute-start(bf16[6,32,128]{2,1,0:T(8,128)(2,1)S(1)} %slice.18), channel_id=1, source_target_pairs={{0,1},{1,2},{2,3},{3,4},{4,5},{5,6},{6,7},{7,8},{8,9},{9,10},{10,1... | collective-permute-start | bytes 147464 | tf_op jit(solution)/shard_map/ppermute | solution.py:271
  56.0 19.4 %collective-permute-start.11 = (bf16[6,32,128]{2,1,0:T(8,128)(2,1)S(1)}, bf16[6,32,128]{2,1,0:T(8,128)(2,1)S(1)}, u32[]{:S(2)}, u32[]{:S(2)}) collective-permute-start(bf16[6,32,128]{2,1,0:T(8,128)(2,1)S(1)} %slice.18), channel_id=1, source_target_pairs={{1,0},{2,1},{3,2},{4,3},{5,4},{6,5},{7,6},{8,7},{9,8},{10,9},{11,1... | collective-permute-start | bytes 147464 | tf_op jit(solution)/shard_map/ppermute | solution.py:271
  61.7 13.6 %collective-permute-start.8 = (bf16[6,32,128]{2,1,0:T(8,128)(2,1)S(1)}, bf16[6,32,128]{2,1,0:T(8,128)(2,1)S(1)}, u32[]{:S(2)}, u32[]{:S(2)}) collective-permute-start(bf16[6,32,128]{2,1,0:T(8,128)(2,1)S(1)} %get-tuple-element.36), channel_id=1, source_target_pairs={{0,32},{32,64},{64,96},{96,128},{128,160},{160,192},{192,224},{1,3... | collective-permute-start | bytes 147464 | tf_op jit(solution)/shard_map/ppermute | solution.py:271
  65.5 9.8 %collective-permute-start.9 = (bf16[6,32,128]{2,1,0:T(8,128)(2,1)S(1)}, bf16[6,32,128]{2,1,0:T(8,128)(2,1)S(1)}, u32[]{:S(2)}, u32[]{:S(2)}) collective-permute-start(bf16[6,32,128]{2,1,0:T(8,128)(2,1)S(1)} %get-tuple-element.37), channel_id=1, source_target_pairs={{32,0},{64,32},{96,64},{128,96},{160,128},{192,160},{224,192},{33,... | collective-permute-start | bytes 147464 | tf_op jit(solution)/shard_map/ppermute | solution.py:271
  72.4 1.0 copy-start.14
  80.3 1.4 collective-permute-start.16
  81.8 4.3 %collective-permute-start.17 = (bf16[32,864]{1,0:T(8,128)(2,1)S(1)}, bf16[32,864]{1,0:T(8,128)(2,1)S(1)}, u32[]{:S(2)}, u32[]{:S(2)}) collective-permute-start(bf16[32,864]{1,0:T(8,128)(2,1)S(1)} %add_convert_fusion.6), channel_id=1, source_target_pairs={{0,2},{1,3},{2,0},{3,1},{4,6},{5,7},{6,4},{7,5},{8,10},{9,11},{10,... | collective-permute-start | bytes 165896 | tf_op jit(solution)/shard_map/ppermute | solution.py:285
  86.0 5.3 %collective-permute-start.18 = (bf16[32,864]{1,0:T(8,128)(2,1)S(1)}, bf16[32,864]{1,0:T(8,128)(2,1)S(1)}, u32[]{:S(2)}, u32[]{:S(2)}) collective-permute-start(bf16[32,864]{1,0:T(8,128)(2,1)S(1)} %add_convert_fusion.5), channel_id=1, source_target_pairs={{0,4},{1,5},{2,6},{3,7},{4,0},{5,1},{6,2},{7,3},{8,12},{9,13},{10,... | collective-permute-start | bytes 165896 | tf_op jit(solution)/shard_map/ppermute | solution.py:285
  91.4 8.8 %collective-permute-start.19 = (bf16[32,864]{1,0:T(8,128)(2,1)S(1)}, bf16[32,864]{1,0:T(8,128)(2,1)S(1)}, u32[]{:S(2)}, u32[]{:S(2)}) collective-permute-start(bf16[32,864]{1,0:T(8,128)(2,1)S(1)} %add_convert_fusion.4), channel_id=1, source_target_pairs={{0,8},{1,9},{2,10},{3,11},{4,12},{5,13},{6,14},{7,15},{8,0},{9,1},... | collective-permute-start | bytes 165896 | tf_op jit(solution)/shard_map/ppermute | solution.py:285
  100.1 4.3 %collective-permute-start.20 = (bf16[32,864]{1,0:T(8,128)(2,1)S(1)}, bf16[32,864]{1,0:T(8,128)(2,1)S(1)}, u32[]{:S(2)}, u32[]{:S(2)}) collective-permute-start(bf16[32,864]{1,0:T(8,128)(2,1)S(1)} %add_convert_fusion.3), channel_id=1, source_target_pairs={{0,16},{1,17},{2,18},{3,19},{4,20},{5,21},{6,22},{7,23},{8,24},{9,... | collective-permute-start | bytes 165896 | tf_op jit(solution)/shard_map/ppermute | solution.py:285
  104.4 5.8 %collective-permute-start.21 = (bf16[32,864]{1,0:T(8,128)(2,1)S(1)}, bf16[32,864]{1,0:T(8,128)(2,1)S(1)}, u32[]{:S(2)}, u32[]{:S(2)}) collective-permute-start(bf16[32,864]{1,0:T(8,128)(2,1)S(1)} %add_convert_fusion.2), channel_id=1, source_target_pairs={{0,32},{32,0},{64,96},{96,64},{128,160},{160,128},{192,224},{224,1... | collective-permute-start | bytes 165896 | tf_op jit(solution)/shard_map/ppermute | solution.py:285
  110.2 4.3 %collective-permute-start.22 = (bf16[32,864]{1,0:T(8,128)(2,1)S(1)}, bf16[32,864]{1,0:T(8,128)(2,1)S(1)}, u32[]{:S(2)}, u32[]{:S(2)}) collective-permute-start(bf16[32,864]{1,0:T(8,128)(2,1)S(1)} %add_convert_fusion.1), channel_id=1, source_target_pairs={{0,64},{32,96},{64,0},{96,32},{128,192},{160,224},{192,128},{224,1... | collective-permute-start | bytes 165896 | tf_op jit(solution)/shard_map/ppermute | solution.py:285
  114.5 5.8 %collective-permute-start.23 = (bf16[32,864]{1,0:T(8,128)(2,1)S(1)}, bf16[32,864]{1,0:T(8,128)(2,1)S(1)}, u32[]{:S(2)}, u32[]{:S(2)}) collective-permute-start(bf16[32,864]{1,0:T(8,128)(2,1)S(1)} %add_convert_fusion), channel_id=1, source_target_pairs={{0,128},{32,160},{64,192},{96,224},{128,0},{160,32},{192,64},{224,... | collective-permute-start | bytes 165896 | tf_op jit(solution)/shard_map/ppermute | solution.py:285
  120.3 24.7 %collective-permute-start.24 = (f32[32,864]{1,0:T(8,128)S(1)}, f32[32,864]{1,0:T(8,128)S(1)}, u32[]{:S(2)}, u32[]{:S(2)}) collective-permute-start(f32[32,864]{1,0:T(8,128)S(1)} %convert_add_fusion), channel_id=1, source_target_pairs={{0,1},{1,0},{2,3},{3,2},{4,5},{5,4},{6,7},{7,6},{8,9},{9,8},{10,11... | collective-permute-start | bytes 331784 | tf_op jit(solution)/shard_map/ppermute | solution.py:285
  120.4 16.4 %collective-permute-start.14 = (bf16[6,32,128]{2,1,0:T(8,128)(2,1)S(1)}, bf16[6,32,128]{2,1,0:T(8,128)(2,1)S(1)}, u32[]{:S(2)}, u32[]{:S(2)}) collective-permute-start(bf16[6,32,128]{2,1,0:T(8,128)(2,1)S(1)} %slice.19), channel_id=1, source_target_pairs={{0,1},{1,2},{2,3},{3,4},{4,5},{5,6},{6,7},{7,8},{8,9},{9,10},{10,1... | collective-permute-start | bytes 147464 | tf_op jit(solution)/shard_map/ppermute | solution.py:271
  122.8 14.0 %collective-permute-start.15 = (bf16[6,32,128]{2,1,0:T(8,128)(2,1)S(1)}, bf16[6,32,128]{2,1,0:T(8,128)(2,1)S(1)}, u32[]{:S(2)}, u32[]{:S(2)}) collective-permute-start(bf16[6,32,128]{2,1,0:T(8,128)(2,1)S(1)} %slice.19), channel_id=1, source_target_pairs={{1,0},{2,1},{3,2},{4,3},{5,4},{6,5},{7,6},{8,7},{9,8},{10,9},{11,1... | collective-permute-start | bytes 147464 | tf_op jit(solution)/shard_map/ppermute | solution.py:271
  128.1 8.7 %collective-permute-start.12 = (bf16[6,32,128]{2,1,0:T(8,128)(2,1)}, bf16[6,32,128]{2,1,0:T(8,128)(2,1)S(1)}, u32[]{:S(2)}, u32[]{:S(2)}) collective-permute-start(bf16[6,32,128]{2,1,0:T(8,128)(2,1)} %get-tuple-element.40), channel_id=1, source_target_pairs={{0,32},{32,64},{64,96},{96,128},{128,160},{160,192},{192,224},{1,3... | collective-permute-start | bytes 147464 | tf_op jit(solution)/shard_map/ppermute | solution.py:271
  133.2 8.6 %collective-permute-start.13 = (bf16[6,32,128]{2,1,0:T(8,128)(2,1)}, bf16[6,32,128]{2,1,0:T(8,128)(2,1)S(1)}, u32[]{:S(2)}, u32[]{:S(2)}) collective-permute-start(bf16[6,32,128]{2,1,0:T(8,128)(2,1)} %get-tuple-element.41), channel_id=1, source_target_pairs={{32,0},{64,32},{96,64},{128,96},{160,128},{192,160},{224,192},{33,... | collective-permute-start | bytes 147464 | tf_op jit(solution)/shard_map/ppermute | solution.py:271

commit v2 on v1

v2 whole, which is shorter than its diff:
```python
import functools
import math

import jax
import jax.numpy as jnp
import numpy as np
from jax import lax
from jax.experimental import pallas as pl
from jax.experimental.pallas import tpu as pltpu
from jax.sharding import PartitionSpec as P

EDGE = 8
LANES = 128
PITCH = 10
SLOTS = 6
CHANS = 32
INNER = EDGE * LANES
WHOLE = (EDGE + 2) * LANES
BF16 = jnp.bfloat16
F32 = jnp.float32
VMEM_LIMIT = 16 * 1024 * 1024


def lane_of(row, col):
    return (row + 1) * PITCH + col + 1


def spread_matrix():
    out = np.zeros((2 * EDGE * EDGE, 2 * LANES), np.float32)
    for half in range(2):
        for row in range(EDGE):
            for col in range(EDGE):
                out[half * 64 + row * EDGE + col, half * LANES + lane_of(row, col)] = 1
    return out


def face_matrices():
    pick = np.zeros((INNER, 256), np.float32)
    put = np.zeros((256, INNER), np.float32)
    for plane in range(EDGE):
        base = plane * LANES
        for at in range(EDGE):
            col = plane * EDGE + at
            pick[base + lane_of(EDGE - 1, at), col] = 1
            pick[base + lane_of(0, at), 64 + col] = 1
            pick[base + lane_of(at, EDGE - 1), 128 + col] = 1
            pick[base + lane_of(at, 0), 192 + col] = 1
            put[col, base + lane_of(-1, at)] = 1
            put[64 + col, base + lane_of(EDGE, at)] = 1
            put[128 + col, base + lane_of(at, -1)] = 1
            put[192 + col, base + lane_of(at, EDGE)] = 1
    return pick, put


SPREAD = spread_matrix()
PICK, PUT = face_matrices()


def dot(lhs, rhs):
    return jnp.dot(lhs, rhs, preferred_element_type=F32)


def spread(field, matrix):
    return [dot(field[:, at * LANES : (at + 1) * LANES], matrix) for at in range(4)]


def emit_faces(place_ref, inner_ref, pick_ref, even_ref, odd_ref, side_ref):
    raised = place_ref[1] == 1
    low = inner_ref[:, :, :LANES]
    high = inner_ref[:, :, INNER - LANES :]
    even_ref[...] = jnp.where(raised, low, high)
    odd_ref[...] = jnp.where(raised, high, low)
    flat = inner_ref[...].reshape(SLOTS * CHANS, INNER)
    side_ref[...] = dot(flat, pick_ref[...]).astype(BF16).reshape(SLOTS, CHANS, 256)


def build_cells(cells_ref, sheet_ref, inner_ref, side_ref, remote_refs, put_ref, neighbours_ref, place_ref):
    base = place_ref[0]
    lane = lax.broadcasted_iota(jnp.int32, (1, LANES), 1)
    lower = (lane < 64).astype(F32).astype(BF16)
    upper = (lane >= 64).astype(F32).astype(BF16)
    zero = jnp.zeros((CHANS, LANES), BF16)

    x_even_ref, x_odd_ref, y_even_ref, y_odd_ref = remote_refs
    pairs = ((x_odd_ref, x_even_ref), (x_even_ref, x_odd_ref), (y_odd_ref, y_even_ref), (y_even_ref, y_odd_ref))

    def picked(slot, face, local):
        ident = neighbours_ref[slot, face]
        place = lax.rem(jnp.maximum(ident, 0), SLOTS)
        value = local(place)
        if face < 4:
            here = (ident >= base) & (ident < base + SLOTS)
            settled, raised = pairs[face]
            distant = jnp.where(place_ref[1 + face // 2] == 1, raised[place], settled[place])
            value = jnp.where(here, value, distant)
        return jnp.where(ident >= 0, value, zero)

    for slot in range(SLOTS):
        cells_ref[slot, :, :LANES] = picked(
            slot, 0, lambda at: inner_ref[at, :, INNER - LANES :]
        )
        cells_ref[slot, :, WHOLE - LANES :] = picked(
            slot, 1, lambda at: inner_ref[at, :, :LANES]
        )
        sides = lambda at: side_ref[at, :, :LANES]
        ends = lambda at: side_ref[at, :, LANES:]
        rows = pl.ds(slot * CHANS, CHANS)
        sheet_ref[rows, :LANES] = (
            picked(slot, 2, sides) * lower + picked(slot, 3, sides) * upper
        )
        sheet_ref[rows, LANES:] = (
            picked(slot, 4, ends) * lower + picked(slot, 5, ends) * upper
        )
    halo = dot(sheet_ref[...], put_ref[...]).astype(BF16).reshape(SLOTS, CHANS, INNER)
    cells_ref[:, :, LANES : LANES + INNER] = inner_ref[...] + halo


def shift_planes(columns_ref, cells_ref, slot):
    for plane in range(EDGE + 2):
        span = slice(plane * LANES, (plane + 1) * LANES)
        tile = cells_ref[slot, :, span]
        for tap in range(9):
            shift = (tap // 3 - 1) * PITCH + tap % 3 - 1
            moved = tile if shift == 0 else pltpu.roll(tile, (-shift) % LANES, 1)
            columns_ref[tap * CHANS : (tap + 1) * CHANS, span] = moved


def stacked(weight):
    return jnp.concatenate([weight[:, at * 288 : (at + 1) * 288] for at in range(3)], axis=0)


def convolve(columns_ref, weight):
    raw = dot(weight, columns_ref[...])
    return (
        raw[:CHANS, :INNER]
        + raw[CHANS : 2 * CHANS, LANES : LANES + INNER]
        + raw[2 * CHANS :, 2 * LANES :]
    )


def enter_kernel(place_ref, features_hbm, occupancy_hbm, spread_hbm, pick_hbm, inner_ref, mask_ref, even_ref, odd_ref, side_ref,
                 features_ref, occupancy_ref, spread_ref, pick_ref, sems):
    loads = [
        pltpu.make_async_copy(source, target, sems.at[at])
        for at, (source, target) in enumerate(
            ((occupancy_hbm, occupancy_ref), (spread_hbm, spread_ref), (features_hbm, features_ref), (pick_hbm, pick_ref))
        )
    ]
    for load in loads:
        load.start()
    for load in loads[:3]:
        load.wait()
    mask = occupancy_ref[...].astype(F32).astype(BF16)
    matrix = spread_ref[...]
    for at, part in enumerate(spread(mask, matrix)):
        mask_ref[:, at * 256 : (at + 1) * 256] = part
    masked = jnp.concatenate(
        [features_ref[slot] * mask[slot : slot + 1, :] for slot in range(SLOTS)], axis=0
    )
    for at, part in enumerate(spread(masked, matrix)):
        inner_ref[:, :, at * 256 : (at + 1) * 256] = part.astype(BF16).reshape(SLOTS, CHANS, 256)
    loads[3].wait()
    emit_faces(place_ref, inner_ref, pick_ref, even_ref, odd_ref, side_ref)


def turned(weight):
    taps = weight.astype(F32).T.astype(BF16)
    rows = []
    for first in range(3):
        blocks = []
        for rest in range(9):
            tap = 26 - first * 9 - rest
            blocks.append(taps[tap * CHANS : (tap + 1) * CHANS])
        rows.append(jnp.concatenate(blocks, axis=1))
    return jnp.concatenate(rows, axis=0)


def turn_kernel(first_ref, second_ref, back_first_ref, back_second_ref):
    back_first_ref[...] = turned(first_ref[...])
    back_second_ref[...] = turned(second_ref[...])


def spread_kernel(cotangent_ref, mask_ref, spread_ref, out_ref):
    flat = cotangent_ref[...].reshape(SLOTS * CHANS, 512)
    for at, part in enumerate(spread(flat, spread_ref[...])):
        span = slice(at * 256, (at + 1) * 256)
        for slot in range(SLOTS):
            out_ref[slot, :, span] = (
                part[slot * CHANS : (slot + 1) * CHANS] * mask_ref[slot : slot + 1, span]
            ).astype(BF16)


def first_kernel(neighbours_ref, place_ref, inner_ref, side_ref, r0, r1, r2, r3, put_ref, pick_ref, weight_ref, mask_ref,
                 cells_ref, hidden_ref, even_ref, odd_ref, hidden_side_ref, sheet_ref, columns_ref):
    build_cells(cells_ref, sheet_ref, inner_ref, side_ref, (r0, r1, r2, r3), put_ref, neighbours_ref, place_ref)
    weight = stacked(weight_ref[...])
    for slot in range(SLOTS):
        buffer = columns_ref.at[slot % 2]
        shift_planes(buffer, cells_ref, slot)
        pre = convolve(buffer, weight)
        hidden_ref[slot] = (jnp.maximum(pre, 0.0) * mask_ref[slot : slot + 1, :]).astype(BF16)
    emit_faces(place_ref, hidden_ref, pick_ref, even_ref, odd_ref, hidden_side_ref)


def pack_rows(inner, gather):
    return [dot(inner[:, at * 256 : (at + 1) * 256], gather) for at in range(4)]


def second_kernel(neighbours_ref, place_ref, inner_ref, side_ref, r0, r1, r2, r3, put_ref, pick_ref, gather_ref, weight_ref,
                  mask_ref, skip_ref, cotangent_ref,
                  cells_ref, result_ref, grad_ref, even_ref, odd_ref, grad_side_ref, sheet_ref, columns_ref, wide_ref):
    build_cells(cells_ref, sheet_ref, inner_ref, side_ref, (r0, r1, r2, r3), put_ref, neighbours_ref, place_ref)
    weight = stacked(weight_ref[...])
    for slot in range(SLOTS):
        buffer = columns_ref.at[slot % 2]
        shift_planes(buffer, cells_ref, slot)
        pre = convolve(buffer, weight) + skip_ref[slot].astype(F32)
        wide_ref[slot] = (jnp.maximum(pre, 0.0) * mask_ref[slot : slot + 1, :]).astype(BF16)
        grad_ref[slot] = jnp.where(pre > 0.0, cotangent_ref[slot].astype(F32), 0.0).astype(BF16)
    emit_faces(place_ref, grad_ref, pick_ref, even_ref, odd_ref, grad_side_ref)
    flat = wide_ref[...].reshape(SLOTS * CHANS, INNER)
    for at, part in enumerate(pack_rows(flat, gather_ref[...])):
        result_ref[:, :, at * LANES : (at + 1) * LANES] = part.astype(BF16).reshape(SLOTS, CHANS, LANES)


def third_kernel(neighbours_ref, place_ref, inner_ref, side_ref, r0, r1, r2, r3, put_ref, pick_ref, weight_ref, mask_ref,
                 hidden_ref, grad_ref, even_ref, odd_ref, grad_side_ref, cells_ref, sheet_ref, columns_ref):
    build_cells(cells_ref, sheet_ref, inner_ref, side_ref, (r0, r1, r2, r3), put_ref, neighbours_ref, place_ref)
    weight = weight_ref[...]
    for slot in range(SLOTS):
        buffer = columns_ref.at[slot % 2]
        shift_planes(buffer, cells_ref, slot)
        grad = convolve(buffer, weight) * mask_ref[slot : slot + 1, :]
        grad_ref[slot] = jnp.where(hidden_ref[slot].astype(F32) > 0.0, grad, 0.0).astype(BF16)
    emit_faces(place_ref, grad_ref, pick_ref, even_ref, odd_ref, grad_side_ref)


def last_kernel(neighbours_ref, place_ref, inner_ref, side_ref, r0, r1, r2, r3, put_ref, gather_ref, weight_ref, mask_ref,
                grad_ref, out_ref, cells_ref, sheet_ref, columns_ref, wide_ref):
    build_cells(cells_ref, sheet_ref, inner_ref, side_ref, (r0, r1, r2, r3), put_ref, neighbours_ref, place_ref)
    weight = weight_ref[...]
    for slot in range(SLOTS):
        buffer = columns_ref.at[slot % 2]
        shift_planes(buffer, cells_ref, slot)
        grad = convolve(buffer, weight) + grad_ref[slot].astype(F32)
        wide_ref[slot] = (grad * mask_ref[slot : slot + 1, :]).astype(BF16)
    flat = wide_ref[...].reshape(SLOTS * CHANS, INNER)
    for at, part in enumerate(pack_rows(flat, gather_ref[...])):
        out_ref[:, :, at * LANES : (at + 1) * LANES] = part.astype(BF16).reshape(SLOTS, CHANS, LANES)


def weight_kernel(cells_ref, grad_ref, out_ref, columns_ref, grads_ref):
    grads_ref[...] = jnp.zeros_like(grads_ref)
    total = jnp.zeros((9 * CHANS, 3 * CHANS), F32)
    for slot in range(SLOTS):
        buffer = columns_ref.at[slot % 2]
        shift_planes(buffer, cells_ref, slot)
        spot = grads_ref.at[slot % 2]
        for at in range(3):
            spot[at * CHANS : (at + 1) * CHANS, at * LANES : at * LANES + INNER] = grad_ref[slot]
        total = total + lax.dot_general(
            buffer[...], spot[...], (((1,), (1,)), ((), ())), preferred_element_type=F32
        )
    turned = total.T
    for at in range(3):
        out_ref[:, at * 288 : (at + 1) * 288] = turned[at * CHANS : (at + 1) * CHANS]


def shape(dims, dtype=BF16):
    return jax.ShapeDtypeStruct(dims, dtype)


FIELD = (SLOTS, CHANS, 512)
INSIDE = (SLOTS, CHANS, INNER)
CELLS = (SLOTS, CHANS, WHOLE)
FACE = (SLOTS, CHANS, LANES)
SIDE = (SLOTS, CHANS, 2 * LANES)
FACES = [shape(FACE), shape(FACE), shape(SIDE)]
SCRATCH = [pltpu.VMEM((SLOTS * CHANS, 256), BF16), pltpu.VMEM((2, 9 * CHANS, WHOLE), BF16)]


def call(kernel, outs, scratch, scalars, flops, name, space=pltpu.VMEM):
    def run(*args):
        specs = [
            pl.BlockSpec(memory_space=pltpu.SMEM if at < scalars else space)
            for at in range(len(args))
        ]
        moved = sum(a.size * a.dtype.itemsize for a in args)
        moved += sum(math.prod(o.shape) * o.dtype.itemsize for o in outs)
        result = pl.pallas_call(
            kernel,
            out_shape=outs,
            in_specs=specs,
            out_specs=[pl.BlockSpec(memory_space=pltpu.VMEM)] * len(outs),
            scratch_shapes=scratch,
            compiler_params=pltpu.CompilerParams(vmem_limit_bytes=VMEM_LIMIT),
            cost_estimate=pl.CostEstimate(flops=flops, bytes_accessed=moved, transcendentals=0),
            name=name,
        )(*args)
        return result

    return run


def swapped(value, axis, bit):
    count = lax.axis_size(axis)
    return lax.ppermute(value, axis, [(at, at ^ bit) for at in range(count)])


def paired(value, axis, odd):
    count = lax.axis_size(axis)
    if not odd:
        return swapped(value, axis, 1)
    return lax.ppermute(
        value, axis, [(at, (at + 1 if at % 2 else at - 1) % count) for at in range(count)]
    )


HOPS = (("tx", 0), ("tx", 1), ("ty", 0), ("ty", 1))


def exchanged(even, odd, side):
    sent = (even, odd, side[:, :, :LANES], side[:, :, :LANES])
    return [paired(value, axis, turn) for value, (axis, turn) in zip(sent, HOPS)]


CONV_FLOPS = 2 * 96 * 288 * WHOLE * SLOTS


def body(features, occupancy, neighbours, w_first, w_second, cotangent):
    row, col = lax.axis_index("tx"), lax.axis_index("ty")
    base = (row * lax.axis_size("ty") + col) * SLOTS
    place = jnp.stack([base, row % 2, col % 2]).astype(jnp.int32)
    widen = jnp.asarray(SPREAD, BF16)
    narrow = jnp.asarray(SPREAD.T, BF16)
    pick = jnp.asarray(PICK, BF16)
    put = jnp.asarray(PUT, BF16)
    enter_scratch = [
        pltpu.VMEM(FIELD, BF16),
        pltpu.VMEM((SLOTS, 512), jnp.int32),
        pltpu.VMEM(SPREAD.shape, BF16),
        pltpu.VMEM(PICK.shape, BF16),
        pltpu.SemaphoreType.DMA((4,)),
    ]
    x_inner, mask, even, odd, side = call(
        enter_kernel, [shape(INSIDE), shape((SLOTS, INNER), F32)] + FACES, enter_scratch, 1, 2 * 192 * 512 * 1024, "enter",
        pltpu.HBM,
    )(place, features, occupancy, widen, pick)
    remote = exchanged(even, odd, side)
    (cot_inner,) = call(spread_kernel, [shape(INSIDE)], [], 0, 2 * 192 * 512 * 256, "spread")(
        cotangent, mask, widen
    )
    back_first, back_second = call(
        turn_kernel, [shape((3 * CHANS, 9 * CHANS))] * 2, [], 0, 1 << 20, "turn"
    )(w_first, w_second)
    x_cells, hidden, even, odd, hidden_side = call(
        first_kernel, [shape(CELLS), shape(INSIDE)] + FACES, SCRATCH, 2, CONV_FLOPS, "first"
    )(neighbours, place, x_inner, side, *remote, put, pick, w_first, mask)
    remote = exchanged(even, odd, hidden_side)
    hidden_cells, result, grad_two, even, odd, grad_side = call(
        second_kernel,
        [shape(CELLS), shape(FIELD), shape(INSIDE)] + FACES,
        SCRATCH + [pltpu.VMEM(INSIDE, BF16)],
        2,
        CONV_FLOPS,
        "second",
    )(neighbours, place, hidden, hidden_side, *remote, put, pick, narrow, w_second, mask, x_inner, cot_inner)
    remote = exchanged(even, odd, grad_side)
    weight_scratch = [SCRATCH[1], pltpu.VMEM((2, 3 * CHANS, WHOLE), BF16)]
    weight_call = call(weight_kernel, [shape((CHANS, 27 * CHANS), F32)], weight_scratch, 0, CONV_FLOPS, "weights")
    (term_second,) = weight_call(hidden_cells, grad_two)
    grad_one, even, odd, one_side = call(
        third_kernel, [shape(INSIDE)] + FACES, [pltpu.VMEM(CELLS, BF16)] + SCRATCH, 2, CONV_FLOPS, "third"
    )(neighbours, place, grad_two, grad_side, *remote, put, pick, back_second, mask, hidden)
    (term_first,) = weight_call(x_cells, grad_one)
    sent = (even, odd, one_side[:, :, :LANES], one_side[:, :, :LANES])
    late = col % 2 == 1
    total = jnp.where(late, term_second, term_first) + swapped(
        jnp.where(late, term_first, term_second), "ty", 1
    )
    remote = []
    for step, (axis, bit) in enumerate(
        (("ty", 2), ("ty", 4), ("ty", 8), ("ty", 16), ("tx", 1), ("tx", 2), ("tx", 4))
    ):
        mine = total.astype(BF16)
        if 1 <= step <= 4:
            mine, remote[-1] = lax.optimization_barrier((mine, remote[-1]))
        if step < 4:
            mine, value = lax.optimization_barrier((mine, sent[step]))
            remote.append(paired(value, *HOPS[step]))
        if step == 5:
            mine, remote = lax.optimization_barrier((mine, remote))
            (grad_features,) = call(
                last_kernel,
                [shape(FIELD)],
                [pltpu.VMEM(CELLS, BF16)] + SCRATCH + [pltpu.VMEM(INSIDE, BF16)],
                2,
                CONV_FLOPS,
                "last",
            )(neighbours, place, grad_one, one_side, *remote, put, narrow, back_first, mask, grad_two)
        total = mine.astype(F32) + swapped(mine, axis, bit).astype(F32)
        if step == 5:
            total, grad_features = lax.optimization_barrier((total, grad_features))
    scale = 1.0 / math.sqrt(SLOTS * lax.axis_size("tx") * lax.axis_size("ty") * EDGE**3)
    total = total * scale
    other = swapped(total, "ty", 1)
    return (result, grad_features, jnp.where(late, other, total), jnp.where(late, total, other))


def solution(mesh):
    return jax.shard_map(
        body,
        mesh=mesh,
        in_specs=(
            P(("tx", "ty"), None, None),
            P(("tx", "ty"), None),
            P(("tx", "ty"), None),
            P(),
            P(),
            P(("tx", "ty"), None, None),
        ),
        out_specs=(P(("tx", "ty"), None, None), P(("tx", "ty"), None, None), P(), P()),
        check_vma=False,
    )
```

time: 146 us -> 106 us (0.73)
  the two profiles are of different devices: /device:TPU:24 before, /device:TPU:1 now
where the time goes in v2:
time: 106 us
  starting transfers between devices  53.1 us (50%)
  waiting for transfers between devices  28.4 us (27%)
  Pallas kernels  17.6 us (17%)
  local copies, waits for them, and re-layouts  4.7 us (4%)
    ppermute x17, starting transfers between devices, swapped(): return lax.ppermute(value, axis, [(at, at ^ bit) for at in range(count)])  35.6 us
    pallas_call x9, Pallas kernels, run(): pl.pallas_call(kernel, out_shape=outs, in_specs=specs, out_specs=[pl.Bloc...  17.6 us
    ppermute x8, starting transfers between devices, paired(): lax.ppermute(value, axis, [(at, (at + 1 if at % 2 else at - 1) % count) f...  17.5 us
    ppermute x17, waiting for transfers between devices, swapped(): return lax.ppermute(value, axis, [(at, at ^ bit) for at in range(count)])  15.2 us
    ppermute x8, waiting for transfers between devices, paired(): lax.ppermute(value, axis, [(at, (at + 1 if at % 2 else at - 1) % count) f...  13.2 us
    unnamed x26, local copies, waits for them, and re-layouts  4.66 us
  transfers between devices with their start and end apart: 25, of which 15 were waited for; matrix products, arithmetic and copies ran while one was open for 0% of the time, Pallas kernels for 5%

profile of v2, /device:TPU:1, one launch (start us, length us, event | category | flops | bytes accessed | tf_op | source)
XLA Modules:
  0.0 105.6 jit_solution(6848831866585860176)
XLA Ops:
  0.7 1.1 %copy-done.1 = bf16[1024,256]{1,0:T(8,128)(2,1)S(1)} copy-done((bf16[1024,256]{1,0:T(8,128)(2,1)S(1)}, bf16[1024,256]{1,0:T(8,128)(2,1)}, u32[]{:S(2)}) %copy-start.1) | copy-done | bytes 524312
  1.8 0.8 copy-done.5
  2.7 0.9 copy-done.9
  3.6 0.7 copy-done.12
  4.3 1.6 %enter.1 = (bf16[6,32,1024]{2,1,0:T(8,128)(2,1)S(1)}, f32[6,1024]{1,0:T(8,128)S(1)}, bf16[6,32,128]{2,1,0:T(8,128)(2,1)S(1)}, bf16[6,32,128]{2,1,0:T(8,128)(2,1)S(1)}, bf16[6,32,256]{2,1,0:T(8,128)(2,1)S(1)}) custom-call(s32[3]{0:T(128)S(1)} %pad_add_fusion.place_ref, bf16[6,32,512]{2,1,0:T(8,128)(2,1)S(1)} %copy-done.9, s32[6,512]{1,0:T(8,128)S(1)} %copy-done.12, ...), custom_call_target="tpu_custom_call" | custom-call | flops 201326592 | bytes 1413132 | tf_op jit(solution)/shard_map/enter/pallas_call | solution.py:290
  6.0 3.3 %collective-permute-start.2 = (bf16[6,32,128]{2,1,0:T(8,128)(2,1)S(1)}, bf16[6,32,128]{2,1,0:T(8,128)(2,1)S(1)}, u32[]{:S(2)}, u32[]{:S(2)}) collective-permute-start(bf16[6,32,128]{2,1,0:T(8,128)(2,1)S(1)} %slice.16), channel_id=1, source_target_pairs={{0,1},{1,0},{2,3},{3,2},{4,5},{5,4},{6,7},{7,6},{8,9},{9,8},{10,11... | collective-permute-start | bytes 147464 | tf_op jit(solution)/shard_map/ppermute | solution.py:307
  9.3 2.8 %collective-permute-start = (bf16[6,32,128]{2,1,0:T(8,128)(2,1)S(1)}, bf16[6,32,128]{2,1,0:T(8,128)(2,1)S(1)}, u32[]{:S(2)}, u32[]{:S(2)}) collective-permute-start(bf16[6,32,128]{2,1,0:T(8,128)(2,1)S(1)} %get-tuple-element.51), channel_id=1, source_target_pairs={{0,32},{32,0},{64,96},{96,64},{128,160},{160,128},{192,224},{224,1... | collective-permute-start | bytes 147464 | tf_op jit(solution)/shard_map/ppermute | solution.py:307
  12.1 2.3 %collective-permute-start.1 = (bf16[6,32,128]{2,1,0:T(8,128)(2,1)S(1)}, bf16[6,32,128]{2,1,0:T(8,128)(2,1)S(1)}, u32[]{:S(2)}, u32[]{:S(2)}) collective-permute-start(bf16[6,32,128]{2,1,0:T(8,128)(2,1)S(1)} %get-tuple-element.52), channel_id=1, source_target_pairs={{0,224},{32,64},{64,32},{96,128},{128,96},{160,192},{192,160},{224... | collective-permute-start | bytes 147464 | tf_op jit(solution)/shard_map/ppermute | solution.py:314
  14.4 4.3 %collective-permute-done.1.r1 = bf16[6,32,128]{2,1,0:T(8,128)(2,1)S(1)} collective-permute-done((bf16[6,32,128]{2,1,0:T(8,128)(2,1)S(1)}, bf16[6,32,128]{2,1,0:T(8,128)(2,1)S(1)}, u32[]{:S(2)}, u32[]{:S(2)}) %collective-permute-start.1) | collective-permute-done | bytes 49184 | tf_op jit(solution)/shard_map/ppermute | solution.py:314
  18.7 1.0 copy-done.2
  19.7 2.5 %first.1 = (bf16[6,32,1280]{2,1,0:T(8,128)(2,1)S(1)}, bf16[6,32,1024]{2,1,0:T(8,128)(2,1)S(1)}, bf16[6,32,128]{2,1,0:T(8,128)(2,1)S(1)}, bf16[6,32,128]{2,1,0:T(8,128)(2,1)S(1)}, bf16[6,32,256]{2,1,0:T(8,128)(2,1)S(1)}) custom-call(s32[6,6]{1,0:T(8,128)S(1)} %copy-done.11, s32[3]{0:T(128)S(1)} %pad_add_fusion.place_ref, ...), custom_call_target="tpu_custom_call" | custom-call | flops 424673280 | bytes 2898076 | tf_op jit(solution)/shard_map/first/pallas_call | solution.py:290
  22.3 6.6 %collective-permute-start.6 = (bf16[6,32,128]{2,1,0:T(8,128)(2,1)S(1)}, bf16[6,32,128]{2,1,0:T(8,128)(2,1)S(1)}, u32[]{:S(2)}, u32[]{:S(2)}) collective-permute-start(bf16[6,32,128]{2,1,0:T(8,128)(2,1)S(1)} %slice.17), channel_id=1, source_target_pairs={{0,1},{1,0},{2,3},{3,2},{4,5},{5,4},{6,7},{7,6},{8,9},{9,8},{10,11... | collective-permute-start | bytes 147464 | tf_op jit(solution)/shard_map/ppermute | solution.py:307
  28.9 3.9 %collective-permute-start.5 = (bf16[6,32,128]{2,1,0:T(8,128)(2,1)S(1)}, bf16[6,32,128]{2,1,0:T(8,128)(2,1)S(1)}, u32[]{:S(2)}, u32[]{:S(2)}) collective-permute-start(bf16[6,32,128]{2,1,0:T(8,128)(2,1)S(1)} %get-tuple-element.57), channel_id=1, source_target_pairs={{0,224},{32,64},{64,32},{96,128},{128,96},{160,192},{192,160},{224... | collective-permute-start | bytes 147464 | tf_op jit(solution)/shard_map/ppermute | solution.py:314
  32.8 0.2 spread.1.cotangent_ref
  33.1 0.2 collective-permute-done.4.r0
  33.3 2.2 %collective-permute-done.5.r1 = bf16[6,32,128]{2,1,0:T(8,128)(2,1)S(1)} collective-permute-done((bf16[6,32,128]{2,1,0:T(8,128)(2,1)S(1)}, bf16[6,32,128]{2,1,0:T(8,128)(2,1)S(1)}, u32[]{:S(2)}, u32[]{:S(2)}) %collective-permute-start.5) | collective-permute-done | bytes 49184 | tf_op jit(solution)/shard_map/ppermute | solution.py:314
  35.5 3.3 %second.1 = (bf16[6,32,1280]{2,1,0:T(8,128)(2,1)S(1)}, bf16[6,32,512]{2,1,0:T(8,128)(2,1)}, bf16[6,32,1024]{2,1,0:T(8,128)(2,1)S(1)}, bf16[6,32,128]{2,1,0:T(8,1...) custom-call(s32[6,6]{1,0:T(8,128)S(1)} %copy-done.11, s32[3]{0:T(128)S(1)} %pad_add_fusion.place_ref, ...), custom_call_target="tpu_custom_call" | custom-call | flops 424673280 | bytes 3946652 | tf_op jit(solution)/shard_map/second/pallas_call | solution.py:290
  38.9 2.3 %collective-permute-start.10 = (bf16[6,32,128]{2,1,0:T(8,128)(2,1)S(1)}, bf16[6,32,128]{2,1,0:T(8,128)(2,1)S(1)}, u32[]{:S(2)}, u32[]{:S(2)}) collective-permute-start(bf16[6,32,128]{2,1,0:T(8,128)(2,1)S(1)} %slice.18), channel_id=1, source_target_pairs={{0,1},{1,0},{2,3},{3,2},{4,5},{5,4},{6,7},{7,6},{8,9},{9,8},{10,11... | collective-permute-start | bytes 147464 | tf_op jit(solution)/shard_map/ppermute | solution.py:307
  41.2 0.7 collective-permute-start.11
  41.9 2.0 %collective-permute-start.8 = (bf16[6,32,128]{2,1,0:T(8,128)(2,1)S(1)}, bf16[6,32,128]{2,1,0:T(8,128)(2,1)S(1)}, u32[]{:S(2)}, u32[]{:S(2)}) collective-permute-start(bf16[6,32,128]{2,1,0:T(8,128)(2,1)S(1)} %get-tuple-element.63), channel_id=1, source_target_pairs={{0,32},{32,0},{64,96},{96,64},{128,160},{160,128},{192,224},{224,1... | collective-permute-start | bytes 147464 | tf_op jit(solution)/shard_map/ppermute | solution.py:307
  43.9 2.6 %collective-permute-start.9 = (bf16[6,32,128]{2,1,0:T(8,128)(2,1)S(1)}, bf16[6,32,128]{2,1,0:T(8,128)(2,1)S(1)}, u32[]{:S(2)}, u32[]{:S(2)}) collective-permute-start(bf16[6,32,128]{2,1,0:T(8,128)(2,1)S(1)} %get-tuple-element.64), channel_id=1, source_target_pairs={{0,224},{32,64},{64,32},{96,128},{128,96},{160,192},{192,160},{224... | collective-permute-start | bytes 147464 | tf_op jit(solution)/shard_map/ppermute | solution.py:314
  46.4 0.3 turn.1
  46.8 1.9 %weights.2 = f32[32,864]{1,0:T(8,128)S(1)} custom-call(bf16[6,32,1280]{2,1,0:T(8,128)(2,1)S(1)} %get-tuple-element.59.cells_ref, bf16[6,32,1024]{2,1,0:T(8,128)(2,1)S(1)} %get-tuple-element.60.grad_ref.inner_ref), custom_call_target="tpu_custom_call" | custom-call | flops 424673280 | bytes 995328 | tf_op jit(solution)/shard_map/weights/pallas_call | solution.py:290
  48.7 1.8 %collective-permute-done.9.r1 = bf16[6,32,128]{2,1,0:T(8,128)(2,1)S(1)} collective-permute-done((bf16[6,32,128]{2,1,0:T(8,128)(2,1)S(1)}, bf16[6,32,128]{2,1,0:T(8,128)(2,1)S(1)}, u32[]{:S(2)}, u32[]{:S(2)}) %collective-permute-start.9) | collective-permute-done | bytes 49184 | tf_op jit(solution)/shard_map/ppermute | solution.py:314
  50.4 2.5 %third.1 = (bf16[6,32,1024]{2,1,0:T(8,128)(2,1)S(1)}, bf16[6,32,128]{2,1,0:T(8,128)(2,1)S(1)}, bf16[6,32,128]{2,1,0:T(8,128)(2,1)S(1)}, bf16[6,32,256]{2,1,0:T(8,128)(2,1)S(1)}) custom-call(s32[6,6]{1,0:T(8,128)S(1)} %copy-done.11, s32[3]{0:T(128)S(1)} %pad_add_fusion.place_ref, bf16[6,32,1024]{2,1,0:T(8,128)(2,1)S(1)} %get-tuple-element.60.grad_ref.inner_ref, ...), custom_call_target="tpu_custom_call" | custom-call | flops 424673280 | bytes 2799772 | tf_op jit(solution)/shard_map/third/pallas_call | solution.py:290
  53.0 1.9 %weights.3 = f32[32,864]{1,0:T(8,128)S(1)} custom-call(bf16[6,32,1280]{2,1,0:T(8,128)(2,1)S(1)} %get-tuple-element.61.cells_ref, bf16[6,32,1024]{2,1,0:T(8,128)(2,1)S(1)} %get-tuple-element.66.grad_ref.inner_ref), custom_call_target="tpu_custom_call" | custom-call | flops 424673280 | bytes 995328 | tf_op jit(solution)/shard_map/weights/pallas_call | solution.py:290
  54.9 2.9 %collective-permute-start.12 = (f32[32,864]{1,0:T(8,128)S(1)}, f32[32,864]{1,0:T(8,128)S(1)}, u32[]{:S(2)}, u32[]{:S(2)}) collective-permute-start(f32[32,864]{1,0:T(8,128)S(1)} %broadcast_select_fusion.2), channel_id=1, source_target_pairs={{0,1},{1,0},{2,3},{3,2},{4,5},{5,4},{6,7},{7,6},{8,9},{9,8},{10,11... | collective-permute-start | bytes 331784 | tf_op jit(solution)/shard_map/ppermute | solution.py:307
  57.8 1.0 collective-permute-done.12
  59.0 2.9 %collective-permute-done.13 = bf16[32,864]{1,0:T(8,128)(2,1)S(1)} collective-permute-done((bf16[32,864]{1,0:T(8,128)(2,1)S(1)}, bf16[32,864]{1,0:T(8,128)(2,1)S(1)}, u32[]{:S(2)}, u32[]{:S(2)}) %collective-permute-start.13) | collective-permute-done | bytes 55328 | tf_op jit(solution)/shard_map/ppermute | solution.py:307
  62.0 1.5 %collective-permute-done.14.r0 = bf16[6,32,128]{2,1,0:T(8,128)(2,1)S(1)} collective-permute-done((bf16[6,32,128]{2,1,0:T(8,128)(2,1)S(1)}, bf16[6,32,128]{2,1,0:T(8,128)(2,1)S(1)}, u32[]{:S(2)}, u32[]{:S(2)}) %collective-permute-start.14) | collective-permute-done | bytes 49184 | tf_op jit(solution)/shard_map/ppermute | solution.py:307
  63.4 0.2 collective-permute-start.15
  63.7 2.7 %collective-permute-start.16 = (bf16[6,32,128]{2,1,0:T(8,128)(2,1)S(1)}, bf16[6,32,128]{2,1,0:T(8,128)(2,1)S(1)}, u32[]{:S(2)}, u32[]{:S(2)}) collective-permute-start(bf16[6,32,128]{2,1,0:T(8,128)(2,1)S(1)} %get-tuple-element.73), channel_id=1, source_target_pairs={{0,224},{32,64},{64,32},{96,128},{128,96},{160,192},{192,160},{224... | collective-permute-start | bytes 147464 | tf_op jit(solution)/shard_map/ppermute | solution.py:314
  66.4 1.0 collective-permute-done.15
  67.4 2.9 %collective-permute-done.16.r1 = bf16[6,32,128]{2,1,0:T(8,128)(2,1)S(1)} collective-permute-done((bf16[6,32,128]{2,1,0:T(8,128)(2,1)S(1)}, bf16[6,32,128]{2,1,0:T(8,128)(2,1)S(1)}, u32[]{:S(2)}, u32[]{:S(2)}) %collective-permute-start.16) | collective-permute-done | bytes 49184 | tf_op jit(solution)/shard_map/ppermute | solution.py:314
  70.3 3.2 %collective-permute-start.17 = (bf16[32,864]{1,0:T(8,128)(2,1)S(1)}, bf16[32,864]{1,0:T(8,128)(2,1)S(1)}, u32[]{:S(2)}, u32[]{:S(2)}) collective-permute-start(bf16[32,864]{1,0:T(8,128)(2,1)S(1)} %add_convert_fusion.3), channel_id=1, source_target_pairs={{0,8},{1,9},{2,10},{3,11},{4,12},{5,13},{6,14},{7,15},{8,0},{9,1},... | collective-permute-start | bytes 165896 | tf_op jit(solution)/shard_map/ppermute | solution.py:307
  73.5 3.3 %collective-permute-start.18 = (bf16[6,32,128]{2,1,0:T(8,128)(2,1)S(1)}, bf16[6,32,128]{2,1,0:T(8,128)(2,1)S(1)}, u32[]{:S(2)}, u32[]{:S(2)}) collective-permute-start(bf16[6,32,128]{2,1,0:T(8,128)(2,1)S(1)} %slice.19), channel_id=1, source_target_pairs={{0,1},{1,0},{2,3},{3,2},{4,5},{5,4},{6,7},{7,6},{8,9},{9,8},{10,11... | collective-permute-start | bytes 147464 | tf_op jit(solution)/shard_map/ppermute | solution.py:307
  76.8 0.5 collective-permute-done.17
  77.3 0.4 collective-permute-done.18.r2
  77.8 5.3 %collective-permute-start.20 = (bf16[6,32,128]{2,1,0:T(8,128)(2,1)S(1)}, bf16[6,32,128]{2,1,0:T(8,128)(2,1)S(1)}, u32[]{:S(2)}, u32[]{:S(2)}) collective-permute-start(bf16[6,32,128]{2,1,0:T(8,128)(2,1)S(1)} %slice.19), channel_id=1, source_target_pairs={{0,31},{1,2},{2,1},{3,4},{4,3},{5,6},{6,5},{7,8},{8,7},{9,10},{10,... | collective-permute-start | bytes 147464 | tf_op jit(solution)/shard_map/ppermute | solution.py:314
  83.1 2.0 %collective-permute-done.20.r3 = bf16[6,32,128]{2,1,0:T(8,128)(2,1)S(1)} collective-permute-done((bf16[6,32,128]{2,1,0:T(8,128)(2,1)S(1)}, bf16[6,32,128]{2,1,0:T(8,128)(2,1)S(1)}, u32[]{:S(2)}, u32[]{:S(2)}) %collective-permute-start.20) | collective-permute-done | bytes 49184 | tf_op jit(solution)/shard_map/ppermute | solution.py:314
  85.2 4.5 %collective-permute-done.21 = bf16[32,864]{1,0:T(8,128)(2,1)S(1)} collective-permute-done((bf16[32,864]{1,0:T(8,128)(2,1)S(1)}, bf16[32,864]{1,0:T(8,128)(2,1)S(1)}, u32[]{:S(2)}, u32[]{:S(2)}) %collective-permute-start.21) | collective-permute-done | bytes 55328 | tf_op jit(solution)/shard_map/ppermute | solution.py:307
  89.7 0.3 collective-permute-start.22
  90.1 3.2 %last.1 = bf16[6,32,512]{2,1,0:T(8,128)(2,1)} custom-call(s32[6,6]{1,0:T(8,128)S(1)} %copy-done.11, s32[3]{0:T(128)S(1)} %pad_add_fusion.place_ref, bf16[6,32,1024]{2,1,0:T(8,128)(2,1)S(1)} %get-tuple-element.66.grad_ref.inner_ref, bf16[6,32,256]{2,1,0:T(8,128)(2,1)S(1)} %get-tuple-element.75.side_ref, bf16[6,32,128]{2,1,0:T(8,128)(2,1)S(1)} %collective-permute-done.14.r0, ...), custom_call_target="tpu_custom_call" | custom-call | flops 424673280 | bytes 1947804 | tf_op jit(solution)/shard_map/last/pallas_call | solution.py:290
  93.3 2.4 %collective-permute-start.23 = (bf16[32,864]{1,0:T(8,128)(2,1)S(1)}, bf16[32,864]{1,0:T(8,128)(2,1)S(1)}, u32[]{:S(2)}, u32[]{:S(2)}) collective-permute-start(bf16[32,864]{1,0:T(8,128)(2,1)S(1)} %convert_add_fusion), channel_id=1, source_target_pairs={{0,128},{32,160},{64,192},{96,224},{128,0},{160,32},{192,64},{224,... | collective-permute-start | bytes 165896 | tf_op jit(solution)/shard_map/ppermute | solution.py:307
  95.7 2.2 %collective-permute-done.23 = bf16[32,864]{1,0:T(8,128)(2,1)S(1)} collective-permute-done((bf16[32,864]{1,0:T(8,128)(2,1)S(1)}, bf16[32,864]{1,0:T(8,128)(2,1)S(1)}, u32[]{:S(2)}, u32[]{:S(2)}) %collective-permute-start.23) | collective-permute-done | bytes 55328 | tf_op jit(solution)/shard_map/ppermute | solution.py:307
  98.0 6.0 %collective-permute-start.24 = (f32[32,864]{1,0:T(8,128)S(1)}, f32[32,864]{1,0:T(8,128)S(1)}, u32[]{:S(2)}, u32[]{:S(2)}) collective-permute-start(f32[32,864]{1,0:T(8,128)S(1)} %add_multiply_fusion), channel_id=1, source_target_pairs={{0,1},{1,0},{2,3},{3,2},{4,5},{5,4},{6,7},{7,6},{8,9},{9,8},{10,11... | collective-permute-start | bytes 331784 | tf_op jit(solution)/shard_map/ppermute | solution.py:307
  103.9 1.0 collective-permute-done.24
  104.9 0.7 broadcast_select_fusion
  (52 shorter events, 0.6 us)
Async XLA Ops:
  0.6 18.0 %copy-start = (bf16[256,1024]{1,0:T(8,128)(2,1)S(1)}, bf16[256,1024]{1,0:T(8,128)(2,1)}, u32[]{:S(2)}) copy-start(bf16[256,1024]{1,0:T(8,128)(2,1)} %constant.46.clone.put_ref) | copy-start | bytes 1572868
  0.7 1.1 %copy-start.1 = (bf16[1024,256]{1,0:T(8,128)(2,1)S(1)}, bf16[1024,256]{1,0:T(8,128)(2,1)}, u32[]{:S(2)}) copy-start(bf16[1024,256]{1,0:T(8,128)(2,1)} %constant.45.clone.pick_hbm.pick_ref) | copy-start | bytes 1572868
  1.8 0.8 copy-start.5
  2.7 0.9 copy-start.9
  3.6 0.7 copy-start.12
  5.9 12.7 %copy-start.7 = (bf16[32,864]{1,0:T(8,128)(2,1)S(1)}, bf16[32,864]{1,0:T(8,128)(2,1)}, u32[]{:S(2)}) copy-start(bf16[32,864]{1,0:T(8,128)(2,1)} %first_ref.1) | copy-start | bytes 165892
  6.0 12.7 %copy-start.11 = (s32[6,6]{1,0:T(8,128)S(1)}, s32[6,6]{1,0:T(8,128)}, u32[]{:S(2)}) copy-start(s32[6,6]{1,0:T(8,128)} %neighbours_ref.7) | copy-start | bytes 436
  6.0 8.4 %collective-permute-start.2 = (bf16[6,32,128]{2,1,0:T(8,128)(2,1)S(1)}, bf16[6,32,128]{2,1,0:T(8,128)(2,1)S(1)}, u32[]{:S(2)}, u32[]{:S(2)}) collective-permute-start(bf16[6,32,128]{2,1,0:T(8,128)(2,1)S(1)} %slice.16), channel_id=1, source_target_pairs={{0,1},{1,0},{2,3},{3,2},{4,5},{5,4},{6,7},{7,6},{8,9},{9,8},{10,11... | collective-permute-start | bytes 147464 | tf_op jit(solution)/shard_map/ppermute | solution.py:307
  9.3 5.1 %collective-permute-start.3 = (bf16[6,32,128]{2,1,0:T(8,128)(2,1)S(1)}, bf16[6,32,128]{2,1,0:T(8,128)(2,1)S(1)}, u32[]{:S(2)}, u32[]{:S(2)}) collective-permute-start(bf16[6,32,128]{2,1,0:T(8,128)(2,1)S(1)} %slice.16), channel_id=1, source_target_pairs={{0,31},{1,2},{2,1},{3,4},{4,3},{5,6},{6,5},{7,8},{8,7},{9,10},{10,... | collective-permute-start | bytes 147464 | tf_op jit(solution)/shard_map/ppermute | solution.py:314
  9.3 5.1 %collective-permute-start = (bf16[6,32,128]{2,1,0:T(8,128)(2,1)S(1)}, bf16[6,32,128]{2,1,0:T(8,128)(2,1)S(1)}, u32[]{:S(2)}, u32[]{:S(2)}) collective-permute-start(bf16[6,32,128]{2,1,0:T(8,128)(2,1)S(1)} %get-tuple-element.51), channel_id=1, source_target_pairs={{0,32},{32,0},{64,96},{96,64},{128,160},{160,128},{192,224},{224,1... | collective-permute-start | bytes 147464 | tf_op jit(solution)/shard_map/ppermute | solution.py:307
  12.1 6.6 %collective-permute-start.1 = (bf16[6,32,128]{2,1,0:T(8,128)(2,1)S(1)}, bf16[6,32,128]{2,1,0:T(8,128)(2,1)S(1)}, u32[]{:S(2)}, u32[]{:S(2)}) collective-permute-start(bf16[6,32,128]{2,1,0:T(8,128)(2,1)S(1)} %get-tuple-element.52), channel_id=1, source_target_pairs={{0,224},{32,64},{64,32},{96,128},{128,96},{160,192},{192,160},{224... | collective-permute-start | bytes 147464 | tf_op jit(solution)/shard_map/ppermute | solution.py:314
  18.7 1.0 copy-start.2
  19.7 13.1 %copy-start.6 = (bf16[128,256]{1,0:T(8,128)(2,1)S(1)}, bf16[128,256]{1,0:T(8,128)(2,1)}, u32[]{:S(2)}) copy-start(bf16[128,256]{1,0:T(8,128)(2,1)} %constant.43.clone.spread_hbm.spread_ref) | copy-start | bytes 196612
  19.7 13.1 %copy-start.10 = (bf16[6,32,512]{2,1,0:T(8,128)(2,1)S(1)}, bf16[6,32,512]{2,1,0:T(8,128)(2,1)}, u32[]{:S(2)}) copy-start(bf16[6,32,512]{2,1,0:T(8,128)(2,1)} %cotangent_ref.1) | copy-start | bytes 589828
  22.2 13.3 %copy-start.3 = (bf16[1024,256]{1,0:T(8,128)(2,1)S(1)}, bf16[1024,256]{1,0:T(8,128)(2,1)}, u32[]{:S(2)}) copy-start(bf16[1024,256]{1,0:T(8,128)(2,1)} %constant.45.clone.pick_hbm.pick_ref) | copy-start | bytes 1572868
  22.3 10.8 %collective-permute-start.6 = (bf16[6,32,128]{2,1,0:T(8,128)(2,1)S(1)}, bf16[6,32,128]{2,1,0:T(8,128)(2,1)S(1)}, u32[]{:S(2)}, u32[]{:S(2)}) collective-permute-start(bf16[6,32,128]{2,1,0:T(8,128)(2,1)S(1)} %slice.17), channel_id=1, source_target_pairs={{0,1},{1,0},{2,3},{3,2},{4,5},{5,4},{6,7},{7,6},{8,9},{9,8},{10,11... | collective-permute-start | bytes 147464 | tf_op jit(solution)/shard_map/ppermute | solution.py:307
  28.8 4.2 %collective-permute-start.7 = (bf16[6,32,128]{2,1,0:T(8,128)(2,1)S(1)}, bf16[6,32,128]{2,1,0:T(8,128)(2,1)S(1)}, u32[]{:S(2)}, u32[]{:S(2)}) collective-permute-start(bf16[6,32,128]{2,1,0:T(8,128)(2,1)S(1)} %slice.17), channel_id=1, source_target_pairs={{0,31},{1,2},{2,1},{3,4},{4,3},{5,6},{6,5},{7,8},{8,7},{9,10},{10,... | collective-permute-start | bytes 147464 | tf_op jit(solution)/shard_map/ppermute | solution.py:314
  28.8 4.4 %collective-permute-start.4 = (bf16[6,32,128]{2,1,0:T(8,128)(2,1)S(1)}, bf16[6,32,128]{2,1,0:T(8,128)(2,1)S(1)}, u32[]{:S(2)}, u32[]{:S(2)}) collective-permute-start(bf16[6,32,128]{2,1,0:T(8,128)(2,1)S(1)} %get-tuple-element.56), channel_id=1, source_target_pairs={{0,32},{32,0},{64,96},{96,64},{128,160},{160,128},{192,224},{224,1... | collective-permute-start | bytes 147464 | tf_op jit(solution)/shard_map/ppermute | solution.py:307
  28.8 6.7 %copy-start.4 = (bf16[256,128]{1,0:T(8,128)(2,1)S(1)}, bf16[256,128]{1,0:T(8,128)(2,1)}, u32[]{:S(2)}) copy-start(bf16[256,128]{1,0:T(8,128)(2,1)} %constant.44.clone.gather_ref) | copy-start | bytes 196612
  28.8 6.7 %copy-start.8 = (bf16[32,864]{1,0:T(8,128)(2,1)S(1)}, bf16[32,864]{1,0:T(8,128)(2,1)}, u32[]{:S(2)}) copy-start(bf16[32,864]{1,0:T(8,128)(2,1)} %second_ref.1) | copy-start | bytes 165892
  28.9 6.6 %collective-permute-start.5 = (bf16[6,32,128]{2,1,0:T(8,128)(2,1)S(1)}, bf16[6,32,128]{2,1,0:T(8,128)(2,1)S(1)}, u32[]{:S(2)}, u32[]{:S(2)}) collective-permute-start(bf16[6,32,128]{2,1,0:T(8,128)(2,1)S(1)} %get-tuple-element.57), channel_id=1, source_target_pairs={{0,224},{32,64},{64,32},{96,128},{128,96},{160,192},{192,160},{224... | collective-permute-start | bytes 147464 | tf_op jit(solution)/shard_map/ppermute | solution.py:314
  38.9 9.8 %collective-permute-start.10 = (bf16[6,32,128]{2,1,0:T(8,128)(2,1)S(1)}, bf16[6,32,128]{2,1,0:T(8,128)(2,1)S(1)}, u32[]{:S(2)}, u32[]{:S(2)}) collective-permute-start(bf16[6,32,128]{2,1,0:T(8,128)(2,1)S(1)} %slice.18), channel_id=1, source_target_pairs={{0,1},{1,0},{2,3},{3,2},{4,5},{5,4},{6,7},{7,6},{8,9},{9,8},{10,11... | collective-permute-start | bytes 147464 | tf_op jit(solution)/shard_map/ppermute | solution.py:307
  41.2 7.5 %collective-permute-start.11 = (bf16[6,32,128]{2,1,0:T(8,128)(2,1)S(1)}, bf16[6,32,128]{2,1,0:T(8,128)(2,1)S(1)}, u32[]{:S(2)}, u32[]{:S(2)}) collective-permute-start(bf16[6,32,128]{2,1,0:T(8,128)(2,1)S(1)} %slice.18), channel_id=1, source_target_pairs={{0,31},{1,2},{2,1},{3,4},{4,3},{5,6},{6,5},{7,8},{8,7},{9,10},{10,... | collective-permute-start | bytes 147464 | tf_op jit(solution)/shard_map/ppermute | solution.py:314
  41.9 6.8 %collective-permute-start.8 = (bf16[6,32,128]{2,1,0:T(8,128)(2,1)S(1)}, bf16[6,32,128]{2,1,0:T(8,128)(2,1)S(1)}, u32[]{:S(2)}, u32[]{:S(2)}) collective-permute-start(bf16[6,32,128]{2,1,0:T(8,128)(2,1)S(1)} %get-tuple-element.63), channel_id=1, source_target_pairs={{0,32},{32,0},{64,96},{96,64},{128,160},{160,128},{192,224},{224,1... | collective-permute-start | bytes 147464 | tf_op jit(solution)/shard_map/ppermute | solution.py:307
  43.9 6.6 %collective-permute-start.9 = (bf16[6,32,128]{2,1,0:T(8,128)(2,1)S(1)}, bf16[6,32,128]{2,1,0:T(8,128)(2,1)S(1)}, u32[]{:S(2)}, u32[]{:S(2)}) collective-permute-start(bf16[6,32,128]{2,1,0:T(8,128)(2,1)S(1)} %get-tuple-element.64), channel_id=1, source_target_pairs={{0,224},{32,64},{64,32},{96,128},{128,96},{160,192},{192,160},{224... | collective-permute-start | bytes 147464 | tf_op jit(solution)/shard_map/ppermute | solution.py:314
  54.9 3.9 %collective-permute-start.12 = (f32[32,864]{1,0:T(8,128)S(1)}, f32[32,864]{1,0:T(8,128)S(1)}, u32[]{:S(2)}, u32[]{:S(2)}) collective-permute-start(f32[32,864]{1,0:T(8,128)S(1)} %broadcast_select_fusion.2), channel_id=1, source_target_pairs={{0,1},{1,0},{2,3},{3,2},{4,5},{5,4},{6,7},{7,6},{8,9},{9,8},{10,11... | collective-permute-start | bytes 331784 | tf_op jit(solution)/shard_map/ppermute | solution.py:307
  58.8 3.1 %collective-permute-start.13 = (bf16[32,864]{1,0:T(8,128)(2,1)S(1)}, bf16[32,864]{1,0:T(8,128)(2,1)S(1)}, u32[]{:S(2)}, u32[]{:S(2)}) collective-permute-start(bf16[32,864]{1,0:T(8,128)(2,1)S(1)} %add_convert_fusion.5), channel_id=1, source_target_pairs={{0,2},{1,3},{2,0},{3,1},{4,6},{5,7},{6,4},{7,5},{8,10},{9,11},{10,... | collective-permute-start | bytes 165896 | tf_op jit(solution)/shard_map/ppermute | solution.py:307
  58.9 4.5 %collective-permute-start.14 = (bf16[6,32,128]{2,1,0:T(8,128)(2,1)S(1)}, bf16[6,32,128]{2,1,0:T(8,128)(2,1)S(1)}, u32[]{:S(2)}, u32[]{:S(2)}) collective-permute-start(bf16[6,32,128]{2,1,0:T(8,128)(2,1)S(1)} %get-tuple-element.69), channel_id=1, source_target_pairs={{0,32},{32,0},{64,96},{96,64},{128,160},{160,128},{192,224},{224,1... | collective-permute-start | bytes 147464 | tf_op jit(solution)/shard_map/ppermute | solution.py:307
  63.4 3.9 %collective-permute-start.15 = (bf16[32,864]{1,0:T(8,128)(2,1)S(1)}, bf16[32,864]{1,0:T(8,128)(2,1)S(1)}, u32[]{:S(2)}, u32[]{:S(2)}) collective-permute-start(bf16[32,864]{1,0:T(8,128)(2,1)S(1)} %add_convert_fusion.4), channel_id=1, source_target_pairs={{0,4},{1,5},{2,6},{3,7},{4,0},{5,1},{6,2},{7,3},{8,12},{9,13},{10,... | collective-permute-start | bytes 165896 | tf_op jit(solution)/shard_map/ppermute | solution.py:307
  63.7 6.6 %collective-permute-start.16 = (bf16[6,32,128]{2,1,0:T(8,128)(2,1)S(1)}, bf16[6,32,128]{2,1,0:T(8,128)(2,1)S(1)}, u32[]{:S(2)}, u32[]{:S(2)}) collective-permute-start(bf16[6,32,128]{2,1,0:T(8,128)(2,1)S(1)} %get-tuple-element.73), channel_id=1, source_target_pairs={{0,224},{32,64},{64,32},{96,128},{128,96},{160,192},{192,160},{224... | collective-permute-start | bytes 147464 | tf_op jit(solution)/shard_map/ppermute | solution.py:314
  70.3 7.0 %collective-permute-start.17 = (bf16[32,864]{1,0:T(8,128)(2,1)S(1)}, bf16[32,864]{1,0:T(8,128)(2,1)S(1)}, u32[]{:S(2)}, u32[]{:S(2)}) collective-permute-start(bf16[32,864]{1,0:T(8,128)(2,1)S(1)} %add_convert_fusion.3), channel_id=1, source_target_pairs={{0,8},{1,9},{2,10},{3,11},{4,12},{5,13},{6,14},{7,15},{8,0},{9,1},... | collective-permute-start | bytes 165896 | tf_op jit(solution)/shard_map/ppermute | solution.py:307
  73.5 4.2 %collective-permute-start.18 = (bf16[6,32,128]{2,1,0:T(8,128)(2,1)S(1)}, bf16[6,32,128]{2,1,0:T(8,128)(2,1)S(1)}, u32[]{:S(2)}, u32[]{:S(2)}) collective-permute-start(bf16[6,32,128]{2,1,0:T(8,128)(2,1)S(1)} %slice.19), channel_id=1, source_target_pairs={{0,1},{1,0},{2,3},{3,2},{4,5},{5,4},{6,7},{7,6},{8,9},{9,8},{10,11... | collective-permute-start | bytes 147464 | tf_op jit(solution)/shard_map/ppermute | solution.py:307
  77.7 5.4 %collective-permute-start.19 = (bf16[32,864]{1,0:T(8,128)(2,1)S(1)}, bf16[32,864]{1,0:T(8,128)(2,1)S(1)}, u32[]{:S(2)}, u32[]{:S(2)}) collective-permute-start(bf16[32,864]{1,0:T(8,128)(2,1)S(1)} %add_convert_fusion.2), channel_id=1, source_target_pairs={{0,16},{1,17},{2,18},{3,19},{4,20},{5,21},{6,22},{7,23},{8,24},{9,... | collective-permute-start | bytes 165896 | tf_op jit(solution)/shard_map/ppermute | solution.py:307
  77.8 7.4 %collective-permute-start.20 = (bf16[6,32,128]{2,1,0:T(8,128)(2,1)S(1)}, bf16[6,32,128]{2,1,0:T(8,128)(2,1)S(1)}, u32[]{:S(2)}, u32[]{:S(2)}) collective-permute-start(bf16[6,32,128]{2,1,0:T(8,128)(2,1)S(1)} %slice.19), channel_id=1, source_target_pairs={{0,31},{1,2},{2,1},{3,4},{4,3},{5,6},{6,5},{7,8},{8,7},{9,10},{10,... | collective-permute-start | bytes 147464 | tf_op jit(solution)/shard_map/ppermute | solution.py:314
  85.2 4.5 %collective-permute-start.21 = (bf16[32,864]{1,0:T(8,128)(2,1)S(1)}, bf16[32,864]{1,0:T(8,128)(2,1)S(1)}, u32[]{:S(2)}, u32[]{:S(2)}) collective-permute-start(bf16[32,864]{1,0:T(8,128)(2,1)S(1)} %add_convert_fusion.1), channel_id=1, source_target_pairs={{0,32},{32,0},{64,96},{96,64},{128,160},{160,128},{192,224},{224,1... | collective-permute-start | bytes 165896 | tf_op jit(solution)/shard_map/ppermute | solution.py:307
  89.7 3.6 %collective-permute-start.22 = (bf16[32,864]{1,0:T(8,128)(2,1)S(1)}, bf16[32,864]{1,0:T(8,128)(2,1)S(1)}, u32[]{:S(2)}, u32[]{:S(2)}) collective-permute-start(bf16[32,864]{1,0:T(8,128)(2,1)S(1)} %add_convert_fusion), channel_id=1, source_target_pairs={{0,64},{32,96},{64,0},{96,32},{128,192},{160,224},{192,128},{224,1... | collective-permute-start | bytes 165896 | tf_op jit(solution)/shard_map/ppermute | solution.py:307
  93.3 4.6 %collective-permute-start.23 = (bf16[32,864]{1,0:T(8,128)(2,1)S(1)}, bf16[32,864]{1,0:T(8,128)(2,1)S(1)}, u32[]{:S(2)}, u32[]{:S(2)}) collective-permute-start(bf16[32,864]{1,0:T(8,128)(2,1)S(1)} %convert_add_fusion), channel_id=1, source_target_pairs={{0,128},{32,160},{64,192},{96,224},{128,0},{160,32},{192,64},{224,... | collective-permute-start | bytes 165896 | tf_op jit(solution)/shard_map/ppermute | solution.py:307
  98.0 6.9 %collective-permute-start.24 = (f32[32,864]{1,0:T(8,128)S(1)}, f32[32,864]{1,0:T(8,128)S(1)}, u32[]{:S(2)}, u32[]{:S(2)}) collective-permute-start(f32[32,864]{1,0:T(8,128)S(1)} %add_multiply_fusion), channel_id=1, source_target_pairs={{0,1},{1,0},{2,3},{3,2},{4,5},{5,4},{6,7},{7,6},{8,9},{9,8},{10,11... | collective-permute-start | bytes 331784 | tf_op jit(solution)/shard_map/ppermute | solution.py:307

commit v3 on v2

v3 whole, which is shorter than its diff:
```python
import math

import jax
import jax.numpy as jnp
from jax import lax
from jax.experimental import pallas as pl
from jax.experimental.pallas import tpu as pltpu
from jax.sharding import PartitionSpec as P


EDGE = 8
LANES = 128
PITCH = 10
SLOTS = 6
CHANS = 32
INNER = EDGE * LANES
WHOLE = (EDGE + 2) * LANES
BF16 = jnp.bfloat16
F32 = jnp.float32
VMEM_LIMIT = 16 * 1024 * 1024


def iota(dims, axis):
    return lax.broadcasted_iota(jnp.int32, dims, axis)


def one_hot(test):
    return jnp.where(test, 1.0, 0.0).astype(BF16)


def spread_lane(at):
    return (at >> 6) * LANES + ((at >> 3) % EDGE + 1) * PITCH + at % EDGE + 1


def widening():
    return one_hot(iota((LANES, 2 * LANES), 1) == spread_lane(iota((LANES, 1), 0)))


def narrowing():
    return one_hot(iota((2 * LANES, LANES), 0) == spread_lane(iota((1, LANES), 1)))


def face_lane(at, lanes):
    spot = at % EDGE
    group = at >> 6
    low_y, high_y, low_z, high_z = lanes
    lane = jnp.where(group == 0, low_y + spot, high_y + spot)
    lane = jnp.where(group == 2, (spot + 1) * PITCH + low_z, lane)
    lane = jnp.where(group == 3, (spot + 1) * PITCH + high_z, lane)
    return ((at >> 3) % EDGE) * LANES + lane


def picking():
    target = face_lane(iota((1, 256), 1), (EDGE * PITCH + 1, PITCH + 1, EDGE, 1))
    return one_hot(iota((INNER, 256), 0) == target)


def putting():
    target = face_lane(iota((256, 1), 0), (1, (EDGE + 1) * PITCH + 1, 0, EDGE + 1))
    return one_hot(iota((256, INNER), 1) == target)


def dot(lhs, rhs):
    return jnp.dot(lhs, rhs, preferred_element_type=F32)


def spread(field, matrix):
    return [dot(field[:, at * LANES : (at + 1) * LANES], matrix) for at in range(4)]


def emit_faces(place_ref, inner_ref, pick_ref, even_ref, odd_ref, side_ref, end_ref):
    raised = place_ref[1] == 1
    low = inner_ref[:, :, :LANES]
    high = inner_ref[:, :, INNER - LANES :]
    even_ref[...] = jnp.where(raised, low, high)
    odd_ref[...] = jnp.where(raised, high, low)
    flat = inner_ref[...].reshape(SLOTS * CHANS, INNER)
    found = dot(flat, pick_ref[...]).astype(BF16)
    side_ref[...] = found[:, :LANES].reshape(FACE)
    end_ref[...] = found[:, LANES:].reshape(FACE)


def build_cells(cells_ref, sheet_ref, inner_ref, side_ref, end_ref, remote_refs, put_ref, neighbours_ref, place_ref):
    base = place_ref[0]
    lane = lax.broadcasted_iota(jnp.int32, (1, LANES), 1)
    lower = (lane < 64).astype(F32).astype(BF16)
    upper = (lane >= 64).astype(F32).astype(BF16)
    zero = jnp.zeros((CHANS, LANES), BF16)

    x_odd_ref, x_even_ref, y_odd_ref, y_even_ref = remote_refs
    pairs = ((x_odd_ref, x_even_ref), (x_even_ref, x_odd_ref), (y_odd_ref, y_even_ref), (y_even_ref, y_odd_ref))

    def picked(slot, face, local):
        ident = neighbours_ref[slot, face]
        place = lax.rem(jnp.maximum(ident, 0), SLOTS)
        value = local(place)
        if face < 4:
            here = (ident >= base) & (ident < base + SLOTS)
            settled, raised = pairs[face]
            distant = jnp.where(place_ref[1 + face // 2] == 1, raised[place], settled[place])
            value = jnp.where(here, value, distant)
        return jnp.where(ident >= 0, value, zero)

    for slot in range(SLOTS):
        cells_ref[slot, :, :LANES] = picked(
            slot, 0, lambda at: inner_ref[at, :, INNER - LANES :]
        )
        cells_ref[slot, :, WHOLE - LANES :] = picked(
            slot, 1, lambda at: inner_ref[at, :, :LANES]
        )
        sides = lambda at: side_ref[at]
        ends = lambda at: end_ref[at]
        rows = pl.ds(slot * CHANS, CHANS)
        sheet_ref[rows, :LANES] = (
            picked(slot, 2, sides) * lower + picked(slot, 3, sides) * upper
        )
        sheet_ref[rows, LANES:] = (
            picked(slot, 4, ends) * lower + picked(slot, 5, ends) * upper
        )
    halo = dot(sheet_ref[...], put_ref[...]).astype(BF16).reshape(SLOTS, CHANS, INNER)
    cells_ref[:, :, LANES : LANES + INNER] = inner_ref[...] + halo


def shift_planes(columns_ref, cells_ref, slot):
    for plane in range(EDGE + 2):
        span = slice(plane * LANES, (plane + 1) * LANES)
        tile = cells_ref[slot, :, span]
        for tap in range(3):
            moved_tile = tile if tap == 1 else pltpu.roll(tile, (1 - tap) % LANES, 1)
            columns_ref[tap * CHANS : (tap + 1) * CHANS, span] = moved_tile


def windows(columns_ref):
    return jnp.concatenate([columns_ref[:, at * LANES : at * LANES + INNER] for at in range(3)], axis=0)


def stacked(weight):
    rows = []
    for mid in range(3):
        parts = [weight[:, (first * 3 + mid) * 96 : (first * 3 + mid + 1) * 96] for first in range(3)]
        rows.append(jnp.concatenate(parts, axis=1))
    return jnp.concatenate(rows, axis=0)


def turn_lanes(value, amount):
    return jnp.concatenate(
        [pltpu.roll(value[:, at * LANES : (at + 1) * LANES], amount % LANES, 1) for at in range(EDGE)], axis=1
    )


def convolve(columns_ref, weight):
    raw = dot(weight, windows(columns_ref))
    return (
        raw[CHANS : 2 * CHANS]
        + turn_lanes(raw[:CHANS], PITCH)
        + turn_lanes(raw[2 * CHANS :], -PITCH)
    )


def enter_kernel(place_ref, features_hbm, occupancy_hbm, inner_ref, mask_ref, pick_ref, even_ref, odd_ref, side_ref, end_ref,
                 features_ref, occupancy_ref, sems):
    loads = [
        pltpu.make_async_copy(occupancy_hbm, occupancy_ref, sems.at[0]),
        pltpu.make_async_copy(features_hbm, features_ref, sems.at[1]),
    ]
    for load in loads:
        load.start()
    pick_ref[...] = picking()
    matrix = widening()
    for load in loads:
        load.wait()
    mask = occupancy_ref[...].astype(F32).astype(BF16)
    for at, part in enumerate(spread(mask, matrix)):
        mask_ref[:, at * 256 : (at + 1) * 256] = part
    masked = jnp.concatenate(
        [features_ref[slot] * mask[slot : slot + 1, :] for slot in range(SLOTS)], axis=0
    )
    for at, part in enumerate(spread(masked, matrix)):
        inner_ref[:, :, at * 256 : (at + 1) * 256] = part.astype(BF16).reshape(SLOTS, CHANS, 256)
    emit_faces(place_ref, inner_ref, pick_ref, even_ref, odd_ref, side_ref, end_ref)


def turned(weight):
    taps = weight.astype(F32).T.astype(BF16)
    rows = []
    for mid in range(3):
        blocks = []
        for first in range(3):
            for last in range(3):
                tap = 26 - (first * 3 + mid) * 3 - last
                blocks.append(taps[tap * CHANS : (tap + 1) * CHANS])
        rows.append(jnp.concatenate(blocks, axis=1))
    return jnp.concatenate(rows, axis=0)


def prepare_kernel(cotangent_ref, mask_ref, first_ref, second_ref, out_ref, back_first_ref, back_second_ref, put_ref):
    put_ref[...] = putting()
    back_first_ref[...] = turned(first_ref[...])
    back_second_ref[...] = turned(second_ref[...])
    flat = cotangent_ref[...].reshape(SLOTS * CHANS, 512)
    for at, part in enumerate(spread(flat, widening())):
        span = slice(at * 256, (at + 1) * 256)
        for slot in range(SLOTS):
            out_ref[slot, :, span] = (
                part[slot * CHANS : (slot + 1) * CHANS] * mask_ref[slot : slot + 1, span]
            ).astype(BF16)


def first_kernel(neighbours_ref, place_ref, inner_ref, side_ref, end_ref, r0, r1, r2, r3, put_ref, pick_ref, weight_ref, mask_ref,
                 cells_ref, hidden_ref, even_ref, odd_ref, side_out_ref, end_out_ref, sheet_ref, columns_ref):
    build_cells(cells_ref, sheet_ref, inner_ref, side_ref, end_ref, (r0, r1, r2, r3), put_ref, neighbours_ref, place_ref)
    weight = stacked(weight_ref[...])
    for slot in range(SLOTS):
        buffer = columns_ref.at[slot % 2]
        shift_planes(buffer, cells_ref, slot)
        pre = convolve(buffer, weight)
        hidden_ref[slot] = (jnp.maximum(pre, 0.0) * mask_ref[slot : slot + 1, :]).astype(BF16)
    emit_faces(place_ref, hidden_ref, pick_ref, even_ref, odd_ref, side_out_ref, end_out_ref)


def pack_rows(inner, gather):
    return [dot(inner[:, at * 256 : (at + 1) * 256], gather) for at in range(4)]


def second_kernel(neighbours_ref, place_ref, inner_ref, side_ref, end_ref, r0, r1, r2, r3, put_ref, pick_ref, weight_ref,
                  mask_ref, skip_ref, cotangent_ref,
                  cells_ref, wide_ref, grad_ref, even_ref, odd_ref, side_out_ref, end_out_ref, sheet_ref, columns_ref):
    build_cells(cells_ref, sheet_ref, inner_ref, side_ref, end_ref, (r0, r1, r2, r3), put_ref, neighbours_ref, place_ref)
    weight = stacked(weight_ref[...])
    for slot in range(SLOTS):
        buffer = columns_ref.at[slot % 2]
        shift_planes(buffer, cells_ref, slot)
        pre = convolve(buffer, weight) + skip_ref[slot].astype(F32)
        wide_ref[slot] = (jnp.maximum(pre, 0.0) * mask_ref[slot : slot + 1, :]).astype(BF16)
        grad_ref[slot] = jnp.where(pre > 0.0, cotangent_ref[slot].astype(F32), 0.0).astype(BF16)
    emit_faces(place_ref, grad_ref, pick_ref, even_ref, odd_ref, side_out_ref, end_out_ref)


def pack_kernel(wide_ref, out_ref):
    flat = wide_ref[...].reshape(SLOTS * CHANS, INNER)
    for at, part in enumerate(pack_rows(flat, narrowing())):
        out_ref[:, :, at * LANES : (at + 1) * LANES] = part.astype(BF16).reshape(SLOTS, CHANS, LANES)


def third_kernel(neighbours_ref, place_ref, inner_ref, side_ref, end_ref, r0, r1, r2, r3, put_ref, pick_ref, weight_ref, mask_ref,
                 hidden_ref, grad_ref, even_ref, odd_ref, side_out_ref, end_out_ref, cells_ref, sheet_ref, columns_ref):
    build_cells(cells_ref, sheet_ref, inner_ref, side_ref, end_ref, (r0, r1, r2, r3), put_ref, neighbours_ref, place_ref)
    weight = weight_ref[...]
    for slot in range(SLOTS):
        buffer = columns_ref.at[slot % 2]
        shift_planes(buffer, cells_ref, slot)
        grad = convolve(buffer, weight) * mask_ref[slot : slot + 1, :]
        grad_ref[slot] = jnp.where(hidden_ref[slot].astype(F32) > 0.0, grad, 0.0).astype(BF16)
    emit_faces(place_ref, grad_ref, pick_ref, even_ref, odd_ref, side_out_ref, end_out_ref)


def last_kernel(neighbours_ref, place_ref, inner_ref, side_ref, end_ref, r0, r1, r2, r3, put_ref, weight_ref, mask_ref,
                grad_ref, out_ref, cells_ref, sheet_ref, columns_ref, wide_ref):
    build_cells(cells_ref, sheet_ref, inner_ref, side_ref, end_ref, (r0, r1, r2, r3), put_ref, neighbours_ref, place_ref)
    weight = weight_ref[...]
    for slot in range(SLOTS):
        buffer = columns_ref.at[slot % 2]
        shift_planes(buffer, cells_ref, slot)
        grad = convolve(buffer, weight) + grad_ref[slot].astype(F32)
        wide_ref[slot] = (grad * mask_ref[slot : slot + 1, :]).astype(BF16)
    flat = wide_ref[...].reshape(SLOTS * CHANS, INNER)
    for at, part in enumerate(pack_rows(flat, narrowing())):
        out_ref[:, :, at * LANES : (at + 1) * LANES] = part.astype(BF16).reshape(SLOTS, CHANS, LANES)


def weight_kernel(cells_ref, grad_ref, out_ref, columns_ref):
    total = jnp.zeros((9 * CHANS, 3 * CHANS), F32)
    for slot in range(SLOTS):
        buffer = columns_ref.at[slot % 2]
        shift_planes(buffer, cells_ref, slot)
        grad = grad_ref[slot]
        grads = jnp.concatenate([turn_lanes(grad, -PITCH), grad, turn_lanes(grad, PITCH)], axis=0)
        total = total + lax.dot_general(
            windows(buffer), grads, (((1,), (1,)), ((), ())), preferred_element_type=F32
        )
    flat = total.T
    for mid in range(3):
        for first in range(3):
            start = (first * 3 + mid) * 96
            out_ref[:, start : start + 96] = flat[mid * CHANS : (mid + 1) * CHANS, first * 96 : (first + 1) * 96]


def shape(dims, dtype=BF16):
    return jax.ShapeDtypeStruct(dims, dtype)


FIELD = (SLOTS, CHANS, 512)
INSIDE = (SLOTS, CHANS, INNER)
CELLS = (SLOTS, CHANS, WHOLE)
FACE = (SLOTS, CHANS, LANES)
FACES = [shape(FACE)] * 4
SCRATCH = [pltpu.VMEM((SLOTS * CHANS, 256), BF16), pltpu.VMEM((2, 3 * CHANS, WHOLE), BF16)]


def call(kernel, outs, scratch, scalars, flops, space=pltpu.VMEM):
    def run(*args):
        far = [at >= scalars and space == pltpu.HBM for at, a in enumerate(args)]
        args = [pltpu.with_memory_space_constraint(a, pltpu.HBM) if f else a for f, a in zip(far, args)]
        specs = [
            pl.BlockSpec(memory_space=pltpu.SMEM if at < scalars else pltpu.HBM if far[at] else pltpu.VMEM)
            for at in range(len(args))
        ]
        moved = sum(a.size * a.dtype.itemsize for a in args)
        moved += sum(math.prod(o.shape) * o.dtype.itemsize for o in outs)
        result = pl.pallas_call(
            kernel,
            out_shape=outs,
            in_specs=specs,
            out_specs=[pl.BlockSpec(memory_space=pltpu.VMEM)] * len(outs),
            scratch_shapes=scratch,
            compiler_params=pltpu.CompilerParams(vmem_limit_bytes=VMEM_LIMIT),
            cost_estimate=pl.CostEstimate(flops=flops, bytes_accessed=moved, transcendentals=0),
        )(*args)
        return result

    return run


AXES = ("tx", "ty")
RING_X, RING_Y, RING_Z = 4, 4, 8


def moved(value, to):
    pairs = []
    for source in range(RING_X * RING_Y * RING_Z * 2):
        row, col = divmod(source, RING_Z * 4)
        x, y_high = divmod(row, 2)
        y_low, rest = divmod(col, RING_Z * 2)
        z, core = divmod(rest, 2)
        x, y, z, core = to(x, y_high * 2 + y_low, z, core)
        x, y = x % RING_X, y % RING_Y
        pairs.append((source, ((x * 2 + y // 2) * 2 + y % 2) * RING_Z * 2 + z * 2 + core))
    return lax.ppermute(value, AXES, pairs)


def paired(value, axis, odd):
    count = lax.axis_size(axis)
    return lax.ppermute(
        value, axis, [(at, (at ^ 1) if not odd else (at + 1 if at % 2 else at - 1) % count) for at in range(count)]
    )


def other_core(value):
    return moved(value, lambda x, y, z, core: (x, y, z, core ^ 1))


ROUNDS = (
    (lambda x, y, z, c: (x, y, z ^ 3, c), lambda x, y, z, c: (x, y, z ^ 2, c), lambda x, y, z, c: (x, y, z ^ 1, c)),
    (lambda x, y, z, c: (x, y, z ^ 4, c),),
    (lambda x, y, z, c: (x, y + 2, z, c), lambda x, y, z, c: (x, y + 1, z, c), lambda x, y, z, c: (x, y - 1, z, c)),
    (lambda x, y, z, c: (x + 2, y, z, c), lambda x, y, z, c: (x + 1, y, z, c), lambda x, y, z, c: (x - 1, y, z, c)),
)
HOPS = (("tx", 1, "x_odd"), ("tx", 0, "x_even"), ("ty", 1, "y_odd"), ("ty", 0, "y_even"))


def hop(value, at):
    axis, odd, _ = HOPS[at]
    return paired(value, axis, odd)


def exchanged(odd, even, side):
    sent = (odd, even, side, side)
    return [hop(value, at) for at, value in enumerate(sent)]


CONV_FLOPS = 2 * 96 * 288 * WHOLE * SLOTS


RIDERS = ((), (0, 1, 2, 3), (), ())


def body(features, occupancy, neighbours, w_first, w_second, cotangent):
    row, col = lax.axis_index("tx"), lax.axis_index("ty")
    base = (row * lax.axis_size("ty") + col) * SLOTS
    place = jnp.stack([base, row % 2, col % 2]).astype(jnp.int32)
    place, late = lax.optimization_barrier((place, col % 2 == 1))
    enter_scratch = [
        pltpu.VMEM(FIELD, BF16),
        pltpu.VMEM((SLOTS, 512), jnp.int32),
        pltpu.SemaphoreType.DMA((2,)),
    ]
    x_inner, mask, pick, even, odd, side, end = call(
        enter_kernel,
        [shape(INSIDE), shape((SLOTS, INNER), F32), shape((INNER, 256))] + FACES,
        enter_scratch,
        1,
        2 * 192 * 512 * 1024,
        pltpu.HBM,
    )(place, features, occupancy)
    remote = exchanged(odd, even, side)
    cot_inner, back_first, back_second, put = call(
        prepare_kernel,
        [shape(INSIDE)] + [shape((3 * CHANS, 9 * CHANS))] * 2 + [shape((256, INNER))],
        [],
        0,
        2 * 192 * 512 * 256,
    )(cotangent, mask, w_first, w_second)
    x_cells, hidden, even, odd, hidden_side, hidden_end = call(
        first_kernel, [shape(CELLS), shape(INSIDE)] + FACES, SCRATCH, 2, CONV_FLOPS
    )(neighbours, place, x_inner, side, end, *remote, put, pick, w_first, mask)
    remote = exchanged(odd, even, hidden_side)
    hidden_cells, wide, grad_two, even, odd, grad_side, grad_end = call(
        second_kernel, [shape(CELLS), shape(INSIDE), shape(INSIDE)] + FACES, SCRATCH, 2, CONV_FLOPS
    )(neighbours, place, hidden, hidden_side, hidden_end, *remote, put, pick, w_second, mask, x_inner, cot_inner)
    remote = exchanged(odd, even, grad_side)
    weight_scratch = [SCRATCH[1]]
    weight_call = call(weight_kernel, [shape((CHANS, 27 * CHANS), F32)], weight_scratch, 0, CONV_FLOPS)
    (result,) = call(pack_kernel, [shape(FIELD)], [], 0, 2 * 192 * 1024 * 128)(wide)
    (term_second,) = weight_call(hidden_cells, grad_two)
    grad_one, even, odd, one_side, one_end = call(
        third_kernel, [shape(INSIDE)] + FACES, [pltpu.VMEM(CELLS, BF16)] + SCRATCH, 2, CONV_FLOPS
    )(neighbours, place, grad_two, grad_side, grad_end, *remote, put, pick, back_second, mask, hidden)
    (term_first,) = weight_call(x_cells, grad_one)
    sent = [odd, even, one_side, one_side]
    total = jnp.where(late, term_second, term_first) + other_core(jnp.where(late, term_first, term_second))
    remote = []
    for step, group in enumerate(ROUNDS):
        mine = total.astype(BF16)
        if step == len(ROUNDS) - 1:
            mine, remote = lax.optimization_barrier((mine, remote))
            (grad_features,) = call(
                last_kernel,
                [shape(FIELD)],
                [pltpu.VMEM(CELLS, BF16)] + SCRATCH + [pltpu.VMEM(INSIDE, BF16)],
                2,
                CONV_FLOPS,
            )(neighbours, place, grad_one, one_side, one_end, *remote, put, back_first, mask, grad_two)
        elif remote:
            mine, remote, result = lax.optimization_barrier((mine, remote, result))
        for at in RIDERS[step]:
            mine, value = lax.optimization_barrier((mine, sent[at]))
            remote.append(hop(value, at))
        parts = [mine.astype(F32)]
        for to in group:
            parts.append(moved(mine, to).astype(F32))
        total = parts[0] + parts[1]
        if len(parts) == 4:
            total = total + (parts[2] + parts[3])
        if step == len(ROUNDS) - 1:
            total, grad_features = lax.optimization_barrier((total, grad_features))
    scale = 1.0 / math.sqrt(SLOTS * lax.axis_size("tx") * lax.axis_size("ty") * EDGE**3)
    total = total * scale
    other = other_core(total)
    return (result, grad_features, jnp.where(late, other, total), jnp.where(late, total, other))


def solution(mesh):
    return jax.shard_map(
        body,
        mesh=mesh,
        in_specs=(
            P(("tx", "ty"), None, None),
            P(("tx", "ty"), None),
            P(("tx", "ty"), None),
            P(),
            P(),
            P(("tx", "ty"), None, None),
        ),
        out_specs=(P(("tx", "ty"), None, None), P(("tx", "ty"), None, None), P(), P()),
        check_vma=False,
    )
```

time: 106 us -> 89.9 us (0.85)
  the two profiles are of different devices: /device:TPU:1 before, /device:TPU:24 now
where the time goes in v3:
time: 89.9 us; the launch traced here: 88.4 us
  starting transfers between devices  51.1 us (57%)
  waiting for transfers between devices  19.5 us (22%)
  Pallas kernels  16.1 us (18%)
  other arithmetic  0.94 us (1%)
    ppermute x16, starting transfers between devices, paired(): lax.ppermute(value, axis, [(at, at ^ 1 if not odd else (at + 1 if at % 2...  31.4 us
    ppermute x12, starting transfers between devices, moved(): return lax.ppermute(value, AXES, pairs)  19.7 us
    pallas_call x9, Pallas kernels, run(): pl.pallas_call(kernel, out_shape=outs, in_specs=specs, out_specs=[pl.Bloc...  16.1 us
    ppermute x12, waiting for transfers between devices, moved(): return lax.ppermute(value, AXES, pairs)  11.3 us
    ppermute x16, waiting for transfers between devices, paired(): lax.ppermute(value, axis, [(at, at ^ 1 if not odd else (at + 1 if at % 2...  8.19 us
  transfers between devices with their start and end apart: 28, of which 12 were waited for; matrix products, arithmetic and copies ran while one was open for 0% of the time, Pallas kernels for 6%

profile of v3, /device:TPU:24, one launch (start us, length us, event | category | flops | bytes accessed | tf_op | source)
XLA Modules:
  0.0 88.4 jit_solution(1436264242431457123)
XLA Ops:
  0.7 0.1 pad_add_fusion.place_ref
  0.7 2.0 %shard_map.93 = (bf16[6,32,1024]{2,1,0:T(8,128)(2,1)S(1)}, f32[6,1024]{1,0:T(8,128)S(1)}, bf16[1024,256]{1,0:T(8,128)(2,1)S(1)}, bf16[6,32,128]{2,1,0:T(8,128)(2...) custom-call(s32[3]{0:T(128)S(1)} %pad_add_fusion.place_ref, ...), custom_call_target="tpu_custom_call" | custom-call | flops 201326592 | bytes 1347596 | tf_op jit(solution)/shard_map/pallas_call | solution.py:310
  2.7 2.2 %collective-permute-start = (bf16[6,32,128]{2,1,0:T(8,128)(2,1)S(1)}, bf16[6,32,128]{2,1,0:T(8,128)(2,1)S(1)}, u32[]{:S(2)}, u32[]{:S(2)}) collective-permute-start(bf16[6,32,128]{2,1,0:T(8,128)(2,1)S(1)} %get-tuple-element.61), channel_id=1, source_target_pairs={{0,224},{32,64},{64,32},{96,128},{128,96},{160,192},{192,160},{224... | collective-permute-start | bytes 147464 | tf_op jit(solution)/shard_map/ppermute | solution.py:343
  5.0 3.6 %collective-permute-start.1 = (bf16[6,32,128]{2,1,0:T(8,128)(2,1)S(1)}, bf16[6,32,128]{2,1,0:T(8,128)(2,1)S(1)}, u32[]{:S(2)}, u32[]{:S(2)}) collective-permute-start(bf16[6,32,128]{2,1,0:T(8,128)(2,1)S(1)} %get-tuple-element.62), channel_id=1, source_target_pairs={{0,32},{32,0},{64,96},{96,64},{128,160},{160,128},{192,224},{224,1... | collective-permute-start | bytes 147464 | tf_op jit(solution)/shard_map/ppermute | solution.py:343
  8.6 0.0 collective-permute-start.3
  8.6 6.1 %collective-permute-start.2 = (bf16[6,32,128]{2,1,0:T(8,128)(2,1)S(1)}, bf16[6,32,128]{2,1,0:T(8,128)(2,1)S(1)}, u32[]{:S(2)}, u32[]{:S(2)}) collective-permute-start(bf16[6,32,128]{2,1,0:T(8,128)(2,1)S(1)} %get-tuple-element.59.side_ref), channel_id=1, source_target_pairs={{0,31},{1,2},{2,1},{3,4},{4,3},{5,6},{6,5},{7,8},{8,7},{9,10},{10,... | collective-permute-start | bytes 147464 | tf_op jit(solution)/shard_map/ppermute | solution.py:343
  14.7 0.6 shard_map.94
  15.3 0.0 copy-start.3
  15.4 1.1 %collective-permute-done.2.r2 = bf16[6,32,128]{2,1,0:T(8,128)(2,1)S(1)} collective-permute-done((bf16[6,32,128]{2,1,0:T(8,128)(2,1)S(1)}, bf16[6,32,128]{2,1,0:T(8,128)(2,1)S(1)}, u32[]{:S(2)}, u32[]{:S(2)}) %collective-permute-start.2) | collective-permute-done | bytes 49184 | tf_op jit(solution)/shard_map/ppermute | solution.py:343
  16.5 2.4 %shard_map.95 = (bf16[6,32,1280]{2,1,0:T(8,128)(2,1)S(1)}, bf16[6,32,1024]{2,1,0:T(8,128)(2,1)S(1)}, bf16[6,32,128]{2,1,0:T(8,128)(2,1)S(1)}, bf16[6,32,128]{2,1...) custom-call(s32[6,6]{1,0:T(8,128)S(1)} %copy-done.3, s32[3]{0:T(128)S(1)} %pad_add_fusion.place_ref, ...), custom_call_target="tpu_custom_call" | custom-call | flops 424673280 | bytes 2898076 | tf_op jit(solution)/shard_map/pallas_call | solution.py:310
  18.9 0.6 collective-permute-start.4
  19.5 3.3 %collective-permute-start.5 = (bf16[6,32,128]{2,1,0:T(8,128)(2,1)S(1)}, bf16[6,32,128]{2,1,0:T(8,128)(2,1)S(1)}, u32[]{:S(2)}, u32[]{:S(2)}) collective-permute-start(bf16[6,32,128]{2,1,0:T(8,128)(2,1)S(1)} %get-tuple-element.70), channel_id=1, source_target_pairs={{0,32},{32,0},{64,96},{96,64},{128,160},{160,128},{192,224},{224,1... | collective-permute-start | bytes 147464 | tf_op jit(solution)/shard_map/ppermute | solution.py:343
  22.7 3.3 %collective-permute-start.6 = (bf16[6,32,128]{2,1,0:T(8,128)(2,1)S(1)}, bf16[6,32,128]{2,1,0:T(8,128)(2,1)S(1)}, u32[]{:S(2)}, u32[]{:S(2)}) collective-permute-start(bf16[6,32,128]{2,1,0:T(8,128)(2,1)S(1)} %get-tuple-element.67.side_ref), channel_id=1, source_target_pairs={{0,31},{1,2},{2,1},{3,4},{4,3},{5,6},{6,5},{7,8},{8,7},{9,10},{10,... | collective-permute-start | bytes 147464 | tf_op jit(solution)/shard_map/ppermute | solution.py:343
  26.0 2.3 %collective-permute-done.6.r2 = bf16[6,32,128]{2,1,0:T(8,128)(2,1)S(1)} collective-permute-done((bf16[6,32,128]{2,1,0:T(8,128)(2,1)S(1)}, bf16[6,32,128]{2,1,0:T(8,128)(2,1)S(1)}, u32[]{:S(2)}, u32[]{:S(2)}) %collective-permute-start.6) | collective-permute-done | bytes 49184 | tf_op jit(solution)/shard_map/ppermute | solution.py:343
  28.4 2.3 %shard_map.96 = (bf16[6,32,1280]{2,1,0:T(8,128)(2,1)S(1)}, bf16[6,32,1024]{2,1,0:T(8,128)(2,1)S(1)}, bf16[6,32,1024]{2,1,0:T(8,128)(2,1)S(1)}, bf16[6,32,128]{2,...) custom-call(s32[6,6]{1,0:T(8,128)S(1)} %copy-done.3, ...), custom_call_target="tpu_custom_call" | custom-call | flops 424673280 | bytes 4077724 | tf_op jit(solution)/shard_map/pallas_call | solution.py:310
  30.7 1.1 %collective-permute-start.8 = (bf16[6,32,128]{2,1,0:T(8,128)(2,1)S(1)}, bf16[6,32,128]{2,1,0:T(8,128)(2,1)S(1)}, u32[]{:S(2)}, u32[]{:S(2)}) collective-permute-start(bf16[6,32,128]{2,1,0:T(8,128)(2,1)S(1)} %get-tuple-element.77), channel_id=1, source_target_pairs={{0,224},{32,64},{64,32},{96,128},{128,96},{160,192},{192,160},{224... | collective-permute-start | bytes 147464 | tf_op jit(solution)/shard_map/ppermute | solution.py:343
  31.7 2.5 %collective-permute-start.9 = (bf16[6,32,128]{2,1,0:T(8,128)(2,1)S(1)}, bf16[6,32,128]{2,1,0:T(8,128)(2,1)S(1)}, u32[]{:S(2)}, u32[]{:S(2)}) collective-permute-start(bf16[6,32,128]{2,1,0:T(8,128)(2,1)S(1)} %get-tuple-element.78), channel_id=1, source_target_pairs={{0,32},{32,0},{64,96},{96,64},{128,160},{160,128},{192,224},{224,1... | collective-permute-start | bytes 147464 | tf_op jit(solution)/shard_map/ppermute | solution.py:343
  34.2 2.7 %collective-permute-start.10 = (bf16[6,32,128]{2,1,0:T(8,128)(2,1)S(1)}, bf16[6,32,128]{2,1,0:T(8,128)(2,1)S(1)}, u32[]{:S(2)}, u32[]{:S(2)}) collective-permute-start(bf16[6,32,128]{2,1,0:T(8,128)(2,1)S(1)} %get-tuple-element.75.side_ref), channel_id=1, source_target_pairs={{0,31},{1,2},{2,1},{3,4},{4,3},{5,6},{6,5},{7,8},{8,7},{9,10},{10,... | collective-permute-start | bytes 147464 | tf_op jit(solution)/shard_map/ppermute | solution.py:343
  36.9 1.4 %shard_map.97 = f32[32,864]{1,0:T(8,128)S(1)} custom-call(bf16[6,32,1280]{2,1,0:T(8,128)(2,1)S(1)} %get-tuple-element.72.cells_ref, bf16[6,32,1024]{2,1,0:T(8,128)(2,1)S(1)} %get-tuple-element.73.grad_ref.inner_ref), custom_call_target="tpu_custom_call" | custom-call | flops 424673280 | bytes 995328 | tf_op jit(solution)/shard_map/pallas_call | solution.py:310
  38.4 1.5 %collective-permute-done.10.r2 = bf16[6,32,128]{2,1,0:T(8,128)(2,1)S(1)} collective-permute-done((bf16[6,32,128]{2,1,0:T(8,128)(2,1)S(1)}, bf16[6,32,128]{2,1,0:T(8,128)(2,1)S(1)}, u32[]{:S(2)}, u32[]{:S(2)}) %collective-permute-start.10) | collective-permute-done | bytes 49184 | tf_op jit(solution)/shard_map/ppermute | solution.py:343
  39.8 2.3 %shard_map.98 = (bf16[6,32,1024]{2,1,0:T(8,128)(2,1)S(1)}, bf16[6,32,128]{2,1,0:T(8,128)(2,1)S(1)}, bf16[6,32,128]{2,1,0:T(8,128)(2,1)S(1)}, bf16[6,32,128]{2,1,0:T(8,128)(2,1)S(1)}, bf16[6,32,128]{2,1,0:T(8,128)(2,1)S(1)}) custom-call(s32[6,6]{1,0:T(8,128)S(1)} %copy-done.3, s32[3]{0:T(128)S(1)} %pad_add_fusion.place_ref, ...), custom_call_target="tpu_custom_call" | custom-call | flops 424673280 | bytes 2799772 | tf_op jit(solution)/shard_map/pallas_call | solution.py:310
  42.1 1.4 %shard_map.99 = f32[32,864]{1,0:T(8,128)S(1)} custom-call(bf16[6,32,1280]{2,1,0:T(8,128)(2,1)S(1)} %get-tuple-element.74.cells_ref, bf16[6,32,1024]{2,1,0:T(8,128)(2,1)S(1)} %get-tuple-element.80.grad_ref.inner_ref), custom_call_target="tpu_custom_call" | custom-call | flops 424673280 | bytes 995328 | tf_op jit(solution)/shard_map/pallas_call | solution.py:310
  43.6 0.1 collective-permute-start.12
  43.7 1.3 %collective-permute-done.12 = f32[32,864]{1,0:T(8,128)S(1)} collective-permute-done((f32[32,864]{1,0:T(8,128)S(1)}, f32[32,864]{1,0:T(8,128)S(1)}, u32[]{:S(2)}, u32[]{:S(2)}) %collective-permute-start.12) | collective-permute-done | bytes 110624 | tf_op jit(solution)/shard_map/ppermute | solution.py:338
  45.0 0.1 collective-permute-start.15
  45.1 0.5 collective-permute-start.14
  45.6 3.8 %collective-permute-start.13 = (bf16[32,864]{1,0:T(8,128)(2,1)S(1)}, bf16[32,864]{1,0:T(8,128)(2,1)S(1)}, u32[]{:S(2)}, u32[]{:S(2)}) collective-permute-start(bf16[32,864]{1,0:T(8,128)(2,1)S(1)} %add_convert_fusion.3), channel_id=1, source_target_pairs={{0,6},{1,7},{2,4},{3,5},{4,2},{5,3},{6,0},{7,1},{8,14},{9,15},{10,... | collective-permute-start | bytes 165896 | tf_op jit(solution)/shard_map/ppermute | solution.py:338
  49.5 0.6 collective-permute-done.15
  50.1 3.1 %collective-permute-done.14 = bf16[32,864]{1,0:T(8,128)(2,1)S(1)} collective-permute-done((bf16[32,864]{1,0:T(8,128)(2,1)S(1)}, bf16[32,864]{1,0:T(8,128)(2,1)S(1)}, u32[]{:S(2)}, u32[]{:S(2)}) %collective-permute-start.14) | collective-permute-done | bytes 55328 | tf_op jit(solution)/shard_map/ppermute | solution.py:338
  53.2 4.4 %collective-permute-start.16 = (bf16[32,864]{1,0:T(8,128)(2,1)S(1)}, bf16[32,864]{1,0:T(8,128)(2,1)S(1)}, u32[]{:S(2)}, u32[]{:S(2)}) collective-permute-start(bf16[32,864]{1,0:T(8,128)(2,1)S(1)} %add_convert_fusion.2), channel_id=1, source_target_pairs={{0,8},{1,9},{2,10},{3,11},{4,12},{5,13},{6,14},{7,15},{8,0},{9,1},... | collective-permute-start | bytes 165896 | tf_op jit(solution)/shard_map/ppermute | solution.py:338
  57.6 0.9 %shard_map.100 = bf16[6,32,512]{2,1,0:T(8,128)(2,1)} custom-call(bf16[6,32,1024]{2,1,0:T(8,128)(2,1)S(1)} %get-tuple-element.92.wide_ref), custom_call_target="tpu_custom_call" | custom-call | flops 50331648 | bytes 589824 | tf_op jit(solution)/shard_map/pallas_call | solution.py:310
  58.6 1.4 %collective-permute-start.19 = (bf16[6,32,128]{2,1,0:T(8,128)(2,1)S(1)}, bf16[6,32,128]{2,1,0:T(8,128)(2,1)S(1)}, u32[]{:S(2)}, u32[]{:S(2)}) collective-permute-start(bf16[6,32,128]{2,1,0:T(8,128)(2,1)S(1)} %get-tuple-element.91.side_ref), channel_id=1, source_target_pairs={{0,31},{1,2},{2,1},{3,4},{4,3},{5,6},{6,5},{7,8},{8,7},{9,10},{10,... | collective-permute-start | bytes 147464 | tf_op jit(solution)/shard_map/ppermute | solution.py:343
  60.0 1.4 %collective-permute-start.18 = (bf16[6,32,128]{2,1,0:T(8,128)(2,1)S(1)}, bf16[6,32,128]{2,1,0:T(8,128)(2,1)S(1)}, u32[]{:S(2)}, u32[]{:S(2)}) collective-permute-start(bf16[6,32,128]{2,1,0:T(8,128)(2,1)S(1)} %get-tuple-element.89), channel_id=1, source_target_pairs={{0,32},{32,0},{64,96},{96,64},{128,160},{160,128},{192,224},{224,1... | collective-permute-start | bytes 147464 | tf_op jit(solution)/shard_map/ppermute | solution.py:343
  61.4 3.2 %collective-permute-start.17 = (bf16[6,32,128]{2,1,0:T(8,128)(2,1)S(1)}, bf16[6,32,128]{2,1,0:T(8,128)(2,1)S(1)}, u32[]{:S(2)}, u32[]{:S(2)}) collective-permute-start(bf16[6,32,128]{2,1,0:T(8,128)(2,1)S(1)} %get-tuple-element.88), channel_id=1, source_target_pairs={{0,224},{32,64},{64,32},{96,128},{128,96},{160,192},{192,160},{224... | collective-permute-start | bytes 147464 | tf_op jit(solution)/shard_map/ppermute | solution.py:343
  64.6 1.5 %collective-permute-done.18.r1 = bf16[6,32,128]{2,1,0:T(8,128)(2,1)S(1)} collective-permute-done((bf16[6,32,128]{2,1,0:T(8,128)(2,1)S(1)}, bf16[6,32,128]{2,1,0:T(8,128)(2,1)S(1)}, u32[]{:S(2)}, u32[]{:S(2)}) %collective-permute-start.18) | collective-permute-done | bytes 49184 | tf_op jit(solution)/shard_map/ppermute | solution.py:343
  66.2 1.7 %collective-permute-done.17.r0 = bf16[6,32,128]{2,1,0:T(8,128)(2,1)S(1)} collective-permute-done((bf16[6,32,128]{2,1,0:T(8,128)(2,1)S(1)}, bf16[6,32,128]{2,1,0:T(8,128)(2,1)S(1)}, u32[]{:S(2)}, u32[]{:S(2)}) %collective-permute-start.17) | collective-permute-done | bytes 49184 | tf_op jit(solution)/shard_map/ppermute | solution.py:343
  67.9 3.3 %collective-permute-start.22 = (bf16[32,864]{1,0:T(8,128)(2,1)S(1)}, bf16[32,864]{1,0:T(8,128)(2,1)S(1)}, u32[]{:S(2)}, u32[]{:S(2)}) collective-permute-start(bf16[32,864]{1,0:T(8,128)(2,1)S(1)} %add_convert_fusion.1), channel_id=1, source_target_pairs={{0,16},{1,17},{2,18},{3,19},{4,20},{5,21},{6,22},{7,23},{8,24},{9,... | collective-permute-start | bytes 165896 | tf_op jit(solution)/shard_map/ppermute | solution.py:338
  71.2 2.1 %collective-permute-start.21 = (bf16[32,864]{1,0:T(8,128)(2,1)S(1)}, bf16[32,864]{1,0:T(8,128)(2,1)S(1)}, u32[]{:S(2)}, u32[]{:S(2)}) collective-permute-start(bf16[32,864]{1,0:T(8,128)(2,1)S(1)} %add_convert_fusion.1), channel_id=1, source_target_pairs={{0,32},{1,33},{2,34},{3,35},{4,36},{5,37},{6,38},{7,39},{8,40},{9,... | collective-permute-start | bytes 165896 | tf_op jit(solution)/shard_map/ppermute | solution.py:338
  73.3 0.5 collective-permute-done.23
  73.8 3.0 %collective-permute-done.21 = bf16[32,864]{1,0:T(8,128)(2,1)S(1)} collective-permute-done((bf16[32,864]{1,0:T(8,128)(2,1)S(1)}, bf16[32,864]{1,0:T(8,128)(2,1)S(1)}, u32[]{:S(2)}, u32[]{:S(2)}) %collective-permute-start.21) | collective-permute-done | bytes 55328 | tf_op jit(solution)/shard_map/ppermute | solution.py:338
  76.9 3.4 %collective-permute-start.26 = (bf16[32,864]{1,0:T(8,128)(2,1)S(1)}, bf16[32,864]{1,0:T(8,128)(2,1)S(1)}, u32[]{:S(2)}, u32[]{:S(2)}) collective-permute-start(bf16[32,864]{1,0:T(8,128)(2,1)S(1)} %add_convert_fusion), channel_id=1, source_target_pairs={{0,192},{1,193},{2,194},{3,195},{4,196},{5,197},{6,198},{7,199},{8... | collective-permute-start | bytes 165896 | tf_op jit(solution)/shard_map/ppermute | solution.py:338
  80.3 0.0 collective-permute-start.25
  80.3 1.8 %collective-permute-start.24 = (bf16[32,864]{1,0:T(8,128)(2,1)S(1)}, bf16[32,864]{1,0:T(8,128)(2,1)S(1)}, u32[]{:S(2)}, u32[]{:S(2)}) collective-permute-start(bf16[32,864]{1,0:T(8,128)(2,1)S(1)} %add_convert_fusion), channel_id=1, source_target_pairs={{0,128},{1,129},{2,130},{3,131},{4,132},{5,133},{6,134},{7,135},{8... | collective-permute-start | bytes 165896 | tf_op jit(solution)/shard_map/ppermute | solution.py:338
  82.0 2.8 %shard_map.101 = bf16[6,32,512]{2,1,0:T(8,128)(2,1)} custom-call(s32[6,6]{1,0:T(8,128)S(1)} %copy-done.3, s32[3]{0:T(128)S(1)} %pad_add_fusion.place_ref, bf16[6,32,1024]{2,1,0:T(8,128)(2,1)S(1)} %get-tuple-element.80.grad_ref.inner_ref, bf16[6,32,128]{2,1,0:T(8,128)(2,1)S(1)} %get-tuple-element.91.side_ref, ...), custom_call_target="tpu_custom_call" | custom-call | flops 424673280 | bytes 1882268 | tf_op jit(solution)/shard_map/pallas_call | solution.py:310
  84.8 1.4 %collective-permute-done.25 = bf16[32,864]{1,0:T(8,128)(2,1)S(1)} collective-permute-done((bf16[32,864]{1,0:T(8,128)(2,1)S(1)}, bf16[32,864]{1,0:T(8,128)(2,1)S(1)}, u32[]{:S(2)}, u32[]{:S(2)}) %collective-permute-start.25) | collective-permute-done | bytes 55328 | tf_op jit(solution)/shard_map/ppermute | solution.py:338
  86.3 0.1 collective-permute-start.27
  86.4 1.3 %collective-permute-done.27 = f32[32,864]{1,0:T(8,128)S(1)} collective-permute-done((f32[32,864]{1,0:T(8,128)S(1)}, f32[32,864]{1,0:T(8,128)S(1)}, u32[]{:S(2)}, u32[]{:S(2)}) %collective-permute-start.27) | collective-permute-done | bytes 110624 | tf_op jit(solution)/shard_map/ppermute | solution.py:338
  87.7 0.7 broadcast_select_fusion
  (34 shorter events, 0.2 us)
Async XLA Ops:
  0.7 14.0 %copy-start = (bf16[32,864]{1,0:T(8,128)(2,1)S(1)}, bf16[32,864]{1,0:T(8,128)(2,1)}, u32[]{:S(2)}) copy-start(bf16[32,864]{1,0:T(8,128)(2,1)} %weight_ref.2) | copy-start | bytes 165892
  0.7 14.0 %copy-start.1 = (bf16[32,864]{1,0:T(8,128)(2,1)S(1)}, bf16[32,864]{1,0:T(8,128)(2,1)}, u32[]{:S(2)}) copy-start(bf16[32,864]{1,0:T(8,128)(2,1)} %weight_ref.3) | copy-start | bytes 165892
  0.7 14.0 %copy-start.2 = (bf16[6,32,512]{2,1,0:T(8,128)(2,1)S(1)}, bf16[6,32,512]{2,1,0:T(8,128)(2,1)}, u32[]{:S(2)}) copy-start(bf16[6,32,512]{2,1,0:T(8,128)(2,1)} %cotangent_ref.1) | copy-start | bytes 589828
  2.7 12.6 %collective-permute-start = (bf16[6,32,128]{2,1,0:T(8,128)(2,1)S(1)}, bf16[6,32,128]{2,1,0:T(8,128)(2,1)S(1)}, u32[]{:S(2)}, u32[]{:S(2)}) collective-permute-start(bf16[6,32,128]{2,1,0:T(8,128)(2,1)S(1)} %get-tuple-element.61), channel_id=1, source_target_pairs={{0,224},{32,64},{64,32},{96,128},{128,96},{160,192},{192,160},{224... | collective-permute-start | bytes 147464 | tf_op jit(solution)/shard_map/ppermute | solution.py:343
  5.0 10.3 %collective-permute-start.1 = (bf16[6,32,128]{2,1,0:T(8,128)(2,1)S(1)}, bf16[6,32,128]{2,1,0:T(8,128)(2,1)S(1)}, u32[]{:S(2)}, u32[]{:S(2)}) collective-permute-start(bf16[6,32,128]{2,1,0:T(8,128)(2,1)S(1)} %get-tuple-element.62), channel_id=1, source_target_pairs={{0,32},{32,0},{64,96},{96,64},{128,160},{160,128},{192,224},{224,1... | collective-permute-start | bytes 147464 | tf_op jit(solution)/shard_map/ppermute | solution.py:343
  8.6 6.8 %collective-permute-start.3 = (bf16[6,32,128]{2,1,0:T(8,128)(2,1)S(1)}, bf16[6,32,128]{2,1,0:T(8,128)(2,1)S(1)}, u32[]{:S(2)}, u32[]{:S(2)}) collective-permute-start(bf16[6,32,128]{2,1,0:T(8,128)(2,1)S(1)} %get-tuple-element.59.side_ref), channel_id=1, source_target_pairs={{0,1},{1,0},{2,3},{3,2},{4,5},{5,4},{6,7},{7,6},{8,9},{9,8},{10,11... | collective-permute-start | bytes 147464 | tf_op jit(solution)/shard_map/ppermute | solution.py:343
  8.6 7.9 %collective-permute-start.2 = (bf16[6,32,128]{2,1,0:T(8,128)(2,1)S(1)}, bf16[6,32,128]{2,1,0:T(8,128)(2,1)S(1)}, u32[]{:S(2)}, u32[]{:S(2)}) collective-permute-start(bf16[6,32,128]{2,1,0:T(8,128)(2,1)S(1)} %get-tuple-element.59.side_ref), channel_id=1, source_target_pairs={{0,31},{1,2},{2,1},{3,4},{4,3},{5,6},{6,5},{7,8},{8,7},{9,10},{10,... | collective-permute-start | bytes 147464 | tf_op jit(solution)/shard_map/ppermute | solution.py:343
  15.3 1.2 %copy-start.3 = (s32[6,6]{1,0:T(8,128)S(1)}, s32[6,6]{1,0:T(8,128)}, u32[]{:S(2)}) copy-start(s32[6,6]{1,0:T(8,128)} %neighbours_ref.7) | copy-start | bytes 436
  18.9 7.2 %collective-permute-start.4 = (bf16[6,32,128]{2,1,0:T(8,128)(2,1)S(1)}, bf16[6,32,128]{2,1,0:T(8,128)(2,1)S(1)}, u32[]{:S(2)}, u32[]{:S(2)}) collective-permute-start(bf16[6,32,128]{2,1,0:T(8,128)(2,1)S(1)} %get-tuple-element.69), channel_id=1, source_target_pairs={{0,224},{32,64},{64,32},{96,128},{128,96},{160,192},{192,160},{224... | collective-permute-start | bytes 147464 | tf_op jit(solution)/shard_map/ppermute | solution.py:343
  19.5 6.6 %collective-permute-start.5 = (bf16[6,32,128]{2,1,0:T(8,128)(2,1)S(1)}, bf16[6,32,128]{2,1,0:T(8,128)(2,1)S(1)}, u32[]{:S(2)}, u32[]{:S(2)}) collective-permute-start(bf16[6,32,128]{2,1,0:T(8,128)(2,1)S(1)} %get-tuple-element.70), channel_id=1, source_target_pairs={{0,32},{32,0},{64,96},{96,64},{128,160},{160,128},{192,224},{224,1... | collective-permute-start | bytes 147464 | tf_op jit(solution)/shard_map/ppermute | solution.py:343
  22.7 3.3 %collective-permute-start.7 = (bf16[6,32,128]{2,1,0:T(8,128)(2,1)S(1)}, bf16[6,32,128]{2,1,0:T(8,128)(2,1)S(1)}, u32[]{:S(2)}, u32[]{:S(2)}) collective-permute-start(bf16[6,32,128]{2,1,0:T(8,128)(2,1)S(1)} %get-tuple-element.67.side_ref), channel_id=1, source_target_pairs={{0,1},{1,0},{2,3},{3,2},{4,5},{5,4},{6,7},{7,6},{8,9},{9,8},{10,11... | collective-permute-start | bytes 147464 | tf_op jit(solution)/shard_map/ppermute | solution.py:343
  22.7 5.6 %collective-permute-start.6 = (bf16[6,32,128]{2,1,0:T(8,128)(2,1)S(1)}, bf16[6,32,128]{2,1,0:T(8,128)(2,1)S(1)}, u32[]{:S(2)}, u32[]{:S(2)}) collective-permute-start(bf16[6,32,128]{2,1,0:T(8,128)(2,1)S(1)} %get-tuple-element.67.side_ref), channel_id=1, source_target_pairs={{0,31},{1,2},{2,1},{3,4},{4,3},{5,6},{6,5},{7,8},{8,7},{9,10},{10,... | collective-permute-start | bytes 147464 | tf_op jit(solution)/shard_map/ppermute | solution.py:343
  30.7 7.7 %collective-permute-start.8 = (bf16[6,32,128]{2,1,0:T(8,128)(2,1)S(1)}, bf16[6,32,128]{2,1,0:T(8,128)(2,1)S(1)}, u32[]{:S(2)}, u32[]{:S(2)}) collective-permute-start(bf16[6,32,128]{2,1,0:T(8,128)(2,1)S(1)} %get-tuple-element.77), channel_id=1, source_target_pairs={{0,224},{32,64},{64,32},{96,128},{128,96},{160,192},{192,160},{224... | collective-permute-start | bytes 147464 | tf_op jit(solution)/shard_map/ppermute | solution.py:343
  31.7 6.6 %collective-permute-start.9 = (bf16[6,32,128]{2,1,0:T(8,128)(2,1)S(1)}, bf16[6,32,128]{2,1,0:T(8,128)(2,1)S(1)}, u32[]{:S(2)}, u32[]{:S(2)}) collective-permute-start(bf16[6,32,128]{2,1,0:T(8,128)(2,1)S(1)} %get-tuple-element.78), channel_id=1, source_target_pairs={{0,32},{32,0},{64,96},{96,64},{128,160},{160,128},{192,224},{224,1... | collective-permute-start | bytes 147464 | tf_op jit(solution)/shard_map/ppermute | solution.py:343
  34.2 4.2 %collective-permute-start.11 = (bf16[6,32,128]{2,1,0:T(8,128)(2,1)S(1)}, bf16[6,32,128]{2,1,0:T(8,128)(2,1)S(1)}, u32[]{:S(2)}, u32[]{:S(2)}) collective-permute-start(bf16[6,32,128]{2,1,0:T(8,128)(2,1)S(1)} %get-tuple-element.75.side_ref), channel_id=1, source_target_pairs={{0,1},{1,0},{2,3},{3,2},{4,5},{5,4},{6,7},{7,6},{8,9},{9,8},{10,11... | collective-permute-start | bytes 147464 | tf_op jit(solution)/shard_map/ppermute | solution.py:343
  34.2 5.6 %collective-permute-start.10 = (bf16[6,32,128]{2,1,0:T(8,128)(2,1)S(1)}, bf16[6,32,128]{2,1,0:T(8,128)(2,1)S(1)}, u32[]{:S(2)}, u32[]{:S(2)}) collective-permute-start(bf16[6,32,128]{2,1,0:T(8,128)(2,1)S(1)} %get-tuple-element.75.side_ref), channel_id=1, source_target_pairs={{0,31},{1,2},{2,1},{3,4},{4,3},{5,6},{6,5},{7,8},{8,7},{9,10},{10,... | collective-permute-start | bytes 147464 | tf_op jit(solution)/shard_map/ppermute | solution.py:343
  43.6 1.4 %collective-permute-start.12 = (f32[32,864]{1,0:T(8,128)S(1)}, f32[32,864]{1,0:T(8,128)S(1)}, u32[]{:S(2)}, u32[]{:S(2)}) collective-permute-start(f32[32,864]{1,0:T(8,128)S(1)} %broadcast_select_fusion.2), channel_id=1, source_target_pairs={{0,1},{1,0},{2,3},{3,2},{4,5},{5,4},{6,7},{7,6},{8,9},{9,8},{10,11... | collective-permute-start | bytes 331784 | tf_op jit(solution)/shard_map/ppermute | solution.py:338
  45.0 5.1 %collective-permute-start.15 = (bf16[32,864]{1,0:T(8,128)(2,1)S(1)}, bf16[32,864]{1,0:T(8,128)(2,1)S(1)}, u32[]{:S(2)}, u32[]{:S(2)}) collective-permute-start(bf16[32,864]{1,0:T(8,128)(2,1)S(1)} %add_convert_fusion.3), channel_id=1, source_target_pairs={{0,2},{1,3},{2,0},{3,1},{4,6},{5,7},{6,4},{7,5},{8,10},{9,11},{10,... | collective-permute-start | bytes 165896 | tf_op jit(solution)/shard_map/ppermute | solution.py:338
  45.1 8.0 %collective-permute-start.14 = (bf16[32,864]{1,0:T(8,128)(2,1)S(1)}, bf16[32,864]{1,0:T(8,128)(2,1)S(1)}, u32[]{:S(2)}, u32[]{:S(2)}) collective-permute-start(bf16[32,864]{1,0:T(8,128)(2,1)S(1)} %add_convert_fusion.3), channel_id=1, source_target_pairs={{0,4},{1,5},{2,6},{3,7},{4,0},{5,1},{6,2},{7,3},{8,12},{9,13},{10,... | collective-permute-start | bytes 165896 | tf_op jit(solution)/shard_map/ppermute | solution.py:338
  45.6 7.5 %collective-permute-start.13 = (bf16[32,864]{1,0:T(8,128)(2,1)S(1)}, bf16[32,864]{1,0:T(8,128)(2,1)S(1)}, u32[]{:S(2)}, u32[]{:S(2)}) collective-permute-start(bf16[32,864]{1,0:T(8,128)(2,1)S(1)} %add_convert_fusion.3), channel_id=1, source_target_pairs={{0,6},{1,7},{2,4},{3,5},{4,2},{5,3},{6,0},{7,1},{8,14},{9,15},{10,... | collective-permute-start | bytes 165896 | tf_op jit(solution)/shard_map/ppermute | solution.py:338
  53.2 11.4 %collective-permute-start.16 = (bf16[32,864]{1,0:T(8,128)(2,1)S(1)}, bf16[32,864]{1,0:T(8,128)(2,1)S(1)}, u32[]{:S(2)}, u32[]{:S(2)}) collective-permute-start(bf16[32,864]{1,0:T(8,128)(2,1)S(1)} %add_convert_fusion.2), channel_id=1, source_target_pairs={{0,8},{1,9},{2,10},{3,11},{4,12},{5,13},{6,14},{7,15},{8,0},{9,1},... | collective-permute-start | bytes 165896 | tf_op jit(solution)/shard_map/ppermute | solution.py:338
  58.6 6.0 %collective-permute-start.20 = (bf16[6,32,128]{2,1,0:T(8,128)(2,1)S(1)}, bf16[6,32,128]{2,1,0:T(8,128)(2,1)S(1)}, u32[]{:S(2)}, u32[]{:S(2)}) collective-permute-start(bf16[6,32,128]{2,1,0:T(8,128)(2,1)S(1)} %get-tuple-element.91.side_ref), channel_id=1, source_target_pairs={{0,1},{1,0},{2,3},{3,2},{4,5},{5,4},{6,7},{7,6},{8,9},{9,8},{10,11... | collective-permute-start | bytes 147464 | tf_op jit(solution)/shard_map/ppermute | solution.py:343
  58.6 6.0 %collective-permute-start.19 = (bf16[6,32,128]{2,1,0:T(8,128)(2,1)S(1)}, bf16[6,32,128]{2,1,0:T(8,128)(2,1)S(1)}, u32[]{:S(2)}, u32[]{:S(2)}) collective-permute-start(bf16[6,32,128]{2,1,0:T(8,128)(2,1)S(1)} %get-tuple-element.91.side_ref), channel_id=1, source_target_pairs={{0,31},{1,2},{2,1},{3,4},{4,3},{5,6},{6,5},{7,8},{8,7},{9,10},{10,... | collective-permute-start | bytes 147464 | tf_op jit(solution)/shard_map/ppermute | solution.py:343
  60.0 6.1 %collective-permute-start.18 = (bf16[6,32,128]{2,1,0:T(8,128)(2,1)S(1)}, bf16[6,32,128]{2,1,0:T(8,128)(2,1)S(1)}, u32[]{:S(2)}, u32[]{:S(2)}) collective-permute-start(bf16[6,32,128]{2,1,0:T(8,128)(2,1)S(1)} %get-tuple-element.89), channel_id=1, source_target_pairs={{0,32},{32,0},{64,96},{96,64},{128,160},{160,128},{192,224},{224,1... | collective-permute-start | bytes 147464 | tf_op jit(solution)/shard_map/ppermute | solution.py:343
  61.4 6.5 %collective-permute-start.17 = (bf16[6,32,128]{2,1,0:T(8,128)(2,1)S(1)}, bf16[6,32,128]{2,1,0:T(8,128)(2,1)S(1)}, u32[]{:S(2)}, u32[]{:S(2)}) collective-permute-start(bf16[6,32,128]{2,1,0:T(8,128)(2,1)S(1)} %get-tuple-element.88), channel_id=1, source_target_pairs={{0,224},{32,64},{64,32},{96,128},{128,96},{160,192},{192,160},{224... | collective-permute-start | bytes 147464 | tf_op jit(solution)/shard_map/ppermute | solution.py:343
  67.9 6.0 %collective-permute-start.23 = (bf16[32,864]{1,0:T(8,128)(2,1)S(1)}, bf16[32,864]{1,0:T(8,128)(2,1)S(1)}, u32[]{:S(2)}, u32[]{:S(2)}) collective-permute-start(bf16[32,864]{1,0:T(8,128)(2,1)S(1)} %add_convert_fusion.1), channel_id=1, source_target_pairs={{0,48},{1,49},{2,50},{3,51},{4,52},{5,53},{6,54},{7,55},{8,56},{9,... | collective-permute-start | bytes 165896 | tf_op jit(solution)/shard_map/ppermute | solution.py:338
  67.9 6.0 %collective-permute-start.22 = (bf16[32,864]{1,0:T(8,128)(2,1)S(1)}, bf16[32,864]{1,0:T(8,128)(2,1)S(1)}, u32[]{:S(2)}, u32[]{:S(2)}) collective-permute-start(bf16[32,864]{1,0:T(8,128)(2,1)S(1)} %add_convert_fusion.1), channel_id=1, source_target_pairs={{0,16},{1,17},{2,18},{3,19},{4,20},{5,21},{6,22},{7,23},{8,24},{9,... | collective-permute-start | bytes 165896 | tf_op jit(solution)/shard_map/ppermute | solution.py:338
  71.2 5.7 %collective-permute-start.21 = (bf16[32,864]{1,0:T(8,128)(2,1)S(1)}, bf16[32,864]{1,0:T(8,128)(2,1)S(1)}, u32[]{:S(2)}, u32[]{:S(2)}) collective-permute-start(bf16[32,864]{1,0:T(8,128)(2,1)S(1)} %add_convert_fusion.1), channel_id=1, source_target_pairs={{0,32},{1,33},{2,34},{3,35},{4,36},{5,37},{6,38},{7,39},{8,40},{9,... | collective-permute-start | bytes 165896 | tf_op jit(solution)/shard_map/ppermute | solution.py:338
  76.9 8.0 %collective-permute-start.26 = (bf16[32,864]{1,0:T(8,128)(2,1)S(1)}, bf16[32,864]{1,0:T(8,128)(2,1)S(1)}, u32[]{:S(2)}, u32[]{:S(2)}) collective-permute-start(bf16[32,864]{1,0:T(8,128)(2,1)S(1)} %add_convert_fusion), channel_id=1, source_target_pairs={{0,192},{1,193},{2,194},{3,195},{4,196},{5,197},{6,198},{7,199},{8... | collective-permute-start | bytes 165896 | tf_op jit(solution)/shard_map/ppermute | solution.py:338
  80.3 6.0 %collective-permute-start.25 = (bf16[32,864]{1,0:T(8,128)(2,1)S(1)}, bf16[32,864]{1,0:T(8,128)(2,1)S(1)}, u32[]{:S(2)}, u32[]{:S(2)}) collective-permute-start(bf16[32,864]{1,0:T(8,128)(2,1)S(1)} %add_convert_fusion), channel_id=1, source_target_pairs={{0,64},{1,65},{2,66},{3,67},{4,68},{5,69},{6,70},{7,71},{8,72},{9,... | collective-permute-start | bytes 165896 | tf_op jit(solution)/shard_map/ppermute | solution.py:338
  80.3 6.0 %collective-permute-start.24 = (bf16[32,864]{1,0:T(8,128)(2,1)S(1)}, bf16[32,864]{1,0:T(8,128)(2,1)S(1)}, u32[]{:S(2)}, u32[]{:S(2)}) collective-permute-start(bf16[32,864]{1,0:T(8,128)(2,1)S(1)} %add_convert_fusion), channel_id=1, source_target_pairs={{0,128},{1,129},{2,130},{3,131},{4,132},{5,133},{6,134},{7,135},{8... | collective-permute-start | bytes 165896 | tf_op jit(solution)/shard_map/ppermute | solution.py:338
  86.3 1.4 %collective-permute-start.27 = (f32[32,864]{1,0:T(8,128)S(1)}, f32[32,864]{1,0:T(8,128)S(1)}, u32[]{:S(2)}, u32[]{:S(2)}) collective-permute-start(f32[32,864]{1,0:T(8,128)S(1)} %broadcast_multiply_fusion), channel_id=1, source_target_pairs={{0,1},{1,0},{2,3},{3,2},{4,5},{5,4},{6,7},{7,6},{8,9},{9,8},{10,11... | collective-permute-start | bytes 331784 | tf_op jit(solution)/shard_map/ppermute | solution.py:338

commit v4 on v3

--- a/solution.py
+++ b/solution.py
@@ -350,7 +350,7 @@
 
 
 ROUNDS = (
-    (lambda x, y, z, c: (x, y, z ^ 3, c), lambda x, y, z, c: (x, y, z ^ 2, c), lambda x, y, z, c: (x, y, z ^ 1, c)),
+    (lambda x, y, z, c: (x, y, z ^ 1, c), lambda x, y, z, c: (x, y, z ^ 2, c), lambda x, y, z, c: (x, y, z ^ 3, c)),
     (lambda x, y, z, c: (x, y, z ^ 4, c),),
     (lambda x, y, z, c: (x, y + 2, z, c), lambda x, y, z, c: (x, y + 1, z, c), lambda x, y, z, c: (x, y - 1, z, c)),
     (lambda x, y, z, c: (x + 2, y, z, c), lambda x, y, z, c: (x + 1, y, z, c), lambda x, y, z, c: (x - 1, y, z, c)),
@@ -410,19 +410,22 @@
     remote = exchanged(odd, even, grad_side)
     weight_scratch = [SCRATCH[1]]
     weight_call = call(weight_kernel, [shape((CHANS, 27 * CHANS), F32)], weight_scratch, 0, CONV_FLOPS)
-    (result,) = call(pack_kernel, [shape(FIELD)], [], 0, 2 * 192 * 1024 * 128)(wide)
     (term_second,) = weight_call(hidden_cells, grad_two)
     grad_one, even, odd, one_side, one_end = call(
         third_kernel, [shape(INSIDE)] + FACES, [pltpu.VMEM(CELLS, BF16)] + SCRATCH, 2, CONV_FLOPS
     )(neighbours, place, grad_two, grad_side, grad_end, *remote, put, pick, back_second, mask, hidden)
     (term_first,) = weight_call(x_cells, grad_one)
     sent = [odd, even, one_side, one_side]
-    total = jnp.where(late, term_second, term_first) + other_core(jnp.where(late, term_first, term_second))
+    given = jnp.where(late, term_first, term_second).astype(BF16)
+    total = jnp.where(late, term_second, term_first) + other_core(given).astype(F32)
     remote = []
     for step, group in enumerate(ROUNDS):
         mine = total.astype(BF16)
+        if step == 2:
+            mine, wide = lax.optimization_barrier((mine, wide))
+            (result,) = call(pack_kernel, [shape(FIELD)], [], 0, 2 * 192 * 1024 * 128)(wide)
         if step == len(ROUNDS) - 1:
-            mine, remote = lax.optimization_barrier((mine, remote))
+            mine, remote, result = lax.optimization_barrier((mine, remote, result))
             (grad_features,) = call(
                 last_kernel,
                 [shape(FIELD)],
@@ -431,7 +434,7 @@
                 CONV_FLOPS,
             )(neighbours, place, grad_one, one_side, one_end, *remote, put, back_first, mask, grad_two)
         elif remote:
-            mine, remote, result = lax.optimization_barrier((mine, remote, result))
+            mine, remote = lax.optimization_barrier((mine, remote))
         for at in RIDERS[step]:
             mine, value = lax.optimization_barrier((mine, sent[at]))
             remote.append(hop(value, at))

time: 89.9 us -> 87.6 us (0.974)
  waiting for transfers between devices: 19.5 us -> 18 us
    ppermute x12, waiting for transfers between devices: 11.3 us -> 9.79 us  [moved(): return lax.ppermute(value, AXES, pairs)]
  transfers between devices with their start and end apart: 28 -> 28, of which waited for: 12 -> 13; matrix products, arithmetic and copies ran while one was open for 0% -> 0% of each run, Pallas kernels for 6% -> 7%
where the time goes in v4:
time: 87.6 us; the launch traced here: 86.2 us
  starting transfers between devices  50.3 us (57%)
  waiting for transfers between devices  18 us (21%)
  Pallas kernels  16.1 us (18%)
  other arithmetic  0.95 us (1%)
    ppermute x16, starting transfers between devices, paired(): lax.ppermute(value, axis, [(at, at ^ 1 if not odd else (at + 1 if at % 2...  31.3 us
    ppermute x12, starting transfers between devices, moved(): return lax.ppermute(value, AXES, pairs)  19 us
    pallas_call x9, Pallas kernels, run(): pl.pallas_call(kernel, out_shape=outs, in_specs=specs, out_specs=[pl.Bloc...  16.1 us
    ppermute x12, waiting for transfers between devices, moved(): return lax.ppermute(value, AXES, pairs)  9.79 us
    ppermute x16, waiting for transfers between devices, paired(): lax.ppermute(value, axis, [(at, at ^ 1 if not odd else (at + 1 if at % 2...  8.2 us
  transfers between devices with their start and end apart: 28, of which 13 were waited for; matrix products, arithmetic and copies ran while one was open for 0% of the time, Pallas kernels for 7%

profile of v4, /device:TPU:24, one launch (start us, length us, event | category | flops | bytes accessed | tf_op | source)
XLA Modules:
  0.0 86.2 jit_solution(1975050783447191464)
XLA Ops:
  0.7 0.1 pad_add_fusion.place_ref
  0.7 2.0 %shard_map.93 = (bf16[6,32,1024]{2,1,0:T(8,128)(2,1)S(1)}, f32[6,1024]{1,0:T(8,128)S(1)}, bf16[1024,256]{1,0:T(8,128)(2,1)S(1)}, bf16[6,32,128]{2,1,0:T(8,128)(2...) custom-call(s32[3]{0:T(128)S(1)} %pad_add_fusion.place_ref, ...), custom_call_target="tpu_custom_call" | custom-call | flops 201326592 | bytes 1347596 | tf_op jit(solution)/shard_map/pallas_call | solution.py:310
  2.7 2.2 %collective-permute-start = (bf16[6,32,128]{2,1,0:T(8,128)(2,1)S(1)}, bf16[6,32,128]{2,1,0:T(8,128)(2,1)S(1)}, u32[]{:S(2)}, u32[]{:S(2)}) collective-permute-start(bf16[6,32,128]{2,1,0:T(8,128)(2,1)S(1)} %get-tuple-element.63), channel_id=1, source_target_pairs={{0,224},{32,64},{64,32},{96,128},{128,96},{160,192},{192,160},{224... | collective-permute-start | bytes 147464 | tf_op jit(solution)/shard_map/ppermute | solution.py:343
  5.0 3.6 %collective-permute-start.1 = (bf16[6,32,128]{2,1,0:T(8,128)(2,1)S(1)}, bf16[6,32,128]{2,1,0:T(8,128)(2,1)S(1)}, u32[]{:S(2)}, u32[]{:S(2)}) collective-permute-start(bf16[6,32,128]{2,1,0:T(8,128)(2,1)S(1)} %get-tuple-element.64), channel_id=1, source_target_pairs={{0,32},{32,0},{64,96},{96,64},{128,160},{160,128},{192,224},{224,1... | collective-permute-start | bytes 147464 | tf_op jit(solution)/shard_map/ppermute | solution.py:343
  8.6 6.1 %collective-permute-start.2 = (bf16[6,32,128]{2,1,0:T(8,128)(2,1)S(1)}, bf16[6,32,128]{2,1,0:T(8,128)(2,1)S(1)}, u32[]{:S(2)}, u32[]{:S(2)}) collective-permute-start(bf16[6,32,128]{2,1,0:T(8,128)(2,1)S(1)} %get-tuple-element.61.side_ref), channel_id=1, source_target_pairs={{0,31},{1,2},{2,1},{3,4},{4,3},{5,6},{6,5},{7,8},{8,7},{9,10},{10,... | collective-permute-start | bytes 147464 | tf_op jit(solution)/shard_map/ppermute | solution.py:343
  14.7 0.6 shard_map.94
  15.3 0.0 copy-start.3
  15.4 1.1 %collective-permute-done.2.r2 = bf16[6,32,128]{2,1,0:T(8,128)(2,1)S(1)} collective-permute-done((bf16[6,32,128]{2,1,0:T(8,128)(2,1)S(1)}, bf16[6,32,128]{2,1,0:T(8,128)(2,1)S(1)}, u32[]{:S(2)}, u32[]{:S(2)}) %collective-permute-start.2) | collective-permute-done | bytes 49184 | tf_op jit(solution)/shard_map/ppermute | solution.py:343
  16.5 2.4 %shard_map.95 = (bf16[6,32,1280]{2,1,0:T(8,128)(2,1)S(1)}, bf16[6,32,1024]{2,1,0:T(8,128)(2,1)S(1)}, bf16[6,32,128]{2,1,0:T(8,128)(2,1)S(1)}, bf16[6,32,128]{2,1...) custom-call(s32[6,6]{1,0:T(8,128)S(1)} %copy-done.3, s32[3]{0:T(128)S(1)} %pad_add_fusion.place_ref, ...), custom_call_target="tpu_custom_call" | custom-call | flops 424673280 | bytes 2898076 | tf_op jit(solution)/shard_map/pallas_call | solution.py:310
  18.9 0.6 collective-permute-start.4
  19.5 3.3 %collective-permute-start.5 = (bf16[6,32,128]{2,1,0:T(8,128)(2,1)S(1)}, bf16[6,32,128]{2,1,0:T(8,128)(2,1)S(1)}, u32[]{:S(2)}, u32[]{:S(2)}) collective-permute-start(bf16[6,32,128]{2,1,0:T(8,128)(2,1)S(1)} %get-tuple-element.72), channel_id=1, source_target_pairs={{0,32},{32,0},{64,96},{96,64},{128,160},{160,128},{192,224},{224,1... | collective-permute-start | bytes 147464 | tf_op jit(solution)/shard_map/ppermute | solution.py:343
  22.7 3.3 %collective-permute-start.6 = (bf16[6,32,128]{2,1,0:T(8,128)(2,1)S(1)}, bf16[6,32,128]{2,1,0:T(8,128)(2,1)S(1)}, u32[]{:S(2)}, u32[]{:S(2)}) collective-permute-start(bf16[6,32,128]{2,1,0:T(8,128)(2,1)S(1)} %get-tuple-element.69.side_ref), channel_id=1, source_target_pairs={{0,31},{1,2},{2,1},{3,4},{4,3},{5,6},{6,5},{7,8},{8,7},{9,10},{10,... | collective-permute-start | bytes 147464 | tf_op jit(solution)/shard_map/ppermute | solution.py:343
  26.0 2.3 %collective-permute-done.6.r2 = bf16[6,32,128]{2,1,0:T(8,128)(2,1)S(1)} collective-permute-done((bf16[6,32,128]{2,1,0:T(8,128)(2,1)S(1)}, bf16[6,32,128]{2,1,0:T(8,128)(2,1)S(1)}, u32[]{:S(2)}, u32[]{:S(2)}) %collective-permute-start.6) | collective-permute-done | bytes 49184 | tf_op jit(solution)/shard_map/ppermute | solution.py:343
  28.4 2.3 %shard_map.96 = (bf16[6,32,1280]{2,1,0:T(8,128)(2,1)S(1)}, bf16[6,32,1024]{2,1,0:T(8,128)(2,1)S(1)}, bf16[6,32,1024]{2,1,0:T(8,128)(2,1)S(1)}, bf16[6,32,128]{2,...) custom-call(s32[6,6]{1,0:T(8,128)S(1)} %copy-done.3, ...), custom_call_target="tpu_custom_call" | custom-call | flops 424673280 | bytes 4077724 | tf_op jit(solution)/shard_map/pallas_call | solution.py:310
  30.7 1.1 %collective-permute-start.8 = (bf16[6,32,128]{2,1,0:T(8,128)(2,1)S(1)}, bf16[6,32,128]{2,1,0:T(8,128)(2,1)S(1)}, u32[]{:S(2)}, u32[]{:S(2)}) collective-permute-start(bf16[6,32,128]{2,1,0:T(8,128)(2,1)S(1)} %get-tuple-element.79), channel_id=1, source_target_pairs={{0,224},{32,64},{64,32},{96,128},{128,96},{160,192},{192,160},{224... | collective-permute-start | bytes 147464 | tf_op jit(solution)/shard_map/ppermute | solution.py:343
  31.7 2.5 %collective-permute-start.9 = (bf16[6,32,128]{2,1,0:T(8,128)(2,1)S(1)}, bf16[6,32,128]{2,1,0:T(8,128)(2,1)S(1)}, u32[]{:S(2)}, u32[]{:S(2)}) collective-permute-start(bf16[6,32,128]{2,1,0:T(8,128)(2,1)S(1)} %get-tuple-element.80), channel_id=1, source_target_pairs={{0,32},{32,0},{64,96},{96,64},{128,160},{160,128},{192,224},{224,1... | collective-permute-start | bytes 147464 | tf_op jit(solution)/shard_map/ppermute | solution.py:343
  34.2 2.7 %collective-permute-start.10 = (bf16[6,32,128]{2,1,0:T(8,128)(2,1)S(1)}, bf16[6,32,128]{2,1,0:T(8,128)(2,1)S(1)}, u32[]{:S(2)}, u32[]{:S(2)}) collective-permute-start(bf16[6,32,128]{2,1,0:T(8,128)(2,1)S(1)} %get-tuple-element.77.side_ref), channel_id=1, source_target_pairs={{0,31},{1,2},{2,1},{3,4},{4,3},{5,6},{6,5},{7,8},{8,7},{9,10},{10,... | collective-permute-start | bytes 147464 | tf_op jit(solution)/shard_map/ppermute | solution.py:343
  36.9 1.4 %shard_map.97 = f32[32,864]{1,0:T(8,128)S(1)} custom-call(bf16[6,32,1280]{2,1,0:T(8,128)(2,1)S(1)} %get-tuple-element.74.cells_ref, bf16[6,32,1024]{2,1,0:T(8,128)(2,1)S(1)} %get-tuple-element.75.grad_ref.inner_ref), custom_call_target="tpu_custom_call" | custom-call | flops 424673280 | bytes 995328 | tf_op jit(solution)/shard_map/pallas_call | solution.py:310
  38.4 1.5 %collective-permute-done.10.r2 = bf16[6,32,128]{2,1,0:T(8,128)(2,1)S(1)} collective-permute-done((bf16[6,32,128]{2,1,0:T(8,128)(2,1)S(1)}, bf16[6,32,128]{2,1,0:T(8,128)(2,1)S(1)}, u32[]{:S(2)}, u32[]{:S(2)}) %collective-permute-start.10) | collective-permute-done | bytes 49184 | tf_op jit(solution)/shard_map/ppermute | solution.py:343
  39.8 2.3 %shard_map.98 = (bf16[6,32,1024]{2,1,0:T(8,128)(2,1)S(1)}, bf16[6,32,128]{2,1,0:T(8,128)(2,1)S(1)}, bf16[6,32,128]{2,1,0:T(8,128)(2,1)S(1)}, bf16[6,32,128]{2,1,0:T(8,128)(2,1)S(1)}, bf16[6,32,128]{2,1,0:T(8,128)(2,1)S(1)}) custom-call(s32[6,6]{1,0:T(8,128)S(1)} %copy-done.3, s32[3]{0:T(128)S(1)} %pad_add_fusion.place_ref, ...), custom_call_target="tpu_custom_call" | custom-call | flops 424673280 | bytes 2799772 | tf_op jit(solution)/shard_map/pallas_call | solution.py:310
  42.1 1.4 %shard_map.99 = f32[32,864]{1,0:T(8,128)S(1)} custom-call(bf16[6,32,1280]{2,1,0:T(8,128)(2,1)S(1)} %get-tuple-element.76.cells_ref, bf16[6,32,1024]{2,1,0:T(8,128)(2,1)S(1)} %get-tuple-element.82.grad_ref.inner_ref), custom_call_target="tpu_custom_call" | custom-call | flops 424673280 | bytes 995328 | tf_op jit(solution)/shard_map/pallas_call | solution.py:310
  43.6 0.1 collective-permute-start.12
  43.7 1.2 %collective-permute-done.12 = bf16[32,864]{1,0:T(8,128)(2,1)S(1)} collective-permute-done((bf16[32,864]{1,0:T(8,128)(2,1)S(1)}, bf16[32,864]{1,0:T(8,128)(2,1)S(1)}, u32[]{:S(2)}, u32[]{:S(2)}) %collective-permute-start.12) | collective-permute-done | bytes 55328 | tf_op jit(solution)/shard_map/ppermute | solution.py:338
  44.9 0.1 collective-permute-start.15
  45.0 0.1 collective-permute-start.14
  45.1 4.3 %collective-permute-start.13 = (bf16[32,864]{1,0:T(8,128)(2,1)S(1)}, bf16[32,864]{1,0:T(8,128)(2,1)S(1)}, u32[]{:S(2)}, u32[]{:S(2)}) collective-permute-start(bf16[32,864]{1,0:T(8,128)(2,1)S(1)} %add_convert_fusion.3), channel_id=1, source_target_pairs={{0,2},{1,3},{2,0},{3,1},{4,6},{5,7},{6,4},{7,5},{8,10},{9,11},{10,... | collective-permute-start | bytes 165896 | tf_op jit(solution)/shard_map/ppermute | solution.py:338
  49.4 2.2 %collective-permute-done.15 = bf16[32,864]{1,0:T(8,128)(2,1)S(1)} collective-permute-done((bf16[32,864]{1,0:T(8,128)(2,1)S(1)}, bf16[32,864]{1,0:T(8,128)(2,1)S(1)}, u32[]{:S(2)}, u32[]{:S(2)}) %collective-permute-start.15) | collective-permute-done | bytes 55328 | tf_op jit(solution)/shard_map/ppermute | solution.py:338
  51.6 0.8 collective-permute-done.14
  52.4 0.2 collective-permute-done.13
  52.7 3.8 %collective-permute-start.16 = (bf16[32,864]{1,0:T(8,128)(2,1)S(1)}, bf16[32,864]{1,0:T(8,128)(2,1)S(1)}, u32[]{:S(2)}, u32[]{:S(2)}) collective-permute-start(bf16[32,864]{1,0:T(8,128)(2,1)S(1)} %add_convert_fusion.2), channel_id=1, source_target_pairs={{0,8},{1,9},{2,10},{3,11},{4,12},{5,13},{6,14},{7,15},{8,0},{9,1},... | collective-permute-start | bytes 165896 | tf_op jit(solution)/shard_map/ppermute | solution.py:338
  56.4 1.3 %collective-permute-start.19 = (bf16[6,32,128]{2,1,0:T(8,128)(2,1)S(1)}, bf16[6,32,128]{2,1,0:T(8,128)(2,1)S(1)}, u32[]{:S(2)}, u32[]{:S(2)}) collective-permute-start(bf16[6,32,128]{2,1,0:T(8,128)(2,1)S(1)} %get-tuple-element.95.side_ref), channel_id=1, source_target_pairs={{0,31},{1,2},{2,1},{3,4},{4,3},{5,6},{6,5},{7,8},{8,7},{9,10},{10,... | collective-permute-start | bytes 147464 | tf_op jit(solution)/shard_map/ppermute | solution.py:343
  57.8 1.4 %collective-permute-start.18 = (bf16[6,32,128]{2,1,0:T(8,128)(2,1)S(1)}, bf16[6,32,128]{2,1,0:T(8,128)(2,1)S(1)}, u32[]{:S(2)}, u32[]{:S(2)}) collective-permute-start(bf16[6,32,128]{2,1,0:T(8,128)(2,1)S(1)} %get-tuple-element.93), channel_id=1, source_target_pairs={{0,32},{32,0},{64,96},{96,64},{128,160},{160,128},{192,224},{224,1... | collective-permute-start | bytes 147464 | tf_op jit(solution)/shard_map/ppermute | solution.py:343
  59.1 3.2 %collective-permute-start.17 = (bf16[6,32,128]{2,1,0:T(8,128)(2,1)S(1)}, bf16[6,32,128]{2,1,0:T(8,128)(2,1)S(1)}, u32[]{:S(2)}, u32[]{:S(2)}) collective-permute-start(bf16[6,32,128]{2,1,0:T(8,128)(2,1)S(1)} %get-tuple-element.92), channel_id=1, source_target_pairs={{0,224},{32,64},{64,32},{96,128},{128,96},{160,192},{192,160},{224... | collective-permute-start | bytes 147464 | tf_op jit(solution)/shard_map/ppermute | solution.py:343
  62.4 0.3 collective-permute-done.19.r2
  62.6 0.9 collective-permute-done.18.r1
  63.5 2.1 %collective-permute-done.17.r0 = bf16[6,32,128]{2,1,0:T(8,128)(2,1)S(1)} collective-permute-done((bf16[6,32,128]{2,1,0:T(8,128)(2,1)S(1)}, bf16[6,32,128]{2,1,0:T(8,128)(2,1)S(1)}, u32[]{:S(2)}, u32[]{:S(2)}) %collective-permute-start.17) | collective-permute-done | bytes 49184 | tf_op jit(solution)/shard_map/ppermute | solution.py:343
  65.6 3.3 %collective-permute-start.22 = (bf16[32,864]{1,0:T(8,128)(2,1)S(1)}, bf16[32,864]{1,0:T(8,128)(2,1)S(1)}, u32[]{:S(2)}, u32[]{:S(2)}) collective-permute-start(bf16[32,864]{1,0:T(8,128)(2,1)S(1)} %add_convert_fusion.1), channel_id=1, source_target_pairs={{0,16},{1,17},{2,18},{3,19},{4,20},{5,21},{6,22},{7,23},{8,24},{9,... | collective-permute-start | bytes 165896 | tf_op jit(solution)/shard_map/ppermute | solution.py:338
  68.9 2.2 %collective-permute-start.21 = (bf16[32,864]{1,0:T(8,128)(2,1)S(1)}, bf16[32,864]{1,0:T(8,128)(2,1)S(1)}, u32[]{:S(2)}, u32[]{:S(2)}) collective-permute-start(bf16[32,864]{1,0:T(8,128)(2,1)S(1)} %add_convert_fusion.1), channel_id=1, source_target_pairs={{0,32},{1,33},{2,34},{3,35},{4,36},{5,37},{6,38},{7,39},{8,40},{9,... | collective-permute-start | bytes 165896 | tf_op jit(solution)/shard_map/ppermute | solution.py:338
  71.1 0.9 %shard_map.100 = bf16[6,32,512]{2,1,0:T(8,128)(2,1)} custom-call(bf16[6,32,1024]{2,1,0:T(8,128)(2,1)S(1)} %get-tuple-element.101.wide_ref), custom_call_target="tpu_custom_call" | custom-call | flops 50331648 | bytes 589824 | tf_op jit(solution)/shard_map/pallas_call | solution.py:310
  72.0 2.6 %collective-permute-done.21 = bf16[32,864]{1,0:T(8,128)(2,1)S(1)} collective-permute-done((bf16[32,864]{1,0:T(8,128)(2,1)S(1)}, bf16[32,864]{1,0:T(8,128)(2,1)S(1)}, u32[]{:S(2)}, u32[]{:S(2)}) %collective-permute-start.21) | collective-permute-done | bytes 55328 | tf_op jit(solution)/shard_map/ppermute | solution.py:338
  74.6 3.4 %collective-permute-start.26 = (bf16[32,864]{1,0:T(8,128)(2,1)S(1)}, bf16[32,864]{1,0:T(8,128)(2,1)S(1)}, u32[]{:S(2)}, u32[]{:S(2)}) collective-permute-start(bf16[32,864]{1,0:T(8,128)(2,1)S(1)} %add_convert_fusion), channel_id=1, source_target_pairs={{0,192},{1,193},{2,194},{3,195},{4,196},{5,197},{6,198},{7,199},{8... | collective-permute-start | bytes 165896 | tf_op jit(solution)/shard_map/ppermute | solution.py:338
  78.0 0.0 collective-permute-start.25
  78.0 1.8 %collective-permute-start.24 = (bf16[32,864]{1,0:T(8,128)(2,1)S(1)}, bf16[32,864]{1,0:T(8,128)(2,1)S(1)}, u32[]{:S(2)}, u32[]{:S(2)}) collective-permute-start(bf16[32,864]{1,0:T(8,128)(2,1)S(1)} %add_convert_fusion), channel_id=1, source_target_pairs={{0,128},{1,129},{2,130},{3,131},{4,132},{5,133},{6,134},{7,135},{8... | collective-permute-start | bytes 165896 | tf_op jit(solution)/shard_map/ppermute | solution.py:338
  79.8 2.8 %shard_map.101 = bf16[6,32,512]{2,1,0:T(8,128)(2,1)} custom-call(s32[6,6]{1,0:T(8,128)S(1)} %copy-done.3, s32[3]{0:T(128)S(1)} %pad_add_fusion.place_ref, bf16[6,32,1024]{2,1,0:T(8,128)(2,1)S(1)} %get-tuple-element.82.grad_ref.inner_ref, bf16[6,32,128]{2,1,0:T(8,128)(2,1)S(1)} %get-tuple-element.95.side_ref, ...), custom_call_target="tpu_custom_call" | custom-call | flops 424673280 | bytes 1882268 | tf_op jit(solution)/shard_map/pallas_call | solution.py:310
  82.6 1.4 %collective-permute-done.25 = bf16[32,864]{1,0:T(8,128)(2,1)S(1)} collective-permute-done((bf16[32,864]{1,0:T(8,128)(2,1)S(1)}, bf16[32,864]{1,0:T(8,128)(2,1)S(1)}, u32[]{:S(2)}, u32[]{:S(2)}) %collective-permute-start.25) | collective-permute-done | bytes 55328 | tf_op jit(solution)/shard_map/ppermute | solution.py:338
  84.1 0.1 collective-permute-start.27
  84.2 1.3 %collective-permute-done.27 = f32[32,864]{1,0:T(8,128)S(1)} collective-permute-done((f32[32,864]{1,0:T(8,128)S(1)}, f32[32,864]{1,0:T(8,128)S(1)}, u32[]{:S(2)}, u32[]{:S(2)}) %collective-permute-start.27) | collective-permute-done | bytes 110624 | tf_op jit(solution)/shard_map/ppermute | solution.py:338
  85.5 0.7 broadcast_select_fusion
  (34 shorter events, 0.2 us)
Async XLA Ops:
  0.7 14.0 %copy-start = (bf16[32,864]{1,0:T(8,128)(2,1)S(1)}, bf16[32,864]{1,0:T(8,128)(2,1)}, u32[]{:S(2)}) copy-start(bf16[32,864]{1,0:T(8,128)(2,1)} %weight_ref.2) | copy-start | bytes 165892
  0.7 14.0 %copy-start.1 = (bf16[32,864]{1,0:T(8,128)(2,1)S(1)}, bf16[32,864]{1,0:T(8,128)(2,1)}, u32[]{:S(2)}) copy-start(bf16[32,864]{1,0:T(8,128)(2,1)} %weight_ref.3) | copy-start | bytes 165892
  0.7 14.0 %copy-start.2 = (bf16[6,32,512]{2,1,0:T(8,128)(2,1)S(1)}, bf16[6,32,512]{2,1,0:T(8,128)(2,1)}, u32[]{:S(2)}) copy-start(bf16[6,32,512]{2,1,0:T(8,128)(2,1)} %cotangent_ref.1) | copy-start | bytes 589828
  2.7 12.6 %collective-permute-start = (bf16[6,32,128]{2,1,0:T(8,128)(2,1)S(1)}, bf16[6,32,128]{2,1,0:T(8,128)(2,1)S(1)}, u32[]{:S(2)}, u32[]{:S(2)}) collective-permute-start(bf16[6,32,128]{2,1,0:T(8,128)(2,1)S(1)} %get-tuple-element.63), channel_id=1, source_target_pairs={{0,224},{32,64},{64,32},{96,128},{128,96},{160,192},{192,160},{224... | collective-permute-start | bytes 147464 | tf_op jit(solution)/shard_map/ppermute | solution.py:343
  5.0 10.3 %collective-permute-start.1 = (bf16[6,32,128]{2,1,0:T(8,128)(2,1)S(1)}, bf16[6,32,128]{2,1,0:T(8,128)(2,1)S(1)}, u32[]{:S(2)}, u32[]{:S(2)}) collective-permute-start(bf16[6,32,128]{2,1,0:T(8,128)(2,1)S(1)} %get-tuple-element.64), channel_id=1, source_target_pairs={{0,32},{32,0},{64,96},{96,64},{128,160},{160,128},{192,224},{224,1... | collective-permute-start | bytes 147464 | tf_op jit(solution)/shard_map/ppermute | solution.py:343
  8.6 6.8 %collective-permute-start.3 = (bf16[6,32,128]{2,1,0:T(8,128)(2,1)S(1)}, bf16[6,32,128]{2,1,0:T(8,128)(2,1)S(1)}, u32[]{:S(2)}, u32[]{:S(2)}) collective-permute-start(bf16[6,32,128]{2,1,0:T(8,128)(2,1)S(1)} %get-tuple-element.61.side_ref), channel_id=1, source_target_pairs={{0,1},{1,0},{2,3},{3,2},{4,5},{5,4},{6,7},{7,6},{8,9},{9,8},{10,11... | collective-permute-start | bytes 147464 | tf_op jit(solution)/shard_map/ppermute | solution.py:343
  8.6 7.9 %collective-permute-start.2 = (bf16[6,32,128]{2,1,0:T(8,128)(2,1)S(1)}, bf16[6,32,128]{2,1,0:T(8,128)(2,1)S(1)}, u32[]{:S(2)}, u32[]{:S(2)}) collective-permute-start(bf16[6,32,128]{2,1,0:T(8,128)(2,1)S(1)} %get-tuple-element.61.side_ref), channel_id=1, source_target_pairs={{0,31},{1,2},{2,1},{3,4},{4,3},{5,6},{6,5},{7,8},{8,7},{9,10},{10,... | collective-permute-start | bytes 147464 | tf_op jit(solution)/shard_map/ppermute | solution.py:343
  15.3 1.2 %copy-start.3 = (s32[6,6]{1,0:T(8,128)S(1)}, s32[6,6]{1,0:T(8,128)}, u32[]{:S(2)}) copy-start(s32[6,6]{1,0:T(8,128)} %neighbours_ref.7) | copy-start | bytes 436
  18.9 7.2 %collective-permute-start.4 = (bf16[6,32,128]{2,1,0:T(8,128)(2,1)S(1)}, bf16[6,32,128]{2,1,0:T(8,128)(2,1)S(1)}, u32[]{:S(2)}, u32[]{:S(2)}) collective-permute-start(bf16[6,32,128]{2,1,0:T(8,128)(2,1)S(1)} %get-tuple-element.71), channel_id=1, source_target_pairs={{0,224},{32,64},{64,32},{96,128},{128,96},{160,192},{192,160},{224... | collective-permute-start | bytes 147464 | tf_op jit(solution)/shard_map/ppermute | solution.py:343
  19.5 6.6 %collective-permute-start.5 = (bf16[6,32,128]{2,1,0:T(8,128)(2,1)S(1)}, bf16[6,32,128]{2,1,0:T(8,128)(2,1)S(1)}, u32[]{:S(2)}, u32[]{:S(2)}) collective-permute-start(bf16[6,32,128]{2,1,0:T(8,128)(2,1)S(1)} %get-tuple-element.72), channel_id=1, source_target_pairs={{0,32},{32,0},{64,96},{96,64},{128,160},{160,128},{192,224},{224,1... | collective-permute-start | bytes 147464 | tf_op jit(solution)/shard_map/ppermute | solution.py:343
  22.7 3.3 %collective-permute-start.7 = (bf16[6,32,128]{2,1,0:T(8,128)(2,1)S(1)}, bf16[6,32,128]{2,1,0:T(8,128)(2,1)S(1)}, u32[]{:S(2)}, u32[]{:S(2)}) collective-permute-start(bf16[6,32,128]{2,1,0:T(8,128)(2,1)S(1)} %get-tuple-element.69.side_ref), channel_id=1, source_target_pairs={{0,1},{1,0},{2,3},{3,2},{4,5},{5,4},{6,7},{7,6},{8,9},{9,8},{10,11... | collective-permute-start | bytes 147464 | tf_op jit(solution)/shard_map/ppermute | solution.py:343
  22.7 5.6 %collective-permute-start.6 = (bf16[6,32,128]{2,1,0:T(8,128)(2,1)S(1)}, bf16[6,32,128]{2,1,0:T(8,128)(2,1)S(1)}, u32[]{:S(2)}, u32[]{:S(2)}) collective-permute-start(bf16[6,32,128]{2,1,0:T(8,128)(2,1)S(1)} %get-tuple-element.69.side_ref), channel_id=1, source_target_pairs={{0,31},{1,2},{2,1},{3,4},{4,3},{5,6},{6,5},{7,8},{8,7},{9,10},{10,... | collective-permute-start | bytes 147464 | tf_op jit(solution)/shard_map/ppermute | solution.py:343
  30.7 7.7 %collective-permute-start.8 = (bf16[6,32,128]{2,1,0:T(8,128)(2,1)S(1)}, bf16[6,32,128]{2,1,0:T(8,128)(2,1)S(1)}, u32[]{:S(2)}, u32[]{:S(2)}) collective-permute-start(bf16[6,32,128]{2,1,0:T(8,128)(2,1)S(1)} %get-tuple-element.79), channel_id=1, source_target_pairs={{0,224},{32,64},{64,32},{96,128},{128,96},{160,192},{192,160},{224... | collective-permute-start | bytes 147464 | tf_op jit(solution)/shard_map/ppermute | solution.py:343
  31.7 6.6 %collective-permute-start.9 = (bf16[6,32,128]{2,1,0:T(8,128)(2,1)S(1)}, bf16[6,32,128]{2,1,0:T(8,128)(2,1)S(1)}, u32[]{:S(2)}, u32[]{:S(2)}) collective-permute-start(bf16[6,32,128]{2,1,0:T(8,128)(2,1)S(1)} %get-tuple-element.80), channel_id=1, source_target_pairs={{0,32},{32,0},{64,96},{96,64},{128,160},{160,128},{192,224},{224,1... | collective-permute-start | bytes 147464 | tf_op jit(solution)/shard_map/ppermute | solution.py:343
  34.2 4.2 %collective-permute-start.11 = (bf16[6,32,128]{2,1,0:T(8,128)(2,1)S(1)}, bf16[6,32,128]{2,1,0:T(8,128)(2,1)S(1)}, u32[]{:S(2)}, u32[]{:S(2)}) collective-permute-start(bf16[6,32,128]{2,1,0:T(8,128)(2,1)S(1)} %get-tuple-element.77.side_ref), channel_id=1, source_target_pairs={{0,1},{1,0},{2,3},{3,2},{4,5},{5,4},{6,7},{7,6},{8,9},{9,8},{10,11... | collective-permute-start | bytes 147464 | tf_op jit(solution)/shard_map/ppermute | solution.py:343
  34.2 5.6 %collective-permute-start.10 = (bf16[6,32,128]{2,1,0:T(8,128)(2,1)S(1)}, bf16[6,32,128]{2,1,0:T(8,128)(2,1)S(1)}, u32[]{:S(2)}, u32[]{:S(2)}) collective-permute-start(bf16[6,32,128]{2,1,0:T(8,128)(2,1)S(1)} %get-tuple-element.77.side_ref), channel_id=1, source_target_pairs={{0,31},{1,2},{2,1},{3,4},{4,3},{5,6},{6,5},{7,8},{8,7},{9,10},{10,... | collective-permute-start | bytes 147464 | tf_op jit(solution)/shard_map/ppermute | solution.py:343
  43.6 1.3 %collective-permute-start.12 = (bf16[32,864]{1,0:T(8,128)(2,1)S(1)}, bf16[32,864]{1,0:T(8,128)(2,1)S(1)}, u32[]{:S(2)}, u32[]{:S(2)}) collective-permute-start(bf16[32,864]{1,0:T(8,128)(2,1)S(1)} %select_convert_fusion), channel_id=1, source_target_pairs={{0,1},{1,0},{2,3},{3,2},{4,5},{5,4},{6,7},{7,6},{8,9},{9,8},{10,11... | collective-permute-start | bytes 165896 | tf_op jit(solution)/shard_map/ppermute | solution.py:338
  44.9 6.7 %collective-permute-start.15 = (bf16[32,864]{1,0:T(8,128)(2,1)S(1)}, bf16[32,864]{1,0:T(8,128)(2,1)S(1)}, u32[]{:S(2)}, u32[]{:S(2)}) collective-permute-start(bf16[32,864]{1,0:T(8,128)(2,1)S(1)} %add_convert_fusion.3), channel_id=1, source_target_pairs={{0,6},{1,7},{2,4},{3,5},{4,2},{5,3},{6,0},{7,1},{8,14},{9,15},{10,... | collective-permute-start | bytes 165896 | tf_op jit(solution)/shard_map/ppermute | solution.py:338
  45.0 7.4 %collective-permute-start.14 = (bf16[32,864]{1,0:T(8,128)(2,1)S(1)}, bf16[32,864]{1,0:T(8,128)(2,1)S(1)}, u32[]{:S(2)}, u32[]{:S(2)}) collective-permute-start(bf16[32,864]{1,0:T(8,128)(2,1)S(1)} %add_convert_fusion.3), channel_id=1, source_target_pairs={{0,4},{1,5},{2,6},{3,7},{4,0},{5,1},{6,2},{7,3},{8,12},{9,13},{10,... | collective-permute-start | bytes 165896 | tf_op jit(solution)/shard_map/ppermute | solution.py:338
  45.1 7.5 %collective-permute-start.13 = (bf16[32,864]{1,0:T(8,128)(2,1)S(1)}, bf16[32,864]{1,0:T(8,128)(2,1)S(1)}, u32[]{:S(2)}, u32[]{:S(2)}) collective-permute-start(bf16[32,864]{1,0:T(8,128)(2,1)S(1)} %add_convert_fusion.3), channel_id=1, source_target_pairs={{0,2},{1,3},{2,0},{3,1},{4,6},{5,7},{6,4},{7,5},{8,10},{9,11},{10,... | collective-permute-start | bytes 165896 | tf_op jit(solution)/shard_map/ppermute | solution.py:338
  52.7 9.7 %collective-permute-start.16 = (bf16[32,864]{1,0:T(8,128)(2,1)S(1)}, bf16[32,864]{1,0:T(8,128)(2,1)S(1)}, u32[]{:S(2)}, u32[]{:S(2)}) collective-permute-start(bf16[32,864]{1,0:T(8,128)(2,1)S(1)} %add_convert_fusion.2), channel_id=1, source_target_pairs={{0,8},{1,9},{2,10},{3,11},{4,12},{5,13},{6,14},{7,15},{8,0},{9,1},... | collective-permute-start | bytes 165896 | tf_op jit(solution)/shard_map/ppermute | solution.py:338
  56.4 5.9 %collective-permute-start.20 = (bf16[6,32,128]{2,1,0:T(8,128)(2,1)S(1)}, bf16[6,32,128]{2,1,0:T(8,128)(2,1)S(1)}, u32[]{:S(2)}, u32[]{:S(2)}) collective-permute-start(bf16[6,32,128]{2,1,0:T(8,128)(2,1)S(1)} %get-tuple-element.95.side_ref), channel_id=1, source_target_pairs={{0,1},{1,0},{2,3},{3,2},{4,5},{5,4},{6,7},{7,6},{8,9},{9,8},{10,11... | collective-permute-start | bytes 147464 | tf_op jit(solution)/shard_map/ppermute | solution.py:343
  56.4 6.2 %collective-permute-start.19 = (bf16[6,32,128]{2,1,0:T(8,128)(2,1)S(1)}, bf16[6,32,128]{2,1,0:T(8,128)(2,1)S(1)}, u32[]{:S(2)}, u32[]{:S(2)}) collective-permute-start(bf16[6,32,128]{2,1,0:T(8,128)(2,1)S(1)} %get-tuple-element.95.side_ref), channel_id=1, source_target_pairs={{0,31},{1,2},{2,1},{3,4},{4,3},{5,6},{6,5},{7,8},{8,7},{9,10},{10,... | collective-permute-start | bytes 147464 | tf_op jit(solution)/shard_map/ppermute | solution.py:343
  57.8 5.7 %collective-permute-start.18 = (bf16[6,32,128]{2,1,0:T(8,128)(2,1)S(1)}, bf16[6,32,128]{2,1,0:T(8,128)(2,1)S(1)}, u32[]{:S(2)}, u32[]{:S(2)}) collective-permute-start(bf16[6,32,128]{2,1,0:T(8,128)(2,1)S(1)} %get-tuple-element.93), channel_id=1, source_target_pairs={{0,32},{32,0},{64,96},{96,64},{128,160},{160,128},{192,224},{224,1... | collective-permute-start | bytes 147464 | tf_op jit(solution)/shard_map/ppermute | solution.py:343
  59.1 6.5 %collective-permute-start.17 = (bf16[6,32,128]{2,1,0:T(8,128)(2,1)S(1)}, bf16[6,32,128]{2,1,0:T(8,128)(2,1)S(1)}, u32[]{:S(2)}, u32[]{:S(2)}) collective-permute-start(bf16[6,32,128]{2,1,0:T(8,128)(2,1)S(1)} %get-tuple-element.92), channel_id=1, source_target_pairs={{0,224},{32,64},{64,32},{96,128},{128,96},{160,192},{192,160},{224... | collective-permute-start | bytes 147464 | tf_op jit(solution)/shard_map/ppermute | solution.py:343
  65.6 6.4 %collective-permute-start.23 = (bf16[32,864]{1,0:T(8,128)(2,1)S(1)}, bf16[32,864]{1,0:T(8,128)(2,1)S(1)}, u32[]{:S(2)}, u32[]{:S(2)}) collective-permute-start(bf16[32,864]{1,0:T(8,128)(2,1)S(1)} %add_convert_fusion.1), channel_id=1, source_target_pairs={{0,48},{1,49},{2,50},{3,51},{4,52},{5,53},{6,54},{7,55},{8,56},{9,... | collective-permute-start | bytes 165896 | tf_op jit(solution)/shard_map/ppermute | solution.py:338
  65.6 6.4 %collective-permute-start.22 = (bf16[32,864]{1,0:T(8,128)(2,1)S(1)}, bf16[32,864]{1,0:T(8,128)(2,1)S(1)}, u32[]{:S(2)}, u32[]{:S(2)}) collective-permute-start(bf16[32,864]{1,0:T(8,128)(2,1)S(1)} %add_convert_fusion.1), channel_id=1, source_target_pairs={{0,16},{1,17},{2,18},{3,19},{4,20},{5,21},{6,22},{7,23},{8,24},{9,... | collective-permute-start | bytes 165896 | tf_op jit(solution)/shard_map/ppermute | solution.py:338
  68.9 5.7 %collective-permute-start.21 = (bf16[32,864]{1,0:T(8,128)(2,1)S(1)}, bf16[32,864]{1,0:T(8,128)(2,1)S(1)}, u32[]{:S(2)}, u32[]{:S(2)}) collective-permute-start(bf16[32,864]{1,0:T(8,128)(2,1)S(1)} %add_convert_fusion.1), channel_id=1, source_target_pairs={{0,32},{1,33},{2,34},{3,35},{4,36},{5,37},{6,38},{7,39},{8,40},{9,... | collective-permute-start | bytes 165896 | tf_op jit(solution)/shard_map/ppermute | solution.py:338
  74.6 7.9 %collective-permute-start.26 = (bf16[32,864]{1,0:T(8,128)(2,1)S(1)}, bf16[32,864]{1,0:T(8,128)(2,1)S(1)}, u32[]{:S(2)}, u32[]{:S(2)}) collective-permute-start(bf16[32,864]{1,0:T(8,128)(2,1)S(1)} %add_convert_fusion), channel_id=1, source_target_pairs={{0,192},{1,193},{2,194},{3,195},{4,196},{5,197},{6,198},{7,199},{8... | collective-permute-start | bytes 165896 | tf_op jit(solution)/shard_map/ppermute | solution.py:338
  78.0 6.0 %collective-permute-start.25 = (bf16[32,864]{1,0:T(8,128)(2,1)S(1)}, bf16[32,864]{1,0:T(8,128)(2,1)S(1)}, u32[]{:S(2)}, u32[]{:S(2)}) collective-permute-start(bf16[32,864]{1,0:T(8,128)(2,1)S(1)} %add_convert_fusion), channel_id=1, source_target_pairs={{0,64},{1,65},{2,66},{3,67},{4,68},{5,69},{6,70},{7,71},{8,72},{9,... | collective-permute-start | bytes 165896 | tf_op jit(solution)/shard_map/ppermute | solution.py:338
  78.0 6.0 %collective-permute-start.24 = (bf16[32,864]{1,0:T(8,128)(2,1)S(1)}, bf16[32,864]{1,0:T(8,128)(2,1)S(1)}, u32[]{:S(2)}, u32[]{:S(2)}) collective-permute-start(bf16[32,864]{1,0:T(8,128)(2,1)S(1)} %add_convert_fusion), channel_id=1, source_target_pairs={{0,128},{1,129},{2,130},{3,131},{4,132},{5,133},{6,134},{7,135},{8... | collective-permute-start | bytes 165896 | tf_op jit(solution)/shard_map/ppermute | solution.py:338
  84.1 1.4 %collective-permute-start.27 = (f32[32,864]{1,0:T(8,128)S(1)}, f32[32,864]{1,0:T(8,128)S(1)}, u32[]{:S(2)}, u32[]{:S(2)}) collective-permute-start(f32[32,864]{1,0:T(8,128)S(1)} %broadcast_multiply_fusion), channel_id=1, source_target_pairs={{0,1},{1,0},{2,3},{3,2},{4,5},{5,4},{6,7},{7,6},{8,9},{9,8},{10,11... | collective-permute-start | bytes 331784 | tf_op jit(solution)/shard_map/ppermute | solution.py:338
